TPU v7x, 32 devices: a whole 2x2x4 slice. The times are simulated.
32 devices in a mesh: seq: 16 (over z, y, x), head: 2 (over core).
Axes of the slice: x: 2, y: 2, z: 4, core: 2. Of those that a mesh axis runs over, the one named last changes fastest.
Arguments:
- queries: bfloat16 [1024, 1024], P('seq', 'head'), may hold values from -9 to 9
- keys: bfloat16 [2, 32768, 128], P('head', 'seq'), may hold values from -9 to 9
- values: bfloat16 [2, 32768, 128], P('head', 'seq'), may hold values from -6 to 6
- mask: int32 [8, 256], P(None, 'seq'), may hold values from 0 to 1, as said below
- out_proj: bfloat16 [1024, 4096], P('head', 'seq'), may hold values from -0.1875 to 0.1875
Outputs:
- output: bfloat16 [1024, 4096], P('seq', 'head')
Inputs may be any that keep to these rules, and one draw needn't show every extreme that they name: `mask`: each entry is 0 or 1; the share of ones differs strongly between the cached positions of different seq shards.
All inputs are finite; a program needn't handle non-finite values.
Results may differ from a plain program's by a relative error of at most 0.0057.
Values may be sent and summed in bfloat16 or wider, within the bound.
No kernel may reach another device: no remote copies, remote signals or barrier semaphores. Data moves between devices by JAX's collectives and lax.ppermute only.
A program may use at most 64 MiB of HBM per device.

v0:
```python
import functools
import math

import jax
import jax.numpy as jnp
from jax import lax
from jax.experimental import pallas as pl
from jax.experimental.pallas import tpu as pltpu
from jax.sharding import PartitionSpec as P


BLK = 128
TILE = 256
CHUNK = 512
VMEM_LIMIT = 24 * 1024 * 1024
LOG2E = math.log2(math.e)
BOTH = ("seq", "head")


def attend_kernel(sources, total_keys, own_rows, flip, has_acc, *refs):
    masks, refs = refs[:sources], refs[sources:]
    q_ref, refs = refs[0], refs[1:]
    keys, refs = refs[:sources], refs[sources:]
    values, refs = refs[:sources], refs[sources:]
    if has_acc:
        acc_in, refs = refs[0], refs[1:]
    out_ref, refs = refs[0], refs[1:]
    if has_acc:
        out_here, refs = refs[0], refs[1:]
    q_here, stacked, total, key_here, value_here, sems = refs
    rows, width = q_ref.shape
    cached, head_size = keys[0].shape
    group = width // head_size
    blocks = rows // own_rows
    part = group * own_rows
    tile = min(TILE, cached)
    chunk = min(CHUNK, cached)
    chunks = cached // chunk
    scale = -LOG2E / math.sqrt(head_size)
    offset = math.log(total_keys) * LOG2E

    loads = [pltpu.make_async_copy(q_ref, q_here, sems.at[0])]
    for n in range(sources):
        for c in range(chunks):
            span = pl.ds(c * chunk, chunk)
            for array, (far, here) in enumerate(((keys[n], key_here), (values[n], value_here))):
                loads.append(
                    pltpu.make_async_copy(
                        far.at[span, :], here.at[n, span, :], sems.at[1 + (n * chunks + c) * 2 + array]
                    )
                )
    if has_acc:
        loads.append(pltpu.make_async_copy(acc_in, out_here, sems.at[1 + sources * chunks * 2]))
    for load in loads:
        load.start()

    seq = lax.axis_index("seq")
    plane = lax.rem(seq, 4)
    line = lax.div(seq, 4)
    odd = lax.rem(lax.axis_index("head"), 2)
    plane = plane ^ jnp.where(odd == 1, flip[1], flip[0])
    mask_rows = [((line ^ j) * 4 + plane) * own_rows // BLK for j in range(blocks)]
    loads[0].wait()
    for j in range(blocks):
        for i in range(group):
            stacked[j * part + i * own_rows : j * part + (i + 1) * own_rows, :] = q_here[
                j * own_rows : (j + 1) * own_rows, i * head_size : (i + 1) * head_size
            ]
    lanes = lax.broadcasted_iota(jnp.int32, (1, tile), 1) // BLK
    first = True
    for n in range(sources):
        for t in range(cached // tile):
            if t * tile % chunk == 0:
                at = 1 + (n * chunks + t * tile // chunk) * 2
                loads[at].wait()
                loads[at + 1].wait()
            score = lax.dot_general(
                stacked[...],
                key_here[n, t * tile : (t + 1) * tile, :],
                (((1,), (1,)), ((), ())),
                preferred_element_type=jnp.float32,
            )
            weights = []
            for j in range(blocks):
                bias = jnp.full((1, tile), offset, jnp.float32)
                for c in range(tile // BLK):
                    live = masks[n][mask_rows[j], t * (tile // BLK) + c] > 0
                    bias = jnp.where(lanes == c, jnp.where(live, offset, 1e30).astype(jnp.float32), bias)
                grown = jnp.exp2(score[j * part : (j + 1) * part] * scale + bias)
                weights.append((1.0 / (1.0 + grown)).astype(jnp.bfloat16))
            weight = jnp.concatenate(weights, axis=0)
            term = jnp.dot(weight, value_here[n, t * tile : (t + 1) * tile, :], preferred_element_type=jnp.float32)
            total[...] = term if first else total[...] + term
            first = False
    if has_acc:
        loads[-1].wait()
    for j in range(blocks):
        for i in range(group):
            here = (slice(j * own_rows, (j + 1) * own_rows), slice(i * head_size, (i + 1) * head_size))
            value = total[j * part + i * own_rows : j * part + (i + 1) * own_rows, :]
            if has_acc:
                value = value + out_here[here]
            out_ref[here] = value.astype(out_ref.dtype)


def attend(q, sources, total_keys, own_rows, flip, acc, dtype):
    rows, width = q.shape
    cached, head_size = sources[0][1].shape
    count = len(sources)
    arrays = (
        [s[0] for s in sources] + [q] + [s[1] for s in sources] + [s[2] for s in sources] + ([] if acc is None else [acc])
    )
    anywhere = pl.BlockSpec(memory_space=pl.ANY)
    smem = pl.BlockSpec(memory_space=pltpu.SMEM)
    scores = rows * (width // head_size) * cached * count
    chunks = cached // min(CHUNK, cached)
    return pl.pallas_call(
        functools.partial(attend_kernel, count, total_keys, own_rows, flip, acc is not None),
        out_shape=jax.ShapeDtypeStruct((rows, width), dtype),
        in_specs=[smem] * count + [anywhere] * (len(arrays) - count),
        out_specs=pl.BlockSpec(memory_space=pltpu.VMEM),
        scratch_shapes=([] if acc is None else [pltpu.VMEM((rows, width), jnp.float32)])
        + [
            pltpu.VMEM((rows, width), jnp.bfloat16),
            pltpu.VMEM((rows * width // head_size, head_size), jnp.bfloat16),
            pltpu.VMEM((rows * width // head_size, head_size), jnp.float32),
            pltpu.VMEM((count, cached, head_size), jnp.bfloat16),
            pltpu.VMEM((count, cached, head_size), jnp.bfloat16),
            pltpu.SemaphoreType.DMA((2 + count * chunks * 2,)),
        ],
        compiler_params=pltpu.CompilerParams(vmem_limit_bytes=VMEM_LIMIT),
        cost_estimate=pl.CostEstimate(
            flops=4 * scores * head_size, transcendentals=2 * scores, bytes_accessed=4 * count * cached * head_size
        ),
    )(*arrays)


def small_call(kernel, out_shapes, args, flops=0):
    vmem = pl.BlockSpec(memory_space=pltpu.VMEM)
    return pl.pallas_call(
        kernel,
        out_shape=out_shapes,
        in_specs=[vmem] * len(args),
        out_specs=jax.tree.map(lambda _: vmem, out_shapes),
        compiler_params=pltpu.CompilerParams(vmem_limit_bytes=VMEM_LIMIT),
        cost_estimate=pl.CostEstimate(flops=flops, transcendentals=0, bytes_accessed=1 << 20),
    )(*args)


def merge_kernel(part_ref, share_ref, own_ref, *block_refs):
    own_rows = own_ref.shape[0]
    for k in range(len(block_refs) + 1):
        rows = slice(k * own_rows, (k + 1) * own_rows)
        value = part_ref[rows, :] + share_ref[rows, :].astype(jnp.float32)
        if k == 0:
            own_ref[...] = value
        else:
            block_refs[k - 1][...] = value.astype(jnp.bfloat16)


def project_kernel(heads, *refs):
    inputs, refs = refs[:heads], refs[heads:]
    blocks, outs = refs[:-4], refs[-4:]
    own_rows = outs[0].shape[0]
    width = inputs[0].shape[1]
    columns = blocks[0].shape[1]
    for m, block in enumerate(blocks):
        value = None
        for k in range(heads):
            term = jnp.dot(
                inputs[k][...], block[k * width : (k + 1) * width, :], preferred_element_type=jnp.float32
            )
            value = term if value is None else value + term
        value = value.astype(jnp.bfloat16)
        for k in range(4):
            outs[k][:, m * columns : (m + 1) * columns] = value[k * own_rows : (k + 1) * own_rows]


def place_kernel(per_head, *refs):
    got, out_ref = refs[:4], refs[4]
    columns = got[0].shape[1] // per_head
    seq = lax.axis_index("seq")
    plane, line = lax.rem(seq, 4), lax.div(seq, 4)
    pieces = [[g[:, m * columns : (m + 1) * columns] for m in range(per_head)] for g in got]
    bit = 1
    while bit < 4:
        here = lax.rem(lax.div(plane, bit), 2) == 1
        pieces = [[jnp.where(here, b, a) for a, b in zip(pieces[k], pieces[k ^ bit])] for k in range(4)]
        bit *= 2
    bit = 1
    while bit < per_head:
        here = lax.rem(lax.div(line, bit), 2) == 1
        pieces = [[jnp.where(here, row[m ^ bit], row[m]) for m in range(per_head)] for row in pieces]
        bit *= 2
    for m in range(per_head):
        for p in range(4):
            at = (m * 4 + p) * columns
            out_ref[:, at : at + columns] = pieces[p][m]


def on_device(queries, keys, values, mask, out_proj):
    seq_size, heads = lax.axis_size("seq"), lax.axis_size("head")
    lines = seq_size // 4
    per_head = lines // heads
    own_rows = queries.shape[0]
    columns = out_proj.shape[1]
    total_keys = keys.shape[1] * seq_size
    seq = lax.axis_index("seq")
    line = seq // 4
    home = line // per_head == lax.axis_index("head")

    def move(x, target):
        pairs = []
        for s in range(seq_size):
            for h in range(heads):
                to = target(s // 4, s % 4, h)
                if to is not None:
                    pairs.append((s * heads + h, (to[0] * 4 + to[1]) * heads + to[2]))
        return lax.ppermute(x, BOTH, pairs)

    def pair(x):
        return move(x, lambda z, p, h: (z, p ^ (1 + h % 2), h))

    def other(x):
        return move(x, lambda z, p, h: (z, p ^ (2 - h % 2), h))

    def along(x, k):
        return move(x, lambda z, p, h: (z ^ k, p, h))

    def inside(x, k):
        return move(x, lambda z, p, h: (z, p ^ k, h))

    def across(x, k):
        return move(x, lambda z, p, h: (z, p, h ^ k))

    key_own, value_own = keys[0], values[0]
    lined = [queries] + [along(queries, k) for k in range(1, lines)]
    mask_pair, key_pair, value_pair = pair(mask), pair(key_own), pair(value_own)
    q_own = jnp.concatenate(lined, axis=0)
    q_other = other(q_own)

    rows_all = jnp.concatenate([out_proj] + [across(out_proj, k) for k in range(1, heads)], axis=0)
    spread = None
    for k in range(per_head, lines, per_head):
        got = move(rows_all, lambda z, p, h, k=k: (z ^ k, p, h) if z // per_head == h else None)
        spread = got if spread is None else spread + got
    proj_here = rows_all if spread is None else jnp.where(home, rows_all, spread)
    proj = [proj_here] + [along(proj_here, k) for k in range(1, per_head)]

    near, far = (mask, key_own, value_own), (mask_pair, key_pair, value_pair)
    part = attend(q_own, [near], total_keys, own_rows, (0, 0), None, jnp.float32)
    share = attend(q_other, [near, far], total_keys, own_rows, (2, 1), None, jnp.bfloat16)
    share = other(share)
    part = attend(q_own, [far], total_keys, own_rows, (0, 0), part, jnp.float32)
    width = part.shape[1]
    block = jax.ShapeDtypeStruct((own_rows, width), jnp.bfloat16)
    merged = small_call(
        merge_kernel, [jax.ShapeDtypeStruct((own_rows, width), jnp.float32)] + [block] * (lines - 1), [part, share]
    )
    sums = merged[0]
    for k in range(1, lines):
        sums = sums + along(merged[k], k).astype(jnp.float32)
    attended = sums.astype(jnp.bfloat16)

    quad = jnp.concatenate([attended] + [inside(attended, k) for k in range(1, 4)], axis=0)
    full = [quad] + [across(quad, k) for k in range(1, heads)]
    piece = jax.ShapeDtypeStruct((own_rows, per_head * columns), jnp.bfloat16)
    result = small_call(
        functools.partial(project_kernel, heads),
        [piece] * 4,
        full + proj,
        flops=8 * own_rows * heads * width * per_head * columns,
    )
    got = [result[0]] + [inside(result[k], k) for k in range(1, 4)]
    return small_call(
        functools.partial(place_kernel, per_head),
        jax.ShapeDtypeStruct((own_rows, 4 * per_head * columns), jnp.bfloat16),
        got,
    )


def solution(mesh):
    placed = (
        P("seq", "head"),
        P("head", "seq", None),
        P("head", "seq", None),
        P(None, "seq"),
        P("head", "seq"),
    )

    return jax.shard_map(on_device, mesh=mesh, in_specs=placed, out_specs=P("seq", "head"), check_vma=False)
```

profile of v0, /device:TPU:0, one launch (start us, length us, event | category | flops | bytes accessed | tf_op | source)
XLA Modules:
  0.0 73.1 jit_solution(4686796217328469080)
XLA Ops:
  0.0 3.1 %collective-permute-start.1 = (bf16[64,512]{1,0:T(8,128)(2,1)}, bf16[64,512]{1,0:T(8,128)(2,1)S(1)}, u32[]{:S(2)}, u32[]{:S(2)}) collective-permute-start(bf16[64,512]{1,0:T(8,128)(2,1)} %param.5), channel_id=1, source_target_pairs={{0,8},{1,9},{2,10},{3,11},{4,12},{5,13},{6,14},{7,15},{8,0},{9,1},... | collective-permute-start | bytes 196616 | tf_op jit(solution)/shard_map/ppermute | solution.py:219
  3.1 2.6 %collective-permute-start.2 = (bf16[64,512]{1,0:T(8,128)(2,1)}, bf16[64,512]{1,0:T(8,128)(2,1)S(1)}, u32[]{:S(2)}, u32[]{:S(2)}) collective-permute-start(bf16[64,512]{1,0:T(8,128)(2,1)} %param.5), channel_id=1, source_target_pairs={{0,16},{1,17},{2,18},{3,19},{4,20},{5,21},{6,22},{7,23},{8,24},{9,... | collective-permute-start | bytes 196616 | tf_op jit(solution)/shard_map/ppermute | solution.py:219
  5.6 0.0 collective-permute-start.3
  5.6 1.7 %collective-permute-start.4 = (bf16[2048,128]{1,0:T(8,128)(2,1)}, bf16[2048,128]{1,0:T(8,128)(2,1)S(1)}, u32[]{:S(2)}, u32[]{:S(2)}) collective-permute-start(bf16[2048,128]{1,0:T(8,128)(2,1)} %bitcast.2), channel_id=1, source_target_pairs={{0,2},{1,5},{2,0},{3,7},{4,6},{5,1},{6,4},{7,3},{8,10},{9,13},{10,... | collective-permute-start | bytes 1572872 | tf_op jit(solution)/shard_map/ppermute | solution.py:219
  7.4 0.0 copy-start.3
  7.4 0.3 collective-permute-start.5
  7.7 0.8 %constant_dynamic-update-slice_fusion.3 = bf16[256,512]{1,0:T(8,128)(2,1)S(1)} fusion(bf16[64,512]{1,0:T(8,128)(2,1)} %param.5), kind=kLoop, calls=%fused_computation.6 | loop fusion | bytes 131072
  8.5 0.0 collective-permute-done.1
  8.5 0.0 collective-permute-start.15
  8.5 2.0 %collective-permute-done.2 = bf16[64,512]{1,0:T(8,128)(2,1)S(1)} collective-permute-done((bf16[64,512]{1,0:T(8,128)(2,1)}, bf16[64,512]{1,0:T(8,128)(2,1)S(1)}, u32[]{:S(2)}, u32[]{:S(2)}) %collective-permute-start.2) | collective-permute-done | bytes 65568 | tf_op jit(solution)/shard_map/ppermute | solution.py:219
  10.5 1.4 %collective-permute-done.3 = bf16[64,512]{1,0:T(8,128)(2,1)S(1)} collective-permute-done((bf16[64,512]{1,0:T(8,128)(2,1)}, bf16[64,512]{1,0:T(8,128)(2,1)S(1)}, u32[]{:S(2)}, u32[]{:S(2)}) %collective-permute-start.3) | collective-permute-done | bytes 65568 | tf_op jit(solution)/shard_map/ppermute | solution.py:219
  11.9 0.0 copy-start.2
  12.0 0.0 copy-start
  12.0 0.0 copy-start.1
  12.0 1.6 %collective-permute-start.6 = (bf16[256,512]{1,0:T(8,128)(2,1)S(1)}, bf16[256,512]{1,0:T(8,128)(2,1)S(1)}, u32[]{:S(2)}, u32[]{:S(2)}) collective-permute-start(bf16[256,512]{1,0:T(8,128)(2,1)S(1)} %constant_dynamic-update-slice_fusion.refs_1_), channel_id=1, source_target_pairs={{0,4},{1,3},{2,6},{3,1},{4,0},{5,7},{6,2},{7,5},{8,12},{9,11},{10,... | collective-permute-start | bytes 786440 | tf_op jit(solution)/shard_map/ppermute | solution.py:219
  13.6 0.0 copy-done.3
  13.6 0.0 collective-permute-done.15
  13.6 4.3 %collective-permute-start.16 = (bf16[1024,256]{1,0:T(8,128)(2,1)S(1)}, bf16[1024,256]{1,0:T(8,128)(2,1)}, u32[]{:S(2)}, u32[]{:S(2)}) collective-permute-start(bf16[1024,256]{1,0:T(8,128)(2,1)S(1)} %constant_dynamic-update-slice_fusion.4), channel_id=1, source_target_pairs={{0,16},{2,18},{4,20},{6,22},{8,24},{10,26},{12,28},{14,30},{17,1},... | collective-permute-start | bytes 1572872 | tf_op jit(solution)/shard_map/ppermute | solution.py:219
  17.9 0.0 copy-done.2
  17.9 1.5 %collective-permute-start = (s32[8,16]{1,0:T(8,128)S(1)}, s32[8,16]{1,0:T(8,128)S(1)}, u32[]{:S(2)}, u32[]{:S(2)}) collective-permute-start(s32[8,16]{1,0:T(8,128)S(1)} %copy-done.2), channel_id=1, source_target_pairs={{0,2},{1,5},{2,0},{3,7},{4,6},{5,1},{6,4},{7,3},{8,10},{9,13},{10,... | collective-permute-start | bytes 1544 | tf_op jit(solution)/shard_map/ppermute | solution.py:219
  19.4 4.1 %collective-permute-done.refs_0_.refs_1_ = s32[8,16]{1,0:T(8,128)S(1)} collective-permute-done((s32[8,16]{1,0:T(8,128)S(1)}, s32[8,16]{1,0:T(8,128)S(1)}, u32[]{:S(2)}, u32[]{:S(2)}) %collective-permute-start) | collective-permute-done | bytes 544 | tf_op jit(solution)/shard_map/ppermute | solution.py:219
  23.5 0.0 collective-permute-done.6.refs_2_
  23.5 0.0 collective-permute-done.4.refs_2_.refs_4_
  23.5 0.0 collective-permute-done.5.refs_3_.refs_6_
  23.5 0.0 copy-done
  23.5 0.0 copy-done.1
  23.5 9.5 %shard_map.57 = bf16[256,512]{1,0:T(8,128)(2,1)S(1)} custom-call(s32[8,16]{1,0:T(8,128)S(1)} %copy-done.2, s32[8,16]{1,0:T(8,128)S(1)} %collective-permute-done.refs_0_.refs_1_, bf16[256,512]{1,0:T(8,128)(2,1)S(1)} %collective-permute-done.6.refs_2_, bf16[2048,128]{1,0:T(8,128)(2,1)S(1)} %bitcast.3, ...), custom_call_target="tpu_custom_call" | custom-call | flops 2147483648 | bytes 2097152 | tf_op jit(solution)/shard_map/pallas_call | solution.py:117
  33.0 1.8 %collective-permute-start.7 = (bf16[256,512]{1,0:T(8,128)(2,1)S(1)}, bf16[256,512]{1,0:T(8,128)(2,1)S(1)}, u32[]{:S(2)}, u32[]{:S(2)}) collective-permute-start(bf16[256,512]{1,0:T(8,128)(2,1)S(1)} %shard_map.57), channel_id=1, source_target_pairs={{0,4},{1,3},{2,6},{3,1},{4,0},{5,7},{6,2},{7,5},{8,12},{9,11},{10,... | collective-permute-start | bytes 786440 | tf_op jit(solution)/shard_map/ppermute | solution.py:219
  34.8 5.1 %shard_map.55.refs_4_ = f32[256,512]{1,0:T(8,128)S(1)} custom-call(s32[8,16]{1,0:T(8,128)S(1)} %copy-done.2, bf16[256,512]{1,0:T(8,128)(2,1)S(1)} %constant_dynamic-update-slice_fusion.refs_1_, bf16[2048,128]{1,0:T(8,128)(2,1)S(1)} %bitcast.4, bf16[2048,128]{1,0:T(8,128)(2,1)S(1)} %bitcast.7), custom_call_target="tpu_custom_call" | custom-call | flops 1073741824 | bytes 1048576 | tf_op jit(solution)/shard_map/pallas_call | solution.py:117
  40.0 5.7 %shard_map.56.part_ref = f32[256,512]{1,0:T(8,128)S(1)} custom-call(s32[8,16]{1,0:T(8,128)S(1)} %collective-permute-done.refs_0_.refs_1_, bf16[256,512]{1,0:T(8,128)(2,1)S(1)} %constant_dynamic-update-slice_fusion.refs_1_, bf16[2048,128]{1,0:T(8,128)(2,1)S(1)} %collective-permute-done.4.refs_2_.refs_4_, ...), custom_call_target="tpu_custom_call" | custom-call | flops 1073741824 | bytes 1048576 | tf_op jit(solution)/shard_map/pallas_call | solution.py:117
  45.7 0.0 collective-permute-done.7.share_ref
  45.7 0.1 shard_map.58
  45.8 3.7 %collective-permute-start.10 = (bf16[64,512]{1,0:T(8,128)(2,1)S(1)}, bf16[64,512]{1,0:T(8,128)(2,1)S(1)}, u32[]{:S(2)}, u32[]{:S(2)}) collective-permute-start(bf16[64,512]{1,0:T(8,128)(2,1)S(1)} %get-tuple-element.16), channel_id=1, source_target_pairs={{0,24},{1,25},{2,26},{3,27},{4,28},{5,29},{6,30},{7,31},{8,16},{9,... | collective-permute-start | bytes 196616 | tf_op jit(solution)/shard_map/ppermute | solution.py:219
  49.4 0.0 collective-permute-start.9
  49.5 0.8 %collective-permute-start.8 = (bf16[64,512]{1,0:T(8,128)(2,1)S(1)}, bf16[64,512]{1,0:T(8,128)(2,1)S(1)}, u32[]{:S(2)}, u32[]{:S(2)}) collective-permute-start(bf16[64,512]{1,0:T(8,128)(2,1)S(1)} %get-tuple-element.14), channel_id=1, source_target_pairs={{0,8},{1,9},{2,10},{3,11},{4,12},{5,13},{6,14},{7,15},{8,0},{9,1},... | collective-permute-start | bytes 196616 | tf_op jit(solution)/shard_map/ppermute | solution.py:219
  50.2 0.0 collective-permute-done.16
  50.2 0.1 broadcast_select_fusion.refs_2_
  50.3 1.3 %collective-permute-start.17 = (bf16[1024,256]{1,0:T(8,128)(2,1)S(1)}, bf16[1024,256]{1,0:T(8,128)(2,1)S(1)}, u32[]{:S(2)}, u32[]{:S(2)}) collective-permute-start(bf16[1024,256]{1,0:T(8,128)(2,1)S(1)} %broadcast_select_fusion.refs_2_), channel_id=1, source_target_pairs={{0,8},{1,9},{2,10},{3,11},{4,12},{5,13},{6,14},{7,15},{8,0},{9,1},... | collective-permute-start | bytes 1572872 | tf_op jit(solution)/shard_map/ppermute | solution.py:219
  51.6 0.5 collective-permute-done.10
  52.1 2.6 %collective-permute-done.9 = bf16[64,512]{1,0:T(8,128)(2,1)S(1)} collective-permute-done((bf16[64,512]{1,0:T(8,128)(2,1)S(1)}, bf16[64,512]{1,0:T(8,128)(2,1)S(1)}, u32[]{:S(2)}, u32[]{:S(2)}) %collective-permute-start.9) | collective-permute-done | bytes 65568 | tf_op jit(solution)/shard_map/ppermute | solution.py:219
  54.7 0.4 collective-permute-done.8
  55.2 1.5 %collective-permute-start.13 = (bf16[64,512]{1,0:T(8,128)(2,1)S(1)}, bf16[64,512]{1,0:T(8,128)(2,1)S(1)}, u32[]{:S(2)}, u32[]{:S(2)}) collective-permute-start(bf16[64,512]{1,0:T(8,128)(2,1)S(1)} %add_convert_fusion), channel_id=1, source_target_pairs={{0,6},{1,7},{2,4},{3,5},{4,2},{5,3},{6,0},{7,1},{8,14},{9,15},{10,... | collective-permute-start | bytes 196616 | tf_op jit(solution)/shard_map/ppermute | solution.py:219
  56.7 1.5 %collective-permute-start.12 = (bf16[64,512]{1,0:T(8,128)(2,1)S(1)}, bf16[64,512]{1,0:T(8,128)(2,1)S(1)}, u32[]{:S(2)}, u32[]{:S(2)}) collective-permute-start(bf16[64,512]{1,0:T(8,128)(2,1)S(1)} %add_convert_fusion), channel_id=1, source_target_pairs={{0,4},{1,5},{2,6},{3,7},{4,0},{5,1},{6,2},{7,3},{8,12},{9,13},{10,... | collective-permute-start | bytes 196616 | tf_op jit(solution)/shard_map/ppermute | solution.py:219
  58.2 0.5 collective-permute-start.11
  58.7 1.7 %collective-permute-done.13 = bf16[64,512]{1,0:T(8,128)(2,1)S(1)} collective-permute-done((bf16[64,512]{1,0:T(8,128)(2,1)S(1)}, bf16[64,512]{1,0:T(8,128)(2,1)S(1)}, u32[]{:S(2)}, u32[]{:S(2)}) %collective-permute-start.13) | collective-permute-done | bytes 65568 | tf_op jit(solution)/shard_map/ppermute | solution.py:219
  60.4 0.7 collective-permute-done.12
  61.1 1.4 %collective-permute-done.11 = bf16[64,512]{1,0:T(8,128)(2,1)S(1)} collective-permute-done((bf16[64,512]{1,0:T(8,128)(2,1)S(1)}, bf16[64,512]{1,0:T(8,128)(2,1)S(1)}, u32[]{:S(2)}, u32[]{:S(2)}) %collective-permute-start.11) | collective-permute-done | bytes 65568 | tf_op jit(solution)/shard_map/ppermute | solution.py:219
  62.5 0.1 collective-permute-start.14
  62.5 1.5 %collective-permute-done.14.refs_1_ = bf16[256,512]{1,0:T(8,128)(2,1)S(1)} collective-permute-done((bf16[256,512]{1,0:T(8,128)(2,1)S(1)}, bf16[256,512]{1,0:T(8,128)(2,1)S(1)}, u32[]{:S(2)}, u32[]{:S(2)}) %collective-permute-start.14) | collective-permute-done | bytes 262176 | tf_op jit(solution)/shard_map/ppermute | solution.py:219
  64.1 0.6 collective-permute-done.17.refs_3_
  64.6 0.4 shard_map.59
  65.1 0.9 %collective-permute-start.18 = (bf16[64,512]{1,0:T(8,128)(2,1)S(1)}, bf16[64,512]{1,0:T(8,128)(2,1)S(1)}, u32[]{:S(2)}, u32[]{:S(2)}) collective-permute-start(bf16[64,512]{1,0:T(8,128)(2,1)S(1)} %get-tuple-element.18), channel_id=1, source_target_pairs={{0,2},{1,3},{2,0},{3,1},{4,6},{5,7},{6,4},{7,5},{8,10},{9,11},{10,... | collective-permute-start | bytes 196616 | tf_op jit(solution)/shard_map/ppermute | solution.py:219
  66.0 1.2 %collective-permute-start.19 = (bf16[64,512]{1,0:T(8,128)(2,1)S(1)}, bf16[64,512]{1,0:T(8,128)(2,1)S(1)}, u32[]{:S(2)}, u32[]{:S(2)}) collective-permute-start(bf16[64,512]{1,0:T(8,128)(2,1)S(1)} %get-tuple-element.19), channel_id=1, source_target_pairs={{0,4},{1,5},{2,6},{3,7},{4,0},{5,1},{6,2},{7,3},{8,12},{9,13},{10,... | collective-permute-start | bytes 196616 | tf_op jit(solution)/shard_map/ppermute | solution.py:219
  67.2 1.4 %collective-permute-start.20 = (bf16[64,512]{1,0:T(8,128)(2,1)S(1)}, bf16[64,512]{1,0:T(8,128)(2,1)S(1)}, u32[]{:S(2)}, u32[]{:S(2)}) collective-permute-start(bf16[64,512]{1,0:T(8,128)(2,1)S(1)} %get-tuple-element.20), channel_id=1, source_target_pairs={{0,6},{1,7},{2,4},{3,5},{4,2},{5,3},{6,0},{7,1},{8,14},{9,15},{10,... | collective-permute-start | bytes 196616 | tf_op jit(solution)/shard_map/ppermute | solution.py:219
  68.6 1.4 %collective-permute-done.18.refs_1_ = bf16[64,512]{1,0:T(8,128)(2,1)S(1)} collective-permute-done((bf16[64,512]{1,0:T(8,128)(2,1)S(1)}, bf16[64,512]{1,0:T(8,128)(2,1)S(1)}, u32[]{:S(2)}, u32[]{:S(2)}) %collective-permute-start.18) | collective-permute-done | bytes 65568 | tf_op jit(solution)/shard_map/ppermute | solution.py:219
  70.1 0.4 collective-permute-done.19.refs_2_
  70.5 1.8 %collective-permute-done.20.refs_3_ = bf16[64,512]{1,0:T(8,128)(2,1)S(1)} collective-permute-done((bf16[64,512]{1,0:T(8,128)(2,1)S(1)}, bf16[64,512]{1,0:T(8,128)(2,1)S(1)}, u32[]{:S(2)}, u32[]{:S(2)}) %collective-permute-start.20) | collective-permute-done | bytes 65568 | tf_op jit(solution)/shard_map/ppermute | solution.py:219
  72.4 0.8 %shard_map.60 = bf16[64,2048]{1,0:T(8,128)(2,1)} custom-call(bf16[64,512]{1,0:T(8,128)(2,1)S(1)} %get-tuple-element.17.refs_0_, bf16[64,512]{1,0:T(8,128)(2,1)S(1)} %collective-permute-done.18.refs_1_, bf16[64,512]{1,0:T(8,128)(2,1)S(1)} %collective-permute-done.19.refs_2_, bf16[64,512]{1,0:T(8,128)(2,1)S(1)} %collective-permute-done.20.refs_3_), custom_call_target="tpu_custom_call" | custom-call | bytes 1048576 | tf_op jit(solution)/shard_map/pallas_call | solution.py:140
  (7 shorter events, 0.1 us)
Async XLA Ops:
  0.0 8.5 %collective-permute-start.1 = (bf16[64,512]{1,0:T(8,128)(2,1)}, bf16[64,512]{1,0:T(8,128)(2,1)S(1)}, u32[]{:S(2)}, u32[]{:S(2)}) collective-permute-start(bf16[64,512]{1,0:T(8,128)(2,1)} %param.5), channel_id=1, source_target_pairs={{0,8},{1,9},{2,10},{3,11},{4,12},{5,13},{6,14},{7,15},{8,0},{9,1},... | collective-permute-start | bytes 196616 | tf_op jit(solution)/shard_map/ppermute | solution.py:219
  3.1 7.5 %collective-permute-start.2 = (bf16[64,512]{1,0:T(8,128)(2,1)}, bf16[64,512]{1,0:T(8,128)(2,1)S(1)}, u32[]{:S(2)}, u32[]{:S(2)}) collective-permute-start(bf16[64,512]{1,0:T(8,128)(2,1)} %param.5), channel_id=1, source_target_pairs={{0,16},{1,17},{2,18},{3,19},{4,20},{5,21},{6,22},{7,23},{8,24},{9,... | collective-permute-start | bytes 196616 | tf_op jit(solution)/shard_map/ppermute | solution.py:219
  5.6 6.3 %collective-permute-start.3 = (bf16[64,512]{1,0:T(8,128)(2,1)}, bf16[64,512]{1,0:T(8,128)(2,1)S(1)}, u32[]{:S(2)}, u32[]{:S(2)}) collective-permute-start(bf16[64,512]{1,0:T(8,128)(2,1)} %param.5), channel_id=1, source_target_pairs={{0,24},{1,25},{2,26},{3,27},{4,28},{5,29},{6,30},{7,31},{8,16},{9,... | collective-permute-start | bytes 196616 | tf_op jit(solution)/shard_map/ppermute | solution.py:219
  5.6 17.9 %collective-permute-start.4 = (bf16[2048,128]{1,0:T(8,128)(2,1)}, bf16[2048,128]{1,0:T(8,128)(2,1)S(1)}, u32[]{:S(2)}, u32[]{:S(2)}) collective-permute-start(bf16[2048,128]{1,0:T(8,128)(2,1)} %bitcast.2), channel_id=1, source_target_pairs={{0,2},{1,5},{2,0},{3,7},{4,6},{5,1},{6,4},{7,3},{8,10},{9,13},{10,... | collective-permute-start | bytes 1572872 | tf_op jit(solution)/shard_map/ppermute | solution.py:219
  7.4 6.2 %copy-start.3 = (bf16[512,256]{1,0:T(8,128)(2,1)S(1)}, bf16[512,256]{1,0:T(8,128)(2,1)}, u32[]{:S(2)}) copy-start(bf16[512,256]{1,0:T(8,128)(2,1)} %param.9) | copy-start | bytes 786436
  7.4 16.2 %collective-permute-start.5 = (bf16[2048,128]{1,0:T(8,128)(2,1)}, bf16[2048,128]{1,0:T(8,128)(2,1)S(1)}, u32[]{:S(2)}, u32[]{:S(2)}) collective-permute-start(bf16[2048,128]{1,0:T(8,128)(2,1)} %bitcast.5), channel_id=1, source_target_pairs={{0,2},{1,5},{2,0},{3,7},{4,6},{5,1},{6,4},{7,3},{8,10},{9,13},{10,... | collective-permute-start | bytes 1572872 | tf_op jit(solution)/shard_map/ppermute | solution.py:219
  8.5 5.1 %collective-permute-start.15 = (bf16[512,256]{1,0:T(8,128)(2,1)}, bf16[512,256]{1,0:T(8,128)(2,1)S(1)}, u32[]{:S(2)}, u32[]{:S(2)}) collective-permute-start(bf16[512,256]{1,0:T(8,128)(2,1)} %param.9), channel_id=1, source_target_pairs={{0,1},{1,0},{2,3},{3,2},{4,5},{5,4},{6,7},{7,6},{8,9},{9,8},{10,11... | collective-permute-start | bytes 786440 | tf_op jit(solution)/shard_map/ppermute | solution.py:219
  11.9 6.0 %copy-start.2 = (s32[8,16]{1,0:T(8,128)S(1)}, s32[8,16]{1,0:T(8,128)}, u32[]{:S(2)}) copy-start(s32[8,16]{1,0:T(8,128)} %refs_0_.3) | copy-start | bytes 1540
  12.0 11.6 %copy-start = (bf16[1,2048,128]{2,1,0:T(8,128)(2,1)S(1)}, bf16[1,2048,128]{2,1,0:T(8,128)(2,1)}, u32[]{:S(2)}) copy-start(bf16[1,2048,128]{2,1,0:T(8,128)(2,1)} %param.6) | copy-start | bytes 1572868
  12.0 11.6 %copy-start.1 = (bf16[1,2048,128]{2,1,0:T(8,128)(2,1)S(1)}, bf16[1,2048,128]{2,1,0:T(8,128)(2,1)}, u32[]{:S(2)}) copy-start(bf16[1,2048,128]{2,1,0:T(8,128)(2,1)} %param.7) | copy-start | bytes 1572868
  12.0 11.5 %collective-permute-start.6 = (bf16[256,512]{1,0:T(8,128)(2,1)S(1)}, bf16[256,512]{1,0:T(8,128)(2,1)S(1)}, u32[]{:S(2)}, u32[]{:S(2)}) collective-permute-start(bf16[256,512]{1,0:T(8,128)(2,1)S(1)} %constant_dynamic-update-slice_fusion.refs_1_), channel_id=1, source_target_pairs={{0,4},{1,3},{2,6},{3,1},{4,0},{5,7},{6,2},{7,5},{8,12},{9,11},{10,... | collective-permute-start | bytes 786440 | tf_op jit(solution)/shard_map/ppermute | solution.py:219
  13.6 36.6 %collective-permute-start.16 = (bf16[1024,256]{1,0:T(8,128)(2,1)S(1)}, bf16[1024,256]{1,0:T(8,128)(2,1)}, u32[]{:S(2)}, u32[]{:S(2)}) collective-permute-start(bf16[1024,256]{1,0:T(8,128)(2,1)S(1)} %constant_dynamic-update-slice_fusion.4), channel_id=1, source_target_pairs={{0,16},{2,18},{4,20},{6,22},{8,24},{10,26},{12,28},{14,30},{17,1},... | collective-permute-start | bytes 1572872 | tf_op jit(solution)/shard_map/ppermute | solution.py:219
  17.9 5.6 %collective-permute-start = (s32[8,16]{1,0:T(8,128)S(1)}, s32[8,16]{1,0:T(8,128)S(1)}, u32[]{:S(2)}, u32[]{:S(2)}) collective-permute-start(s32[8,16]{1,0:T(8,128)S(1)} %copy-done.2), channel_id=1, source_target_pairs={{0,2},{1,5},{2,0},{3,7},{4,6},{5,1},{6,4},{7,3},{8,10},{9,13},{10,... | collective-permute-start | bytes 1544 | tf_op jit(solution)/shard_map/ppermute | solution.py:219
  33.0 12.7 %collective-permute-start.7 = (bf16[256,512]{1,0:T(8,128)(2,1)S(1)}, bf16[256,512]{1,0:T(8,128)(2,1)S(1)}, u32[]{:S(2)}, u32[]{:S(2)}) collective-permute-start(bf16[256,512]{1,0:T(8,128)(2,1)S(1)} %shard_map.57), channel_id=1, source_target_pairs={{0,4},{1,3},{2,6},{3,1},{4,0},{5,7},{6,2},{7,5},{8,12},{9,11},{10,... | collective-permute-start | bytes 786440 | tf_op jit(solution)/shard_map/ppermute | solution.py:219
  45.8 6.3 %collective-permute-start.10 = (bf16[64,512]{1,0:T(8,128)(2,1)S(1)}, bf16[64,512]{1,0:T(8,128)(2,1)S(1)}, u32[]{:S(2)}, u32[]{:S(2)}) collective-permute-start(bf16[64,512]{1,0:T(8,128)(2,1)S(1)} %get-tuple-element.16), channel_id=1, source_target_pairs={{0,24},{1,25},{2,26},{3,27},{4,28},{5,29},{6,30},{7,31},{8,16},{9,... | collective-permute-start | bytes 196616 | tf_op jit(solution)/shard_map/ppermute | solution.py:219
  49.4 5.3 %collective-permute-start.9 = (bf16[64,512]{1,0:T(8,128)(2,1)S(1)}, bf16[64,512]{1,0:T(8,128)(2,1)S(1)}, u32[]{:S(2)}, u32[]{:S(2)}) collective-permute-start(bf16[64,512]{1,0:T(8,128)(2,1)S(1)} %get-tuple-element.15), channel_id=1, source_target_pairs={{0,16},{1,17},{2,18},{3,19},{4,20},{5,21},{6,22},{7,23},{8,24},{9,... | collective-permute-start | bytes 196616 | tf_op jit(solution)/shard_map/ppermute | solution.py:219
  49.5 5.7 %collective-permute-start.8 = (bf16[64,512]{1,0:T(8,128)(2,1)S(1)}, bf16[64,512]{1,0:T(8,128)(2,1)S(1)}, u32[]{:S(2)}, u32[]{:S(2)}) collective-permute-start(bf16[64,512]{1,0:T(8,128)(2,1)S(1)} %get-tuple-element.14), channel_id=1, source_target_pairs={{0,8},{1,9},{2,10},{3,11},{4,12},{5,13},{6,14},{7,15},{8,0},{9,1},... | collective-permute-start | bytes 196616 | tf_op jit(solution)/shard_map/ppermute | solution.py:219
  50.3 14.3 %collective-permute-start.17 = (bf16[1024,256]{1,0:T(8,128)(2,1)S(1)}, bf16[1024,256]{1,0:T(8,128)(2,1)S(1)}, u32[]{:S(2)}, u32[]{:S(2)}) collective-permute-start(bf16[1024,256]{1,0:T(8,128)(2,1)S(1)} %broadcast_select_fusion.refs_2_), channel_id=1, source_target_pairs={{0,8},{1,9},{2,10},{3,11},{4,12},{5,13},{6,14},{7,15},{8,0},{9,1},... | collective-permute-start | bytes 1572872 | tf_op jit(solution)/shard_map/ppermute | solution.py:219
  55.2 5.2 %collective-permute-start.13 = (bf16[64,512]{1,0:T(8,128)(2,1)S(1)}, bf16[64,512]{1,0:T(8,128)(2,1)S(1)}, u32[]{:S(2)}, u32[]{:S(2)}) collective-permute-start(bf16[64,512]{1,0:T(8,128)(2,1)S(1)} %add_convert_fusion), channel_id=1, source_target_pairs={{0,6},{1,7},{2,4},{3,5},{4,2},{5,3},{6,0},{7,1},{8,14},{9,15},{10,... | collective-permute-start | bytes 196616 | tf_op jit(solution)/shard_map/ppermute | solution.py:219
  56.7 4.4 %collective-permute-start.12 = (bf16[64,512]{1,0:T(8,128)(2,1)S(1)}, bf16[64,512]{1,0:T(8,128)(2,1)S(1)}, u32[]{:S(2)}, u32[]{:S(2)}) collective-permute-start(bf16[64,512]{1,0:T(8,128)(2,1)S(1)} %add_convert_fusion), channel_id=1, source_target_pairs={{0,4},{1,5},{2,6},{3,7},{4,0},{5,1},{6,2},{7,3},{8,12},{9,13},{10,... | collective-permute-start | bytes 196616 | tf_op jit(solution)/shard_map/ppermute | solution.py:219
  58.2 4.3 %collective-permute-start.11 = (bf16[64,512]{1,0:T(8,128)(2,1)S(1)}, bf16[64,512]{1,0:T(8,128)(2,1)S(1)}, u32[]{:S(2)}, u32[]{:S(2)}) collective-permute-start(bf16[64,512]{1,0:T(8,128)(2,1)S(1)} %add_convert_fusion), channel_id=1, source_target_pairs={{0,2},{1,3},{2,0},{3,1},{4,6},{5,7},{6,4},{7,5},{8,10},{9,11},{10,... | collective-permute-start | bytes 196616 | tf_op jit(solution)/shard_map/ppermute | solution.py:219
  62.5 1.6 %collective-permute-start.14 = (bf16[256,512]{1,0:T(8,128)(2,1)S(1)}, bf16[256,512]{1,0:T(8,128)(2,1)S(1)}, u32[]{:S(2)}, u32[]{:S(2)}) collective-permute-start(bf16[256,512]{1,0:T(8,128)(2,1)S(1)} %pad_maximum_fusion.refs_0_), channel_id=1, source_target_pairs={{0,1},{1,0},{2,3},{3,2},{4,5},{5,4},{6,7},{7,6},{8,9},{9,8},{10,11... | collective-permute-start | bytes 786440 | tf_op jit(solution)/shard_map/ppermute | solution.py:219
  65.1 5.0 %collective-permute-start.18 = (bf16[64,512]{1,0:T(8,128)(2,1)S(1)}, bf16[64,512]{1,0:T(8,128)(2,1)S(1)}, u32[]{:S(2)}, u32[]{:S(2)}) collective-permute-start(bf16[64,512]{1,0:T(8,128)(2,1)S(1)} %get-tuple-element.18), channel_id=1, source_target_pairs={{0,2},{1,3},{2,0},{3,1},{4,6},{5,7},{6,4},{7,5},{8,10},{9,11},{10,... | collective-permute-start | bytes 196616 | tf_op jit(solution)/shard_map/ppermute | solution.py:219
  66.0 4.5 %collective-permute-start.19 = (bf16[64,512]{1,0:T(8,128)(2,1)S(1)}, bf16[64,512]{1,0:T(8,128)(2,1)S(1)}, u32[]{:S(2)}, u32[]{:S(2)}) collective-permute-start(bf16[64,512]{1,0:T(8,128)(2,1)S(1)} %get-tuple-element.19), channel_id=1, source_target_pairs={{0,4},{1,5},{2,6},{3,7},{4,0},{5,1},{6,2},{7,3},{8,12},{9,13},{10,... | collective-permute-start | bytes 196616 | tf_op jit(solution)/shard_map/ppermute | solution.py:219
  67.2 5.2 %collective-permute-start.20 = (bf16[64,512]{1,0:T(8,128)(2,1)S(1)}, bf16[64,512]{1,0:T(8,128)(2,1)S(1)}, u32[]{:S(2)}, u32[]{:S(2)}) collective-permute-start(bf16[64,512]{1,0:T(8,128)(2,1)S(1)} %get-tuple-element.20), channel_id=1, source_target_pairs={{0,6},{1,7},{2,4},{3,5},{4,2},{5,3},{6,0},{7,1},{8,14},{9,15},{10,... | collective-permute-start | bytes 196616 | tf_op jit(solution)/shard_map/ppermute | solution.py:219
where the time goes:
time: 73.3 us; the launch traced here: 73.1 us
  starting transfers between devices  29.8 us (41%)
  Pallas kernels  21.6 us (29%)
  waiting for transfers between devices  20.6 us (28%)
  local copies, waits for them, and re-layouts  0.92 us (1%)
    ppermute x21, starting transfers between devices, move(): return lax.ppermute(x, BOTH, pairs)  29.8 us
    ppermute x21, waiting for transfers between devices, move(): return lax.ppermute(x, BOTH, pairs)  20.6 us
    pallas_call x3, Pallas kernels, attend(): pl.pallas_call(functools.partial(attend_kernel, count, total_keys, own_ro...  20.3 us
  transfers between devices with their start and end apart: 21, of which 14 were waited for; matrix products, arithmetic and copies ran while one was open for 1% of the time, Pallas kernels for 28%

commit v1 on v0

v1 whole, which is shorter than its diff:
```python
import functools
import math

import jax
import jax.numpy as jnp
from jax import lax
from jax.experimental import pallas as pl
from jax.experimental.pallas import tpu as pltpu
from jax.sharding import PartitionSpec as P


BLK = 128
TILE = 256
VMEM_LIMIT = 24 * 1024 * 1024
LOG2E = math.log2(math.e)
BOTH = ("seq", "head")


def attend_kernel(own_rows, flip, has_acc, bias_ref, q_ref, k_ref, v_ref, *refs):
    if has_acc:
        acc_in, refs = refs[0], refs[1:]
    out_ref, stacked, total = refs
    rows, width = q_ref.shape
    cached, head_size = k_ref.shape
    group = width // head_size
    blocks = rows // own_rows
    part = group * own_rows
    tile = min(TILE, cached)
    scale = -LOG2E / math.sqrt(head_size)
    seq = lax.axis_index("seq")
    plane = lax.rem(seq, 4)
    line = lax.div(seq, 4)
    odd = lax.rem(lax.axis_index("head"), 2)
    plane = plane ^ jnp.where(odd == 1, flip[1], flip[0])
    biases = []
    for j in range(blocks):
        mask_row = ((line ^ j) * 4 + plane) * own_rows // BLK
        biases.append(bias_ref[pl.ds(mask_row, 1), :])
    for j in range(blocks):
        for i in range(group):
            stacked[j * part + i * own_rows : j * part + (i + 1) * own_rows, :] = q_ref[
                j * own_rows : (j + 1) * own_rows, i * head_size : (i + 1) * head_size
            ]
    for t in range(cached // tile):
        score = lax.dot_general(
            stacked[...],
            k_ref[t * tile : (t + 1) * tile, :],
            (((1,), (1,)), ((), ())),
            preferred_element_type=jnp.float32,
        )
        weights = []
        for j in range(blocks):
            bias = jnp.concatenate(
                [
                    jnp.broadcast_to(biases[j][:, c : c + 1], (1, BLK))
                    for c in range(t * (tile // BLK), (t + 1) * (tile // BLK))
                ],
                axis=1,
            )
            grown = jnp.exp2(score[j * part : (j + 1) * part] * scale + bias)
            weights.append((1.0 / (1.0 + grown)).astype(jnp.bfloat16))
        weight = jnp.concatenate(weights, axis=0)
        term = jnp.dot(weight, v_ref[t * tile : (t + 1) * tile, :], preferred_element_type=jnp.float32)
        total[...] = term if t == 0 else total[...] + term
    for j in range(blocks):
        for i in range(group):
            here = (slice(j * own_rows, (j + 1) * own_rows), slice(i * head_size, (i + 1) * head_size))
            value = total[j * part + i * own_rows : j * part + (i + 1) * own_rows, :]
            if has_acc:
                value = value + acc_in[here]
            out_ref[here] = value.astype(out_ref.dtype)


def attend(q, source, own_rows, flip, acc, dtype):
    rows, width = q.shape
    cached, head_size = source[1].shape
    stacked = (rows * width // head_size, head_size)
    scores = stacked[0] * cached
    vmem = pl.BlockSpec(memory_space=pltpu.VMEM)
    args = [source[0], q, source[1], source[2]] + ([] if acc is None else [acc])
    return pl.pallas_call(
        functools.partial(attend_kernel, own_rows, flip, acc is not None),
        out_shape=jax.ShapeDtypeStruct((rows, width), dtype),
        in_specs=[vmem] * len(args),
        out_specs=vmem,
        scratch_shapes=[pltpu.VMEM(stacked, jnp.bfloat16), pltpu.VMEM(stacked, jnp.float32)],
        compiler_params=pltpu.CompilerParams(vmem_limit_bytes=VMEM_LIMIT),
        cost_estimate=pl.CostEstimate(
            flops=4 * scores * head_size, transcendentals=2 * scores, bytes_accessed=4 * cached * head_size
        ),
    )(*args)


def small_call(kernel, out_shapes, args, flops=0):
    vmem = pl.BlockSpec(memory_space=pltpu.VMEM)
    return pl.pallas_call(
        kernel,
        out_shape=out_shapes,
        in_specs=[vmem] * len(args),
        out_specs=jax.tree.map(lambda _: vmem, out_shapes),
        compiler_params=pltpu.CompilerParams(vmem_limit_bytes=VMEM_LIMIT),
        cost_estimate=pl.CostEstimate(flops=flops, transcendentals=0, bytes_accessed=1 << 20),
    )(*args)


def stage_kernel(key_far, value_far, key_here, value_here, sems):
    copies = [
        pltpu.make_async_copy(far, here, sems.at[i])
        for i, (far, here) in enumerate(((key_far, key_here), (value_far, value_here)))
    ]
    for copy in copies:
        copy.start()
    for copy in copies:
        copy.wait()


def stage(keys, values):
    vmem = pl.BlockSpec(memory_space=pltpu.VMEM)
    return pl.pallas_call(
        stage_kernel,
        name="stage",
        out_shape=[jax.ShapeDtypeStruct(x.shape, x.dtype) for x in (keys, values)],
        in_specs=[pl.BlockSpec(memory_space=pl.ANY)] * 2,
        out_specs=[vmem] * 2,
        scratch_shapes=[pltpu.SemaphoreType.DMA((2,))],
        compiler_params=pltpu.CompilerParams(vmem_limit_bytes=VMEM_LIMIT),
        cost_estimate=pl.CostEstimate(flops=0, transcendentals=0, bytes_accessed=4 * keys.size),
    )(keys, values)


def merge_kernel(part_ref, share_ref, own_ref, *block_refs):
    own_rows = own_ref.shape[0]
    for k in range(len(block_refs) + 1):
        rows = slice(k * own_rows, (k + 1) * own_rows)
        value = part_ref[rows, :] + share_ref[rows, :].astype(jnp.float32)
        if k == 0:
            own_ref[...] = value
        else:
            block_refs[k - 1][...] = value.astype(jnp.bfloat16)


def project_kernel(heads, *refs):
    inputs, refs = refs[:heads], refs[heads:]
    blocks, outs = refs[:-4], refs[-4:]
    own_rows = outs[0].shape[0]
    width = inputs[0].shape[1]
    columns = blocks[0].shape[1]
    for m, block in enumerate(blocks):
        value = None
        for k in range(heads):
            term = jnp.dot(
                inputs[k][...], block[k * width : (k + 1) * width, :], preferred_element_type=jnp.float32
            )
            value = term if value is None else value + term
        value = value.astype(jnp.bfloat16)
        for k in range(4):
            outs[k][:, m * columns : (m + 1) * columns] = value[k * own_rows : (k + 1) * own_rows]


def place_kernel(per_head, *refs):
    got, out_ref = refs[:4], refs[4]
    columns = got[0].shape[1] // per_head
    seq = lax.axis_index("seq")
    plane, line = lax.rem(seq, 4), lax.div(seq, 4)
    pieces = [[g[:, m * columns : (m + 1) * columns] for m in range(per_head)] for g in got]
    bit = 1
    while bit < 4:
        here = lax.rem(lax.div(plane, bit), 2) == 1
        pieces = [[jnp.where(here, b, a) for a, b in zip(pieces[k], pieces[k ^ bit])] for k in range(4)]
        bit *= 2
    bit = 1
    while bit < per_head:
        here = lax.rem(lax.div(line, bit), 2) == 1
        pieces = [[jnp.where(here, row[m ^ bit], row[m]) for m in range(per_head)] for row in pieces]
        bit *= 2
    for m in range(per_head):
        for p in range(4):
            at = (m * 4 + p) * columns
            out_ref[:, at : at + columns] = pieces[p][m]


def on_device(queries, keys, values, mask, out_proj):
    seq_size, heads = lax.axis_size("seq"), lax.axis_size("head")
    lines = seq_size // 4
    per_head = lines // heads
    own_rows = queries.shape[0]
    columns = out_proj.shape[1]
    total_keys = keys.shape[1] * seq_size
    line, head = lax.axis_index("seq") // 4, lax.axis_index("head")

    def move(x, target):
        pairs = []
        for s in range(seq_size):
            for h in range(heads):
                to = target(s // 4, s % 4, h)
                if to is not None:
                    pairs.append((s * heads + h, (to[0] * 4 + to[1]) * heads + to[2]))
        return lax.ppermute(x, BOTH, pairs)

    def pair(x):
        return move(x, lambda z, p, h: (z, p ^ (1 + h % 2), h))

    def other(x):
        return move(x, lambda z, p, h: (z, p ^ (2 - h % 2), h))

    def along(x, k):
        return move(x, lambda z, p, h: (z ^ k, p, h))

    def inside(x, k):
        return move(x, lambda z, p, h: (z, p ^ k, h))

    def across(x, k):
        return move(x, lambda z, p, h: (z, p, h ^ k))

    key_own, value_own = keys[0], values[0]
    lined = [queries] + [along(queries, k) for k in range(1, lines)]
    bias = jnp.where(mask > 0, jnp.float32(math.log(total_keys) * LOG2E), jnp.float32(1e30))
    bias_pair, key_pair, value_pair = pair(bias), pair(key_own), pair(value_own)
    q_own = jnp.concatenate(lined, axis=0)
    q_other = other(q_own)

    held, step = [out_proj], per_head
    while step < lines:
        held += [along(block, step) for block in held]
        step *= 2
    bit = 1
    while bit < heads:
        here = ((line // per_head) ^ head) // bit % 2 == 1
        held = [jnp.where(here, held[i ^ bit], held[i]) for i in range(heads)]
        bit *= 2
    rows_all = jnp.concatenate([held[0]] + [across(held[k], k) for k in range(1, heads)], axis=0)
    proj = [rows_all] + [along(rows_all, k) for k in range(1, per_head)]

    near, far = (bias, *stage(key_own, value_own)), (bias_pair, key_pair, value_pair)

    def attention(q, source, flip, acc, dtype=jnp.float32):
        return attend(q, source, own_rows, flip, acc, dtype)

    part = attention(q_own, near, (0, 0), None)
    share = attention(q_other, near, (2, 1), None)
    share = other(attention(q_other, far, (2, 1), share, jnp.bfloat16))
    part = attention(q_own, far, (0, 0), part)
    width = part.shape[1]
    block = jax.ShapeDtypeStruct((own_rows, width), jnp.bfloat16)
    merged = small_call(
        merge_kernel, [jax.ShapeDtypeStruct((own_rows, width), jnp.float32)] + [block] * (lines - 1), [part, share]
    )
    sums = merged[0]
    for k in range(1, lines):
        sums = sums + along(merged[k], k).astype(jnp.float32)
    attended = sums.astype(jnp.bfloat16)

    quad = jnp.concatenate([attended] + [inside(attended, k) for k in range(1, 4)], axis=0)
    full = [quad] + [across(quad, k) for k in range(1, heads)]
    piece = jax.ShapeDtypeStruct((own_rows, per_head * columns), jnp.bfloat16)
    result = small_call(
        functools.partial(project_kernel, heads),
        [piece] * 4,
        full + proj,
        flops=8 * own_rows * heads * width * per_head * columns,
    )
    got = [result[0]] + [inside(result[k], k) for k in range(1, 4)]
    return small_call(
        functools.partial(place_kernel, per_head),
        jax.ShapeDtypeStruct((own_rows, 4 * per_head * columns), jnp.bfloat16),
        got,
    )


def solution(mesh):
    placed = (
        P("seq", "head"),
        P("head", "seq", None),
        P("head", "seq", None),
        P(None, "seq"),
        P("head", "seq"),
    )

    return jax.shard_map(on_device, mesh=mesh, in_specs=placed, out_specs=P("seq", "head"), check_vma=False)
```

time: 73.3 us -> 62.7 us (0.86)
  Pallas kernels: 21.6 us -> 11.2 us
  starting transfers between devices: 29.8 us -> 26.9 us
  local copies, waits for them, and re-layouts: 0.92 us -> 1.91 us
  waiting for transfers between devices: 20.6 us -> 21.4 us
    pallas_call x3 -> x5, Pallas kernels: 20.3 us -> 10 us  [the longest x4 9.91 us: attend(): pl.pallas_call(functools.partial(attend_kernel, own_rows, flip, acc is no...]
    ppermute x21, starting transfers between devices: 29.8 us -> 26.9 us  [move(): return lax.ppermute(x, BOTH, pairs)]
    unnamed x12 -> x9, local copies, waits for them, and re-layouts: 0.89 us -> 1.91 us
    ppermute x21, waiting for transfers between devices: 20.6 us -> 21.4 us  [move(): return lax.ppermute(x, BOTH, pairs)]
  transfers between devices with their start and end apart: 21 -> 21, of which waited for: 14 -> 13; matrix products, arithmetic and copies ran while one was open for 1% -> 3% of each run, Pallas kernels for 28% -> 16%
where the time goes in v1:
time: 62.7 us; the launch traced here: 62.5 us
  starting transfers between devices  26.9 us (43%)
  waiting for transfers between devices  21.4 us (34%)
  Pallas kernels  11.2 us (18%)
  local copies, waits for them, and re-layouts  1.91 us (3%)
  other arithmetic  0.81 us (1%)
    ppermute x21, starting transfers between devices, move(): return lax.ppermute(x, BOTH, pairs)  26.9 us
    ppermute x21, waiting for transfers between devices, move(): return lax.ppermute(x, BOTH, pairs)  21.4 us
    pallas_call x4, Pallas kernels, attend(): pl.pallas_call(functools.partial(attend_kernel, own_rows, flip, acc is no...  9.91 us
    unnamed x9, local copies, waits for them, and re-layouts  1.91 us
  transfers between devices with their start and end apart: 21, of which 13 were waited for; matrix products, arithmetic and copies ran while one was open for 3% of the time, Pallas kernels for 16%

profile of v1, /device:TPU:0, one launch (start us, length us, event | category | flops | bytes accessed | tf_op | source)
XLA Modules:
  0.0 62.5 jit_solution(14504309894842485495)
XLA Ops:
  0.0 0.0 copy-start
  0.0 3.1 %collective-permute-start.1 = (bf16[64,512]{1,0:T(8,128)(2,1)}, bf16[64,512]{1,0:T(8,128)(2,1)S(1)}, u32[]{:S(2)}, u32[]{:S(2)}) collective-permute-start(bf16[64,512]{1,0:T(8,128)(2,1)} %param.5), channel_id=1, source_target_pairs={{0,8},{1,9},{2,10},{3,11},{4,12},{5,13},{6,14},{7,15},{8,0},{9,1},... | collective-permute-start | bytes 196616 | tf_op jit(solution)/shard_map/ppermute | solution.py:198
  3.1 2.6 %collective-permute-start.2 = (bf16[64,512]{1,0:T(8,128)(2,1)}, bf16[64,512]{1,0:T(8,128)(2,1)S(1)}, u32[]{:S(2)}, u32[]{:S(2)}) collective-permute-start(bf16[64,512]{1,0:T(8,128)(2,1)} %param.5), channel_id=1, source_target_pairs={{0,16},{1,17},{2,18},{3,19},{4,20},{5,21},{6,22},{7,23},{8,24},{9,... | collective-permute-start | bytes 196616 | tf_op jit(solution)/shard_map/ppermute | solution.py:198
  5.6 0.0 collective-permute-start.3
  5.6 1.7 %collective-permute-start.4 = (bf16[2048,128]{1,0:T(8,128)(2,1)}, bf16[2048,128]{1,0:T(8,128)(2,1)S(1)}, u32[]{:S(2)}, u32[]{:S(2)}) collective-permute-start(bf16[2048,128]{1,0:T(8,128)(2,1)} %bitcast.2), channel_id=1, source_target_pairs={{0,2},{1,5},{2,0},{3,7},{4,6},{5,1},{6,4},{7,3},{8,10},{9,13},{10,... | collective-permute-start | bytes 1572872 | tf_op jit(solution)/shard_map/ppermute | solution.py:198
  7.4 0.3 collective-permute-start.5
  7.7 0.8 %constant_dynamic-update-slice_fusion.3 = bf16[256,512]{1,0:T(8,128)(2,1)S(1)} fusion(bf16[64,512]{1,0:T(8,128)(2,1)} %param.5), kind=kLoop, calls=%fused_computation.8 | loop fusion | bytes 131072
  8.5 0.0 collective-permute-done.1
  8.5 2.0 %collective-permute-done.2 = bf16[64,512]{1,0:T(8,128)(2,1)S(1)} collective-permute-done((bf16[64,512]{1,0:T(8,128)(2,1)}, bf16[64,512]{1,0:T(8,128)(2,1)S(1)}, u32[]{:S(2)}, u32[]{:S(2)}) %collective-permute-start.2) | collective-permute-done | bytes 65568 | tf_op jit(solution)/shard_map/ppermute | solution.py:198
  10.6 1.4 %collective-permute-done.3 = bf16[64,512]{1,0:T(8,128)(2,1)S(1)} collective-permute-done((bf16[64,512]{1,0:T(8,128)(2,1)}, bf16[64,512]{1,0:T(8,128)(2,1)S(1)}, u32[]{:S(2)}, u32[]{:S(2)}) %collective-permute-start.3) | collective-permute-done | bytes 65568 | tf_op jit(solution)/shard_map/ppermute | solution.py:198
  12.0 1.5 %collective-permute-start.6 = (bf16[256,512]{1,0:T(8,128)(2,1)S(1)}, bf16[256,512]{1,0:T(8,128)(2,1)S(1)}, u32[]{:S(2)}, u32[]{:S(2)}) collective-permute-start(bf16[256,512]{1,0:T(8,128)(2,1)S(1)} %constant_dynamic-update-slice_fusion.q_ref), channel_id=1, source_target_pairs={{0,4},{1,3},{2,6},{3,1},{4,0},{5,7},{6,2},{7,5},{8,12},{9,11},{10,... | collective-permute-start | bytes 786440 | tf_op jit(solution)/shard_map/ppermute | solution.py:198
  13.5 1.6 %collective-permute-start.15 = (bf16[512,256]{1,0:T(8,128)(2,1)}, bf16[512,256]{1,0:T(8,128)(2,1)S(1)}, u32[]{:S(2)}, u32[]{:S(2)}) collective-permute-start(bf16[512,256]{1,0:T(8,128)(2,1)} %param.9), channel_id=1, source_target_pairs={{0,16},{1,17},{2,18},{3,19},{4,20},{5,21},{6,22},{7,23},{8,24},{9,... | collective-permute-start | bytes 786440 | tf_op jit(solution)/shard_map/ppermute | solution.py:198
  15.0 0.7 %compare_select_fusion.bias_ref = f32[8,16]{1,0:T(8,128)S(1)} fusion(s32[8,16]{1,0:T(8,128)} %param.8), kind=kLoop, calls=%fused_computation.9 | loop fusion | flops 256 | bytes 1024 | tf_op jit(solution)/shard_map/jit(_where)/select_n | solution.py:217
  15.7 1.5 %collective-permute-start = (f32[8,16]{1,0:T(8,128)S(1)}, f32[8,16]{1,0:T(8,128)S(1)}, u32[]{:S(2)}, u32[]{:S(2)}) collective-permute-start(f32[8,16]{1,0:T(8,128)S(1)} %compare_select_fusion.bias_ref), channel_id=1, source_target_pairs={{0,2},{1,5},{2,0},{3,7},{4,6},{5,1},{6,4},{7,3},{8,10},{9,13},{10,... | collective-permute-start | bytes 1544 | tf_op jit(solution)/shard_map/ppermute | solution.py:198
  17.2 0.0 copy-done
  17.2 0.0 copy-start.1
  17.2 1.0 %copy-done.1 = bf16[1,2048,128]{2,1,0:T(8,128)(2,1)S(1)} copy-done((bf16[1,2048,128]{2,1,0:T(8,128)(2,1)S(1)}, bf16[1,2048,128]{2,1,0:T(8,128)(2,1)}, u32[]{:S(2)}) %copy-start.1) | copy-done | bytes 524312
  18.3 0.1 stage.1
  18.4 2.7 %collective-permute-done.6.q_ref = bf16[256,512]{1,0:T(8,128)(2,1)S(1)} collective-permute-done((bf16[256,512]{1,0:T(8,128)(2,1)S(1)}, bf16[256,512]{1,0:T(8,128)(2,1)S(1)}, u32[]{:S(2)}, u32[]{:S(2)}) %collective-permute-start.6) | collective-permute-done | bytes 262176 | tf_op jit(solution)/shard_map/ppermute | solution.py:198
  21.1 2.5 %shard_map.57.refs_0_ = f32[256,512]{1,0:T(8,128)S(1)} custom-call(f32[8,16]{1,0:T(8,128)S(1)} %compare_select_fusion.bias_ref, bf16[256,512]{1,0:T(8,128)(2,1)S(1)} %collective-permute-done.6.q_ref, bf16[2048,128]{1,0:T(8,128)(2,1)S(1)} %get-tuple-element.15.k_ref, bf16[2048,128]{1,0:T(8,128)(2,1)S(1)} %get-tuple-element.16.v_ref), custom_call_target="tpu_custom_call" | custom-call | flops 1073741824 | bytes 1048576 | tf_op jit(solution)/shard_map/pallas_call | solution.py:81
  23.6 0.0 copy-start.2
  23.6 0.0 collective-permute-done.bias_ref
  23.6 0.0 collective-permute-done.4.k_ref
  23.6 0.0 collective-permute-done.5.v_ref
  23.6 2.5 %shard_map.58 = bf16[256,512]{1,0:T(8,128)(2,1)S(1)} custom-call(f32[8,16]{1,0:T(8,128)S(1)} %collective-permute-done.bias_ref, bf16[256,512]{1,0:T(8,128)(2,1)S(1)} %collective-permute-done.6.q_ref, bf16[2048,128]{1,0:T(8,128)(2,1)S(1)} %collective-permute-done.4.k_ref, bf16[2048,128]{1,0:T(8,128)(2,1)S(1)} %collective-permute-done.5.v_ref, ...), custom_call_target="tpu_custom_call" | custom-call | flops 1073741824 | bytes 1048576 | tf_op jit(solution)/shard_map/pallas_call | solution.py:81
  26.1 1.7 %collective-permute-start.7 = (bf16[256,512]{1,0:T(8,128)(2,1)S(1)}, bf16[256,512]{1,0:T(8,128)(2,1)S(1)}, u32[]{:S(2)}, u32[]{:S(2)}) collective-permute-start(bf16[256,512]{1,0:T(8,128)(2,1)S(1)} %shard_map.58), channel_id=1, source_target_pairs={{0,4},{1,3},{2,6},{3,1},{4,0},{5,7},{6,2},{7,5},{8,12},{9,11},{10,... | collective-permute-start | bytes 786440 | tf_op jit(solution)/shard_map/ppermute | solution.py:198
  27.8 0.0 collective-permute-done.15
  27.8 0.0 copy-done.2
  27.9 0.1 collective-permute-start.16
  27.9 2.5 %shard_map.55.refs_0_ = f32[256,512]{1,0:T(8,128)S(1)} custom-call(f32[8,16]{1,0:T(8,128)S(1)} %compare_select_fusion.bias_ref, bf16[256,512]{1,0:T(8,128)(2,1)S(1)} %constant_dynamic-update-slice_fusion.q_ref, bf16[2048,128]{1,0:T(8,128)(2,1)S(1)} %get-tuple-element.15.k_ref, bf16[2048,128]{1,0:T(8,128)(2,1)S(1)} %get-tuple-element.16.v_ref), custom_call_target="tpu_custom_call" | custom-call | flops 1073741824 | bytes 1048576 | tf_op jit(solution)/shard_map/pallas_call | solution.py:81
  30.4 2.5 %shard_map.56.part_ref = f32[256,512]{1,0:T(8,128)S(1)} custom-call(f32[8,16]{1,0:T(8,128)S(1)} %collective-permute-done.bias_ref, bf16[256,512]{1,0:T(8,128)(2,1)S(1)} %constant_dynamic-update-slice_fusion.q_ref, bf16[2048,128]{1,0:T(8,128)(2,1)S(1)} %collective-permute-done.4.k_ref, bf16[2048,128]{1,0:T(8,128)(2,1)S(1)} %collective-permute-done.5.v_ref, ...), custom_call_target="tpu_custom_call" | custom-call | flops 1073741824 | bytes 1048576 | tf_op jit(solution)/shard_map/pallas_call | solution.py:81
  32.9 0.0 collective-permute-done.7.share_ref
  33.0 3.7 %collective-permute-start.10 = (bf16[64,512]{1,0:T(8,128)(2,1)S(1)}, bf16[64,512]{1,0:T(8,128)(2,1)S(1)}, u32[]{:S(2)}, u32[]{:S(2)}) collective-permute-start(bf16[64,512]{1,0:T(8,128)(2,1)S(1)} %get-tuple-element.20), channel_id=1, source_target_pairs={{0,24},{1,25},{2,26},{3,27},{4,28},{5,29},{6,30},{7,31},{8,16},{9,... | collective-permute-start | bytes 196616 | tf_op jit(solution)/shard_map/ppermute | solution.py:198
  36.6 0.0 collective-permute-start.9
  36.6 0.8 %collective-permute-start.8 = (bf16[64,512]{1,0:T(8,128)(2,1)S(1)}, bf16[64,512]{1,0:T(8,128)(2,1)S(1)}, u32[]{:S(2)}, u32[]{:S(2)}) collective-permute-start(bf16[64,512]{1,0:T(8,128)(2,1)S(1)} %get-tuple-element.18), channel_id=1, source_target_pairs={{0,8},{1,9},{2,10},{3,11},{4,12},{5,13},{6,14},{7,15},{8,0},{9,1},... | collective-permute-start | bytes 196616 | tf_op jit(solution)/shard_map/ppermute | solution.py:198
  37.4 0.0 collective-permute-done.16
  37.5 1.3 %collective-permute-start.17 = (bf16[1024,256]{1,0:T(8,128)(2,1)S(1)}, bf16[1024,256]{1,0:T(8,128)(2,1)S(1)}, u32[]{:S(2)}, u32[]{:S(2)}) collective-permute-start(bf16[1024,256]{1,0:T(8,128)(2,1)S(1)} %pad_maximum_fusion.refs_2_), channel_id=1, source_target_pairs={{0,8},{1,9},{2,10},{3,11},{4,12},{5,13},{6,14},{7,15},{8,0},{9,1},... | collective-permute-start | bytes 1572872 | tf_op jit(solution)/shard_map/ppermute | solution.py:198
  38.8 1.0 %collective-permute-done.10 = bf16[64,512]{1,0:T(8,128)(2,1)S(1)} collective-permute-done((bf16[64,512]{1,0:T(8,128)(2,1)S(1)}, bf16[64,512]{1,0:T(8,128)(2,1)S(1)}, u32[]{:S(2)}, u32[]{:S(2)}) %collective-permute-start.10) | collective-permute-done | bytes 65568 | tf_op jit(solution)/shard_map/ppermute | solution.py:198
  39.8 2.5 %collective-permute-done.9 = bf16[64,512]{1,0:T(8,128)(2,1)S(1)} collective-permute-done((bf16[64,512]{1,0:T(8,128)(2,1)S(1)}, bf16[64,512]{1,0:T(8,128)(2,1)S(1)}, u32[]{:S(2)}, u32[]{:S(2)}) %collective-permute-start.9) | collective-permute-done | bytes 65568 | tf_op jit(solution)/shard_map/ppermute | solution.py:198
  42.3 0.7 %collective-permute-done.8 = bf16[64,512]{1,0:T(8,128)(2,1)S(1)} collective-permute-done((bf16[64,512]{1,0:T(8,128)(2,1)S(1)}, bf16[64,512]{1,0:T(8,128)(2,1)S(1)}, u32[]{:S(2)}, u32[]{:S(2)}) %collective-permute-start.8) | collective-permute-done | bytes 65568 | tf_op jit(solution)/shard_map/ppermute | solution.py:198
  43.1 2.2 %collective-permute-start.13 = (bf16[64,512]{1,0:T(8,128)(2,1)S(1)}, bf16[64,512]{1,0:T(8,128)(2,1)S(1)}, u32[]{:S(2)}, u32[]{:S(2)}) collective-permute-start(bf16[64,512]{1,0:T(8,128)(2,1)S(1)} %add_convert_fusion), channel_id=1, source_target_pairs={{0,6},{1,7},{2,4},{3,5},{4,2},{5,3},{6,0},{7,1},{8,14},{9,15},{10,... | collective-permute-start | bytes 196616 | tf_op jit(solution)/shard_map/ppermute | solution.py:198
  45.3 0.8 %collective-permute-start.12 = (bf16[64,512]{1,0:T(8,128)(2,1)S(1)}, bf16[64,512]{1,0:T(8,128)(2,1)S(1)}, u32[]{:S(2)}, u32[]{:S(2)}) collective-permute-start(bf16[64,512]{1,0:T(8,128)(2,1)S(1)} %add_convert_fusion), channel_id=1, source_target_pairs={{0,4},{1,5},{2,6},{3,7},{4,0},{5,1},{6,2},{7,3},{8,12},{9,13},{10,... | collective-permute-start | bytes 196616 | tf_op jit(solution)/shard_map/ppermute | solution.py:198
  46.1 0.5 collective-permute-start.11
  46.6 1.7 %collective-permute-done.13 = bf16[64,512]{1,0:T(8,128)(2,1)S(1)} collective-permute-done((bf16[64,512]{1,0:T(8,128)(2,1)S(1)}, bf16[64,512]{1,0:T(8,128)(2,1)S(1)}, u32[]{:S(2)}, u32[]{:S(2)}) %collective-permute-start.13) | collective-permute-done | bytes 65568 | tf_op jit(solution)/shard_map/ppermute | solution.py:198
  48.3 1.3 %collective-permute-done.12 = bf16[64,512]{1,0:T(8,128)(2,1)S(1)} collective-permute-done((bf16[64,512]{1,0:T(8,128)(2,1)S(1)}, bf16[64,512]{1,0:T(8,128)(2,1)S(1)}, u32[]{:S(2)}, u32[]{:S(2)}) %collective-permute-start.12) | collective-permute-done | bytes 65568 | tf_op jit(solution)/shard_map/ppermute | solution.py:198
  49.5 0.8 %collective-permute-done.11 = bf16[64,512]{1,0:T(8,128)(2,1)S(1)} collective-permute-done((bf16[64,512]{1,0:T(8,128)(2,1)S(1)}, bf16[64,512]{1,0:T(8,128)(2,1)S(1)}, u32[]{:S(2)}, u32[]{:S(2)}) %collective-permute-start.11) | collective-permute-done | bytes 65568 | tf_op jit(solution)/shard_map/ppermute | solution.py:198
  50.4 0.1 collective-permute-start.14
  50.4 3.2 %collective-permute-done.17.refs_3_ = bf16[1024,256]{1,0:T(8,128)(2,1)S(1)} collective-permute-done((bf16[1024,256]{1,0:T(8,128)(2,1)S(1)}, bf16[1024,256]{1,0:T(8,128)(2,1)S(1)}, u32[]{:S(2)}, u32[]{:S(2)}) %collective-permute-start.17) | collective-permute-done | bytes 524320 | tf_op jit(solution)/shard_map/ppermute | solution.py:198
  53.7 0.0 collective-permute-done.14.refs_1_
  53.7 0.4 shard_map.60
  54.1 1.6 %collective-permute-start.18 = (bf16[64,512]{1,0:T(8,128)(2,1)S(1)}, bf16[64,512]{1,0:T(8,128)(2,1)S(1)}, u32[]{:S(2)}, u32[]{:S(2)}) collective-permute-start(bf16[64,512]{1,0:T(8,128)(2,1)S(1)} %get-tuple-element.22), channel_id=1, source_target_pairs={{0,2},{1,3},{2,0},{3,1},{4,6},{5,7},{6,4},{7,5},{8,10},{9,11},{10,... | collective-permute-start | bytes 196616 | tf_op jit(solution)/shard_map/ppermute | solution.py:198
  55.7 0.9 %collective-permute-start.19 = (bf16[64,512]{1,0:T(8,128)(2,1)S(1)}, bf16[64,512]{1,0:T(8,128)(2,1)S(1)}, u32[]{:S(2)}, u32[]{:S(2)}) collective-permute-start(bf16[64,512]{1,0:T(8,128)(2,1)S(1)} %get-tuple-element.23), channel_id=1, source_target_pairs={{0,4},{1,5},{2,6},{3,7},{4,0},{5,1},{6,2},{7,3},{8,12},{9,13},{10,... | collective-permute-start | bytes 196616 | tf_op jit(solution)/shard_map/ppermute | solution.py:198
  56.6 1.1 %collective-permute-start.20 = (bf16[64,512]{1,0:T(8,128)(2,1)S(1)}, bf16[64,512]{1,0:T(8,128)(2,1)S(1)}, u32[]{:S(2)}, u32[]{:S(2)}) collective-permute-start(bf16[64,512]{1,0:T(8,128)(2,1)S(1)} %get-tuple-element.24), channel_id=1, source_target_pairs={{0,6},{1,7},{2,4},{3,5},{4,2},{5,3},{6,0},{7,1},{8,14},{9,15},{10,... | collective-permute-start | bytes 196616 | tf_op jit(solution)/shard_map/ppermute | solution.py:198
  57.7 0.8 %collective-permute-done.18.refs_1_ = bf16[64,512]{1,0:T(8,128)(2,1)S(1)} collective-permute-done((bf16[64,512]{1,0:T(8,128)(2,1)S(1)}, bf16[64,512]{1,0:T(8,128)(2,1)S(1)}, u32[]{:S(2)}, u32[]{:S(2)}) %collective-permute-start.18) | collective-permute-done | bytes 65568 | tf_op jit(solution)/shard_map/ppermute | solution.py:198
  58.5 1.8 %collective-permute-done.19.refs_2_ = bf16[64,512]{1,0:T(8,128)(2,1)S(1)} collective-permute-done((bf16[64,512]{1,0:T(8,128)(2,1)S(1)}, bf16[64,512]{1,0:T(8,128)(2,1)S(1)}, u32[]{:S(2)}, u32[]{:S(2)}) %collective-permute-start.19) | collective-permute-done | bytes 65568 | tf_op jit(solution)/shard_map/ppermute | solution.py:198
  60.2 1.6 %collective-permute-done.20.refs_3_ = bf16[64,512]{1,0:T(8,128)(2,1)S(1)} collective-permute-done((bf16[64,512]{1,0:T(8,128)(2,1)S(1)}, bf16[64,512]{1,0:T(8,128)(2,1)S(1)}, u32[]{:S(2)}, u32[]{:S(2)}) %collective-permute-start.20) | collective-permute-done | bytes 65568 | tf_op jit(solution)/shard_map/ppermute | solution.py:198
  61.8 0.8 %shard_map.61 = bf16[64,2048]{1,0:T(8,128)(2,1)} custom-call(bf16[64,512]{1,0:T(8,128)(2,1)S(1)} %get-tuple-element.21.refs_0_, bf16[64,512]{1,0:T(8,128)(2,1)S(1)} %collective-permute-done.18.refs_1_, bf16[64,512]{1,0:T(8,128)(2,1)S(1)} %collective-permute-done.19.refs_2_, bf16[64,512]{1,0:T(8,128)(2,1)S(1)} %collective-permute-done.20.refs_3_), custom_call_target="tpu_custom_call" | custom-call | bytes 1048576 | tf_op jit(solution)/shard_map/pallas_call | solution.py:96
  (8 shorter events, 0.2 us)
Async XLA Ops:
  0.0 17.2 %copy-start = (bf16[1,2048,128]{2,1,0:T(8,128)(2,1)S(1)}, bf16[1,2048,128]{2,1,0:T(8,128)(2,1)}, u32[]{:S(2)}) copy-start(bf16[1,2048,128]{2,1,0:T(8,128)(2,1)} %param.6) | copy-start | bytes 1572868
  0.0 8.5 %collective-permute-start.1 = (bf16[64,512]{1,0:T(8,128)(2,1)}, bf16[64,512]{1,0:T(8,128)(2,1)S(1)}, u32[]{:S(2)}, u32[]{:S(2)}) collective-permute-start(bf16[64,512]{1,0:T(8,128)(2,1)} %param.5), channel_id=1, source_target_pairs={{0,8},{1,9},{2,10},{3,11},{4,12},{5,13},{6,14},{7,15},{8,0},{9,1},... | collective-permute-start | bytes 196616 | tf_op jit(solution)/shard_map/ppermute | solution.py:198
  3.1 7.5 %collective-permute-start.2 = (bf16[64,512]{1,0:T(8,128)(2,1)}, bf16[64,512]{1,0:T(8,128)(2,1)S(1)}, u32[]{:S(2)}, u32[]{:S(2)}) collective-permute-start(bf16[64,512]{1,0:T(8,128)(2,1)} %param.5), channel_id=1, source_target_pairs={{0,16},{1,17},{2,18},{3,19},{4,20},{5,21},{6,22},{7,23},{8,24},{9,... | collective-permute-start | bytes 196616 | tf_op jit(solution)/shard_map/ppermute | solution.py:198
  5.6 6.3 %collective-permute-start.3 = (bf16[64,512]{1,0:T(8,128)(2,1)}, bf16[64,512]{1,0:T(8,128)(2,1)S(1)}, u32[]{:S(2)}, u32[]{:S(2)}) collective-permute-start(bf16[64,512]{1,0:T(8,128)(2,1)} %param.5), channel_id=1, source_target_pairs={{0,24},{1,25},{2,26},{3,27},{4,28},{5,29},{6,30},{7,31},{8,16},{9,... | collective-permute-start | bytes 196616 | tf_op jit(solution)/shard_map/ppermute | solution.py:198
  5.6 18.0 %collective-permute-start.4 = (bf16[2048,128]{1,0:T(8,128)(2,1)}, bf16[2048,128]{1,0:T(8,128)(2,1)S(1)}, u32[]{:S(2)}, u32[]{:S(2)}) collective-permute-start(bf16[2048,128]{1,0:T(8,128)(2,1)} %bitcast.2), channel_id=1, source_target_pairs={{0,2},{1,5},{2,0},{3,7},{4,6},{5,1},{6,4},{7,3},{8,10},{9,13},{10,... | collective-permute-start | bytes 1572872 | tf_op jit(solution)/shard_map/ppermute | solution.py:198
  7.4 16.3 %collective-permute-start.5 = (bf16[2048,128]{1,0:T(8,128)(2,1)}, bf16[2048,128]{1,0:T(8,128)(2,1)S(1)}, u32[]{:S(2)}, u32[]{:S(2)}) collective-permute-start(bf16[2048,128]{1,0:T(8,128)(2,1)} %bitcast.4), channel_id=1, source_target_pairs={{0,2},{1,5},{2,0},{3,7},{4,6},{5,1},{6,4},{7,3},{8,10},{9,13},{10,... | collective-permute-start | bytes 1572872 | tf_op jit(solution)/shard_map/ppermute | solution.py:198
  12.0 9.2 %collective-permute-start.6 = (bf16[256,512]{1,0:T(8,128)(2,1)S(1)}, bf16[256,512]{1,0:T(8,128)(2,1)S(1)}, u32[]{:S(2)}, u32[]{:S(2)}) collective-permute-start(bf16[256,512]{1,0:T(8,128)(2,1)S(1)} %constant_dynamic-update-slice_fusion.q_ref), channel_id=1, source_target_pairs={{0,4},{1,3},{2,6},{3,1},{4,0},{5,7},{6,2},{7,5},{8,12},{9,11},{10,... | collective-permute-start | bytes 786440 | tf_op jit(solution)/shard_map/ppermute | solution.py:198
  13.5 14.3 %collective-permute-start.15 = (bf16[512,256]{1,0:T(8,128)(2,1)}, bf16[512,256]{1,0:T(8,128)(2,1)S(1)}, u32[]{:S(2)}, u32[]{:S(2)}) collective-permute-start(bf16[512,256]{1,0:T(8,128)(2,1)} %param.9), channel_id=1, source_target_pairs={{0,16},{1,17},{2,18},{3,19},{4,20},{5,21},{6,22},{7,23},{8,24},{9,... | collective-permute-start | bytes 786440 | tf_op jit(solution)/shard_map/ppermute | solution.py:198
  15.7 7.9 %collective-permute-start = (f32[8,16]{1,0:T(8,128)S(1)}, f32[8,16]{1,0:T(8,128)S(1)}, u32[]{:S(2)}, u32[]{:S(2)}) collective-permute-start(f32[8,16]{1,0:T(8,128)S(1)} %compare_select_fusion.bias_ref), channel_id=1, source_target_pairs={{0,2},{1,5},{2,0},{3,7},{4,6},{5,1},{6,4},{7,3},{8,10},{9,13},{10,... | collective-permute-start | bytes 1544 | tf_op jit(solution)/shard_map/ppermute | solution.py:198
  17.2 1.0 %copy-start.1 = (bf16[1,2048,128]{2,1,0:T(8,128)(2,1)S(1)}, bf16[1,2048,128]{2,1,0:T(8,128)(2,1)}, u32[]{:S(2)}) copy-start(bf16[1,2048,128]{2,1,0:T(8,128)(2,1)} %param.7) | copy-start | bytes 1572868
  23.6 4.2 %copy-start.2 = (bf16[512,256]{1,0:T(8,128)(2,1)S(1)}, bf16[512,256]{1,0:T(8,128)(2,1)}, u32[]{:S(2)}) copy-start(bf16[512,256]{1,0:T(8,128)(2,1)} %param.9) | copy-start | bytes 786436
  26.1 6.8 %collective-permute-start.7 = (bf16[256,512]{1,0:T(8,128)(2,1)S(1)}, bf16[256,512]{1,0:T(8,128)(2,1)S(1)}, u32[]{:S(2)}, u32[]{:S(2)}) collective-permute-start(bf16[256,512]{1,0:T(8,128)(2,1)S(1)} %shard_map.58), channel_id=1, source_target_pairs={{0,4},{1,3},{2,6},{3,1},{4,0},{5,7},{6,2},{7,5},{8,12},{9,11},{10,... | collective-permute-start | bytes 786440 | tf_op jit(solution)/shard_map/ppermute | solution.py:198
  27.9 9.6 %collective-permute-start.16 = (bf16[512,256]{1,0:T(8,128)(2,1)S(1)}, bf16[512,256]{1,0:T(8,128)(2,1)S(1)}, u32[]{:S(2)}, u32[]{:S(2)}) collective-permute-start(bf16[512,256]{1,0:T(8,128)(2,1)S(1)} %get-tuple-element.26), channel_id=1, source_target_pairs={{0,1},{1,0},{2,3},{3,2},{4,5},{5,4},{6,7},{7,6},{8,9},{9,8},{10,11... | collective-permute-start | bytes 786440 | tf_op jit(solution)/shard_map/ppermute | solution.py:198
  33.0 6.8 %collective-permute-start.10 = (bf16[64,512]{1,0:T(8,128)(2,1)S(1)}, bf16[64,512]{1,0:T(8,128)(2,1)S(1)}, u32[]{:S(2)}, u32[]{:S(2)}) collective-permute-start(bf16[64,512]{1,0:T(8,128)(2,1)S(1)} %get-tuple-element.20), channel_id=1, source_target_pairs={{0,24},{1,25},{2,26},{3,27},{4,28},{5,29},{6,30},{7,31},{8,16},{9,... | collective-permute-start | bytes 196616 | tf_op jit(solution)/shard_map/ppermute | solution.py:198
  36.6 5.7 %collective-permute-start.9 = (bf16[64,512]{1,0:T(8,128)(2,1)S(1)}, bf16[64,512]{1,0:T(8,128)(2,1)S(1)}, u32[]{:S(2)}, u32[]{:S(2)}) collective-permute-start(bf16[64,512]{1,0:T(8,128)(2,1)S(1)} %get-tuple-element.19), channel_id=1, source_target_pairs={{0,16},{1,17},{2,18},{3,19},{4,20},{5,21},{6,22},{7,23},{8,24},{9,... | collective-permute-start | bytes 196616 | tf_op jit(solution)/shard_map/ppermute | solution.py:198
  36.6 6.4 %collective-permute-start.8 = (bf16[64,512]{1,0:T(8,128)(2,1)S(1)}, bf16[64,512]{1,0:T(8,128)(2,1)S(1)}, u32[]{:S(2)}, u32[]{:S(2)}) collective-permute-start(bf16[64,512]{1,0:T(8,128)(2,1)S(1)} %get-tuple-element.18), channel_id=1, source_target_pairs={{0,8},{1,9},{2,10},{3,11},{4,12},{5,13},{6,14},{7,15},{8,0},{9,1},... | collective-permute-start | bytes 196616 | tf_op jit(solution)/shard_map/ppermute | solution.py:198
  37.5 16.2 %collective-permute-start.17 = (bf16[1024,256]{1,0:T(8,128)(2,1)S(1)}, bf16[1024,256]{1,0:T(8,128)(2,1)S(1)}, u32[]{:S(2)}, u32[]{:S(2)}) collective-permute-start(bf16[1024,256]{1,0:T(8,128)(2,1)S(1)} %pad_maximum_fusion.refs_2_), channel_id=1, source_target_pairs={{0,8},{1,9},{2,10},{3,11},{4,12},{5,13},{6,14},{7,15},{8,0},{9,1},... | collective-permute-start | bytes 1572872 | tf_op jit(solution)/shard_map/ppermute | solution.py:198
  43.1 5.2 %collective-permute-start.13 = (bf16[64,512]{1,0:T(8,128)(2,1)S(1)}, bf16[64,512]{1,0:T(8,128)(2,1)S(1)}, u32[]{:S(2)}, u32[]{:S(2)}) collective-permute-start(bf16[64,512]{1,0:T(8,128)(2,1)S(1)} %add_convert_fusion), channel_id=1, source_target_pairs={{0,6},{1,7},{2,4},{3,5},{4,2},{5,3},{6,0},{7,1},{8,14},{9,15},{10,... | collective-permute-start | bytes 196616 | tf_op jit(solution)/shard_map/ppermute | solution.py:198
  45.3 4.3 %collective-permute-start.12 = (bf16[64,512]{1,0:T(8,128)(2,1)S(1)}, bf16[64,512]{1,0:T(8,128)(2,1)S(1)}, u32[]{:S(2)}, u32[]{:S(2)}) collective-permute-start(bf16[64,512]{1,0:T(8,128)(2,1)S(1)} %add_convert_fusion), channel_id=1, source_target_pairs={{0,4},{1,5},{2,6},{3,7},{4,0},{5,1},{6,2},{7,3},{8,12},{9,13},{10,... | collective-permute-start | bytes 196616 | tf_op jit(solution)/shard_map/ppermute | solution.py:198
  46.1 4.3 %collective-permute-start.11 = (bf16[64,512]{1,0:T(8,128)(2,1)S(1)}, bf16[64,512]{1,0:T(8,128)(2,1)S(1)}, u32[]{:S(2)}, u32[]{:S(2)}) collective-permute-start(bf16[64,512]{1,0:T(8,128)(2,1)S(1)} %add_convert_fusion), channel_id=1, source_target_pairs={{0,2},{1,3},{2,0},{3,1},{4,6},{5,7},{6,4},{7,5},{8,10},{9,11},{10,... | collective-permute-start | bytes 196616 | tf_op jit(solution)/shard_map/ppermute | solution.py:198
  50.4 3.3 %collective-permute-start.14 = (bf16[256,512]{1,0:T(8,128)(2,1)S(1)}, bf16[256,512]{1,0:T(8,128)(2,1)S(1)}, u32[]{:S(2)}, u32[]{:S(2)}) collective-permute-start(bf16[256,512]{1,0:T(8,128)(2,1)S(1)} %pad_maximum_fusion.1.refs_0_), channel_id=1, source_target_pairs={{0,1},{1,0},{2,3},{3,2},{4,5},{5,4},{6,7},{7,6},{8,9},{9,8},{10,11... | collective-permute-start | bytes 786440 | tf_op jit(solution)/shard_map/ppermute | solution.py:198
  54.1 4.3 %collective-permute-start.18 = (bf16[64,512]{1,0:T(8,128)(2,1)S(1)}, bf16[64,512]{1,0:T(8,128)(2,1)S(1)}, u32[]{:S(2)}, u32[]{:S(2)}) collective-permute-start(bf16[64,512]{1,0:T(8,128)(2,1)S(1)} %get-tuple-element.22), channel_id=1, source_target_pairs={{0,2},{1,3},{2,0},{3,1},{4,6},{5,7},{6,4},{7,5},{8,10},{9,11},{10,... | collective-permute-start | bytes 196616 | tf_op jit(solution)/shard_map/ppermute | solution.py:198
  55.7 4.5 %collective-permute-start.19 = (bf16[64,512]{1,0:T(8,128)(2,1)S(1)}, bf16[64,512]{1,0:T(8,128)(2,1)S(1)}, u32[]{:S(2)}, u32[]{:S(2)}) collective-permute-start(bf16[64,512]{1,0:T(8,128)(2,1)S(1)} %get-tuple-element.23), channel_id=1, source_target_pairs={{0,4},{1,5},{2,6},{3,7},{4,0},{5,1},{6,2},{7,3},{8,12},{9,13},{10,... | collective-permute-start | bytes 196616 | tf_op jit(solution)/shard_map/ppermute | solution.py:198
  56.6 5.2 %collective-permute-start.20 = (bf16[64,512]{1,0:T(8,128)(2,1)S(1)}, bf16[64,512]{1,0:T(8,128)(2,1)S(1)}, u32[]{:S(2)}, u32[]{:S(2)}) collective-permute-start(bf16[64,512]{1,0:T(8,128)(2,1)S(1)} %get-tuple-element.24), channel_id=1, source_target_pairs={{0,6},{1,7},{2,4},{3,5},{4,2},{5,3},{6,0},{7,1},{8,14},{9,15},{10,... | collective-permute-start | bytes 196616 | tf_op jit(solution)/shard_map/ppermute | solution.py:198

commit v2 on v1

v2 whole, which is shorter than its diff:
```python
import functools
import math

import jax
import jax.numpy as jnp
from jax import lax
from jax.experimental import pallas as pl
from jax.experimental.pallas import tpu as pltpu
from jax.sharding import PartitionSpec as P


BLK = 128
TILE = 256
VMEM_LIMIT = 24 * 1024 * 1024
LOG2E = math.log2(math.e)
BOTH = ("seq", "head")


def attend_kernel(own_rows, flip, members, sources, has_acc, q_ref, *refs):
    given, refs = refs[: 3 * sources], refs[3 * sources :]
    if has_acc:
        acc_in, refs = refs[0], refs[1:]
    out_ref, stacked, total = refs
    width = q_ref.shape[1]
    cached, head_size = given[1].shape
    group = width // head_size
    part = group * own_rows
    tile = min(TILE, cached)
    scale = -LOG2E / math.sqrt(head_size)
    seq = lax.axis_index("seq")
    plane = lax.rem(seq, 4)
    line = lax.div(seq, 4)
    odd = lax.rem(lax.axis_index("head"), 2)
    plane = plane ^ jnp.where(odd == 1, flip[1], flip[0])
    for j, member in enumerate(members):
        for i in range(group):
            stacked[j * part + i * own_rows : j * part + (i + 1) * own_rows, :] = q_ref[
                member * own_rows : (member + 1) * own_rows, i * head_size : (i + 1) * head_size
            ]
    for n in range(sources):
        bias_ref, k_ref, v_ref = given[3 * n : 3 * n + 3]
        biases = []
        for member in members:
            mask_row = ((line ^ member) * 4 + plane) * own_rows // BLK
            biases.append(bias_ref[pl.ds(mask_row, 1), :])
        for t in range(cached // tile):
            score = lax.dot_general(
                stacked[...],
                k_ref[t * tile : (t + 1) * tile, :],
                (((1,), (1,)), ((), ())),
                preferred_element_type=jnp.float32,
            )
            weights = []
            for j in range(len(members)):
                bias = jnp.concatenate(
                    [
                        jnp.broadcast_to(biases[j][:, c : c + 1], (1, BLK))
                        for c in range(t * (tile // BLK), (t + 1) * (tile // BLK))
                    ],
                    axis=1,
                )
                grown = jnp.exp2(score[j * part : (j + 1) * part] * scale + bias)
                weights.append((1.0 / (1.0 + grown)).astype(jnp.bfloat16))
            weight = jnp.concatenate(weights, axis=0)
            term = jnp.dot(weight, v_ref[t * tile : (t + 1) * tile, :], preferred_element_type=jnp.float32)
            total[...] = term if n == 0 and t == 0 else total[...] + term
    for j in range(len(members)):
        for i in range(group):
            here = (slice(j * own_rows, (j + 1) * own_rows), slice(i * head_size, (i + 1) * head_size))
            value = total[j * part + i * own_rows : j * part + (i + 1) * own_rows, :]
            if has_acc:
                value = value + acc_in[here]
            out_ref[here] = value.astype(out_ref.dtype)


def attend(q, sources, own_rows, flip, members, acc, dtype):
    width = q.shape[1]
    cached, head_size = sources[0][1].shape
    rows = len(members) * own_rows
    stacked = (rows * width // head_size, head_size)
    scores = stacked[0] * cached * len(sources)
    vmem = pl.BlockSpec(memory_space=pltpu.VMEM)
    args = [q] + [x for source in sources for x in source] + ([] if acc is None else [acc])
    return pl.pallas_call(
        functools.partial(attend_kernel, own_rows, flip, members, len(sources), acc is not None),
        out_shape=jax.ShapeDtypeStruct((rows, width), dtype),
        in_specs=[vmem] * len(args),
        out_specs=vmem,
        scratch_shapes=[pltpu.VMEM(stacked, jnp.bfloat16), pltpu.VMEM(stacked, jnp.float32)],
        compiler_params=pltpu.CompilerParams(vmem_limit_bytes=VMEM_LIMIT),
        cost_estimate=pl.CostEstimate(
            flops=4 * scores * head_size, transcendentals=2 * scores, bytes_accessed=4 * cached * head_size
        ),
    )(*args)


def small_call(kernel, out_shapes, args, flops=0):
    vmem = pl.BlockSpec(memory_space=pltpu.VMEM)
    return pl.pallas_call(
        kernel,
        out_shape=out_shapes,
        in_specs=[vmem] * len(args),
        out_specs=jax.tree.map(lambda _: vmem, out_shapes),
        compiler_params=pltpu.CompilerParams(vmem_limit_bytes=VMEM_LIMIT),
        cost_estimate=pl.CostEstimate(flops=flops, transcendentals=0, bytes_accessed=1 << 20),
    )(*args)


def stage_kernel(key_far, value_far, key_here, value_here, sems):
    copies = [
        pltpu.make_async_copy(far, here, sems.at[i])
        for i, (far, here) in enumerate(((key_far, key_here), (value_far, value_here)))
    ]
    for copy in copies:
        copy.start()
    for copy in copies:
        copy.wait()


def stage(keys, values):
    vmem = pl.BlockSpec(memory_space=pltpu.VMEM)
    return pl.pallas_call(
        stage_kernel,
        name="stage",
        out_shape=[jax.ShapeDtypeStruct(x.shape, x.dtype) for x in (keys, values)],
        in_specs=[pl.BlockSpec(memory_space=pl.ANY)] * 2,
        out_specs=[vmem] * 2,
        scratch_shapes=[pltpu.SemaphoreType.DMA((2,))],
        compiler_params=pltpu.CompilerParams(vmem_limit_bytes=VMEM_LIMIT),
        cost_estimate=pl.CostEstimate(flops=0, transcendentals=0, bytes_accessed=4 * keys.size),
    )(keys, values)


def merge_kernel(members, part_ref, share_ref, *out_refs):
    own_rows = out_refs[0].shape[0]
    for j, member in enumerate(members):
        value = part_ref[member * own_rows : (member + 1) * own_rows, :]
        value = value + share_ref[j * own_rows : (j + 1) * own_rows, :].astype(jnp.float32)
        out_refs[j][...] = value.astype(out_refs[j].dtype)


def project_kernel(heads, *refs):
    inputs, refs = refs[:heads], refs[heads:]
    blocks, outs = refs[:-4], refs[-4:]
    own_rows = outs[0].shape[0]
    width = inputs[0].shape[1]
    columns = blocks[0].shape[1]
    for m, block in enumerate(blocks):
        value = None
        for k in range(heads):
            term = jnp.dot(
                inputs[k][...], block[k * width : (k + 1) * width, :], preferred_element_type=jnp.float32
            )
            value = term if value is None else value + term
        value = value.astype(jnp.bfloat16)
        for k in range(4):
            outs[k][:, m * columns : (m + 1) * columns] = value[k * own_rows : (k + 1) * own_rows]


def place_kernel(*refs):
    got, out_ref = refs[:4], refs[4]
    columns = got[0].shape[1] // 2
    seq = lax.axis_index("seq")
    pieces = [[g[:, :columns], g[:, columns:]] for g in got]
    here = lax.rem(seq, 2) == 1
    pieces = [[jnp.where(here, b, a) for a, b in zip(pieces[k], pieces[k ^ 1])] for k in range(4)]
    here = lax.rem(lax.div(seq, 4), 2) == 1
    pieces = [[jnp.where(here, b, a) for a, b in zip(pieces[k], pieces[k ^ 2])] for k in range(4)]
    here = lax.rem(lax.div(seq, 2), 2) == 1
    for k in range(4):
        for m in range(2):
            at = ((k // 2) * 4 + m * 2 + k % 2) * columns
            out_ref[:, at : at + columns] = jnp.where(here, pieces[k][m ^ 1], pieces[k][m])


def on_device(queries, keys, values, mask, out_proj):
    seq_size, heads = lax.axis_size("seq"), lax.axis_size("head")
    lines = seq_size // 4
    per_head = lines // heads
    assert per_head == 2
    own_rows = queries.shape[0]
    columns = out_proj.shape[1]
    total_keys = keys.shape[1] * seq_size
    line, head = lax.axis_index("seq") // 4, lax.axis_index("head")

    def move(x, target):
        pairs = []
        for s in range(seq_size):
            for h in range(heads):
                to = target(s // 4, s % 4, h)
                if to is not None:
                    pairs.append((s * heads + h, (to[0] * 4 + to[1]) * heads + to[2]))
        return lax.ppermute(x, BOTH, pairs)

    def pair(x):
        return move(x, lambda z, p, h: (z, p ^ (1 + h % 2), h))

    def other(x):
        return move(x, lambda z, p, h: (z, p ^ (2 - h % 2), h))

    def along(x, k):
        return move(x, lambda z, p, h: (z ^ k, p, h))

    def inside(x, k):
        return move(x, lambda z, p, h: (z ^ (k >> 1), p ^ (k & 1), h))

    def across(x, k):
        return move(x, lambda z, p, h: (z, p, h ^ k))

    key_own, value_own = keys[0], values[0]
    lined = [queries] + [along(queries, k) for k in range(1, lines)]
    bias = jnp.where(mask > 0, jnp.float32(math.log(total_keys) * LOG2E), jnp.float32(1e30))
    bias_pair, key_pair, value_pair = pair(bias), pair(key_own), pair(value_own)
    q_own = jnp.concatenate(lined, axis=0)
    q_other = other(q_own)

    held, step = [out_proj], 2
    while step < lines:
        held += [along(block, step) for block in held]
        step *= 2
    bit = 1
    while bit < heads:
        here = ((line // 2) ^ head) // bit % 2 == 1
        held = [jnp.where(here, held[i ^ bit], held[i]) for i in range(heads)]
        bit *= 2
    rows_all = jnp.concatenate([held[0]] + [across(held[k], k) for k in range(1, heads)], axis=0)
    proj = [rows_all, move(rows_all, lambda z, p, h: (z, p ^ 2, h))]

    near, far = (bias, *stage(key_own, value_own)), (bias_pair, key_pair, value_pair)

    def attention(q, sources, flip, members, acc=None, dtype=jnp.float32):
        return attend(q, sources, own_rows, flip, members, acc, dtype)

    every, upper, lower = range(lines), range(lines // 2, lines), range(lines // 2)
    part = attention(q_own, [near], (0, 0), every)
    share_upper = attention(q_other, [near, far], (2, 1), upper, dtype=jnp.bfloat16)
    share_upper = other(share_upper)
    share_lower = attention(q_other, [near, far], (2, 1), lower, dtype=jnp.bfloat16)
    share_lower = other(share_lower)
    part = attention(q_own, [far], (0, 0), every, part)
    width = part.shape[1]

    def merge(share, members):
        shapes = [jax.ShapeDtypeStruct((own_rows, width), jnp.bfloat16 if m else jnp.float32) for m in members]
        return small_call(functools.partial(merge_kernel, members), shapes, [part, share])

    merged = merge(share_upper, upper)
    merged = merge(share_lower, lower) + merged
    sums = merged[0]
    for k in range(1, lines):
        sums = sums + along(merged[k], k).astype(jnp.float32)
    attended = sums.astype(jnp.bfloat16)

    quad = jnp.concatenate([attended] + [inside(attended, k) for k in range(1, 4)], axis=0)
    full = [quad] + [across(quad, k) for k in range(1, heads)]
    piece = jax.ShapeDtypeStruct((own_rows, per_head * columns), jnp.bfloat16)
    result = small_call(
        functools.partial(project_kernel, heads),
        [piece] * 4,
        full + proj,
        flops=8 * own_rows * heads * width * per_head * columns,
    )
    got = [result[0]] + [inside(result[k], k) for k in range(1, 4)]
    return small_call(place_kernel, jax.ShapeDtypeStruct((own_rows, 4 * per_head * columns), jnp.bfloat16), got)


def solution(mesh):
    placed = (
        P("seq", "head"),
        P("head", "seq", None),
        P("head", "seq", None),
        P(None, "seq"),
        P("head", "seq"),
    )

    return jax.shard_map(on_device, mesh=mesh, in_specs=placed, out_specs=P("seq", "head"), check_vma=False)
```

time: 62.7 us -> 62.7 us (level)
  waiting for transfers between devices: 21.4 us -> 19.2 us
  starting transfers between devices: 26.9 us -> 28.1 us
  other arithmetic: 0.81 us -> 1.76 us
    ppermute x21 -> x22, waiting for transfers between devices: 21.4 us -> 19.2 us  [move(): return lax.ppermute(x, BOTH, pairs)]
    ppermute x21 -> x22, starting transfers between devices: 26.9 us -> 28.1 us  [move(): return lax.ppermute(x, BOTH, pairs)]
    select_n x1, other arithmetic: 0.04 us -> 0.99 us  [on_device(): held = [jnp.where(here, held[i ^ bit], held[i]) for i in range(heads)]]
  transfers between devices with their start and end apart: 21 -> 22, of which waited for: 13 -> 12; matrix products, arithmetic and copies ran while one was open for 3% -> 4% of each run, Pallas kernels for 16% -> 16%
where the time goes in v2:
time: 62.7 us; the launch traced here: 62.4 us
  starting transfers between devices  28.1 us (45%)
  waiting for transfers between devices  19.2 us (31%)
  Pallas kernels  11.2 us (18%)
  local copies, waits for them, and re-layouts  1.91 us (3%)
  other arithmetic  1.76 us (3%)
    ppermute x22, starting transfers between devices, move(): return lax.ppermute(x, BOTH, pairs)  28.1 us
    ppermute x22, waiting for transfers between devices, move(): return lax.ppermute(x, BOTH, pairs)  19.2 us
    pallas_call x4, Pallas kernels, attend(): pl.pallas_call(functools.partial(attend_kernel, own_rows, flip, members,...  9.92 us
    unnamed x9, local copies, waits for them, and re-layouts  1.9 us
  transfers between devices with their start and end apart: 22, of which 12 were waited for; matrix products, arithmetic and copies ran while one was open for 4% of the time, Pallas kernels for 16%

profile of v2, /device:TPU:0, one launch (start us, length us, event | category | flops | bytes accessed | tf_op | source)
XLA Modules:
  0.0 62.4 jit_solution(10336569533123992719)
XLA Ops:
  0.0 0.0 copy-start
  0.0 3.1 %collective-permute-start = (bf16[64,512]{1,0:T(8,128)(2,1)}, bf16[64,512]{1,0:T(8,128)(2,1)S(1)}, u32[]{:S(2)}, u32[]{:S(2)}) collective-permute-start(bf16[64,512]{1,0:T(8,128)(2,1)} %param.5), channel_id=1, source_target_pairs={{0,8},{1,9},{2,10},{3,11},{4,12},{5,13},{6,14},{7,15},{8,0},{9,1},... | collective-permute-start | bytes 196616 | tf_op jit(solution)/shard_map/ppermute | solution.py:193
  3.1 2.6 %collective-permute-start.1 = (bf16[64,512]{1,0:T(8,128)(2,1)}, bf16[64,512]{1,0:T(8,128)(2,1)S(1)}, u32[]{:S(2)}, u32[]{:S(2)}) collective-permute-start(bf16[64,512]{1,0:T(8,128)(2,1)} %param.5), channel_id=1, source_target_pairs={{0,16},{1,17},{2,18},{3,19},{4,20},{5,21},{6,22},{7,23},{8,24},{9,... | collective-permute-start | bytes 196616 | tf_op jit(solution)/shard_map/ppermute | solution.py:193
  5.6 0.0 collective-permute-start.2
  5.6 1.7 %collective-permute-start.4 = (bf16[2048,128]{1,0:T(8,128)(2,1)}, bf16[2048,128]{1,0:T(8,128)(2,1)S(1)}, u32[]{:S(2)}, u32[]{:S(2)}) collective-permute-start(bf16[2048,128]{1,0:T(8,128)(2,1)} %bitcast.2), channel_id=1, source_target_pairs={{0,2},{1,5},{2,0},{3,7},{4,6},{5,1},{6,4},{7,3},{8,10},{9,13},{10,... | collective-permute-start | bytes 1572872 | tf_op jit(solution)/shard_map/ppermute | solution.py:193
  7.4 0.3 collective-permute-start.5
  7.7 0.8 %constant_dynamic-update-slice_fusion.3 = bf16[256,512]{1,0:T(8,128)(2,1)S(1)} fusion(bf16[64,512]{1,0:T(8,128)(2,1)} %param.5), kind=kLoop, calls=%fused_computation.8 | loop fusion | bytes 131072
  8.5 0.0 collective-permute-done
  8.5 1.9 %collective-permute-start.16 = (bf16[512,256]{1,0:T(8,128)(2,1)}, bf16[512,256]{1,0:T(8,128)(2,1)}, u32[]{:S(2)}, u32[]{:S(2)}) collective-permute-start(bf16[512,256]{1,0:T(8,128)(2,1)} %param.9), channel_id=1, source_target_pairs={{0,16},{1,17},{2,18},{3,19},{4,20},{5,21},{6,22},{7,23},{8,24},{9,... | collective-permute-start | bytes 786440 | tf_op jit(solution)/shard_map/ppermute | solution.py:193
  10.4 0.1 collective-permute-done.1
  10.6 1.5 %collective-permute-done.2 = bf16[64,512]{1,0:T(8,128)(2,1)S(1)} collective-permute-done((bf16[64,512]{1,0:T(8,128)(2,1)}, bf16[64,512]{1,0:T(8,128)(2,1)S(1)}, u32[]{:S(2)}, u32[]{:S(2)}) %collective-permute-start.2) | collective-permute-done | bytes 65568 | tf_op jit(solution)/shard_map/ppermute | solution.py:193
  12.1 1.5 %collective-permute-start.6 = (bf16[256,512]{1,0:T(8,128)(2,1)S(1)}, bf16[256,512]{1,0:T(8,128)(2,1)S(1)}, u32[]{:S(2)}, u32[]{:S(2)}) collective-permute-start(bf16[256,512]{1,0:T(8,128)(2,1)S(1)} %constant_dynamic-update-slice_fusion.q_ref), channel_id=1, source_target_pairs={{0,4},{1,3},{2,6},{3,1},{4,0},{5,7},{6,2},{7,5},{8,12},{9,11},{10,... | collective-permute-start | bytes 786440 | tf_op jit(solution)/shard_map/ppermute | solution.py:193
  13.6 0.7 %compare_select_fusion.refs_0_ = f32[8,16]{1,0:T(8,128)S(1)} fusion(s32[8,16]{1,0:T(8,128)} %param.8), kind=kLoop, calls=%fused_computation.9 | loop fusion | flops 256 | bytes 1024 | tf_op jit(solution)/shard_map/jit(_where)/select_n | solution.py:212
  14.3 1.5 %collective-permute-start.3 = (f32[8,16]{1,0:T(8,128)S(1)}, f32[8,16]{1,0:T(8,128)S(1)}, u32[]{:S(2)}, u32[]{:S(2)}) collective-permute-start(f32[8,16]{1,0:T(8,128)S(1)} %compare_select_fusion.refs_0_), channel_id=1, source_target_pairs={{0,2},{1,5},{2,0},{3,7},{4,6},{5,1},{6,4},{7,3},{8,10},{9,13},{10,... | collective-permute-start | bytes 1544 | tf_op jit(solution)/shard_map/ppermute | solution.py:193
  15.8 0.0 copy-done
  15.8 0.0 copy-start.1
  15.8 1.0 %copy-done.1 = bf16[1,2048,128]{2,1,0:T(8,128)(2,1)S(1)} copy-done((bf16[1,2048,128]{2,1,0:T(8,128)(2,1)S(1)}, bf16[1,2048,128]{2,1,0:T(8,128)(2,1)}, u32[]{:S(2)}) %copy-start.1) | copy-done | bytes 524312
  16.8 0.0 copy-start.2
  16.9 0.1 stage.1
  17.0 6.3 %collective-permute-done.16 = bf16[512,256]{1,0:T(8,128)(2,1)} collective-permute-done((bf16[512,256]{1,0:T(8,128)(2,1)}, bf16[512,256]{1,0:T(8,128)(2,1)}, u32[]{:S(2)}, u32[]{:S(2)}) %collective-permute-start.16) | collective-permute-done | bytes 262176 | tf_op jit(solution)/shard_map/ppermute | solution.py:193
  23.3 0.0 copy-done.2
  23.3 1.0 %broadcast_select_fusion.1 = (bf16[512,256]{1,0:T(8,128)(2,1)S(1)}, bf16[512,256]{1,0:T(8,128)(2,1)S(1)}) fusion(bf16[512,256]{1,0:T(8,128)(2,1)} %collective-permute-done.16, bf16[512,256]{1,0:T(8,128)(2,1)S(1)} %copy-done.2, pred[]{:T(512)S(6)} %eq.5), kind=kLoop, calls=%fused_computation.3 | loop fusion | flops 262144 | bytes 1048577 | tf_op jit(solution)/shard_map/jit(_where)/select_n | solution.py:224
  24.3 0.1 collective-permute-start.17
  24.4 0.0 collective-permute-done.3.refs_0_.refs_3_
  24.4 0.0 collective-permute-done.6.q_ref
  24.4 0.0 collective-permute-done.4.refs_1_.refs_4_
  24.4 0.0 collective-permute-done.5.refs_2_.refs_5_
  24.4 2.5 %shard_map.59 = bf16[128,512]{1,0:T(8,128)(2,1)S(1)} custom-call(bf16[256,512]{1,0:T(8,128)(2,1)S(1)} %collective-permute-done.6.q_ref, f32[8,16]{1,0:T(8,128)S(1)} %compare_select_fusion.refs_0_, bf16[2048,128]{1,0:T(8,128)(2,1)S(1)} %get-tuple-element.15.refs_1_, bf16[2048,128]{1,0:T(8,128)(2,1)S(1)} %get-tuple-element.16.refs_2_, ...), custom_call_target="tpu_custom_call" | custom-call | flops 1073741824 | bytes 1048576 | tf_op jit(solution)/shard_map/pallas_call | solution.py:84
  26.9 1.6 %collective-permute-start.9 = (bf16[128,512]{1,0:T(8,128)(2,1)S(1)}, bf16[128,512]{1,0:T(8,128)(2,1)S(1)}, u32[]{:S(2)}, u32[]{:S(2)}) collective-permute-start(bf16[128,512]{1,0:T(8,128)(2,1)S(1)} %shard_map.59), channel_id=1, source_target_pairs={{0,4},{1,3},{2,6},{3,1},{4,0},{5,7},{6,2},{7,5},{8,12},{9,11},{10,... | collective-permute-start | bytes 393224 | tf_op jit(solution)/shard_map/ppermute | solution.py:193
  28.5 2.5 %shard_map.57 = bf16[128,512]{1,0:T(8,128)(2,1)S(1)} custom-call(bf16[256,512]{1,0:T(8,128)(2,1)S(1)} %collective-permute-done.6.q_ref, f32[8,16]{1,0:T(8,128)S(1)} %compare_select_fusion.refs_0_, bf16[2048,128]{1,0:T(8,128)(2,1)S(1)} %get-tuple-element.15.refs_1_, bf16[2048,128]{1,0:T(8,128)(2,1)S(1)} %get-tuple-element.16.refs_2_, ...), custom_call_target="tpu_custom_call" | custom-call | flops 1073741824 | bytes 1048576 | tf_op jit(solution)/shard_map/pallas_call | solution.py:84
  31.0 0.6 collective-permute-start.7
  31.5 2.5 %shard_map.55.refs_3_ = f32[256,512]{1,0:T(8,128)S(1)} custom-call(bf16[256,512]{1,0:T(8,128)(2,1)S(1)} %constant_dynamic-update-slice_fusion.q_ref, f32[8,16]{1,0:T(8,128)S(1)} %compare_select_fusion.refs_0_, bf16[2048,128]{1,0:T(8,128)(2,1)S(1)} %get-tuple-element.15.refs_1_, bf16[2048,128]{1,0:T(8,128)(2,1)S(1)} %get-tuple-element.16.refs_2_), custom_call_target="tpu_custom_call" | custom-call | flops 1073741824 | bytes 1048576 | tf_op jit(solution)/shard_map/pallas_call | solution.py:84
  34.0 2.5 %shard_map.56.part_ref = f32[256,512]{1,0:T(8,128)S(1)} custom-call(bf16[256,512]{1,0:T(8,128)(2,1)S(1)} %constant_dynamic-update-slice_fusion.q_ref, f32[8,16]{1,0:T(8,128)S(1)} %collective-permute-done.3.refs_0_.refs_3_, bf16[2048,128]{1,0:T(8,128)(2,1)S(1)} %collective-permute-done.4.refs_1_.refs_4_, ...), custom_call_target="tpu_custom_call" | custom-call | flops 1073741824 | bytes 1048576 | tf_op jit(solution)/shard_map/pallas_call | solution.py:84
  36.5 0.0 collective-permute-done.9.share_ref
  36.5 3.0 %collective-permute-start.11 = (bf16[64,512]{1,0:T(8,128)(2,1)S(1)}, bf16[64,512]{1,0:T(8,128)(2,1)S(1)}, u32[]{:S(2)}, u32[]{:S(2)}) collective-permute-start(bf16[64,512]{1,0:T(8,128)(2,1)S(1)} %get-tuple-element.20), channel_id=1, source_target_pairs={{0,24},{1,25},{2,26},{3,27},{4,28},{5,29},{6,30},{7,31},{8,16},{9,... | collective-permute-start | bytes 196616 | tf_op jit(solution)/shard_map/ppermute | solution.py:193
  39.5 0.0 collective-permute-start.10
  39.6 0.0 collective-permute-done.7.share_ref
  39.6 1.5 %collective-permute-start.8 = (bf16[64,512]{1,0:T(8,128)(2,1)S(1)}, bf16[64,512]{1,0:T(8,128)(2,1)S(1)}, u32[]{:S(2)}, u32[]{:S(2)}) collective-permute-start(bf16[64,512]{1,0:T(8,128)(2,1)S(1)} %get-tuple-element.18), channel_id=1, source_target_pairs={{0,8},{1,9},{2,10},{3,11},{4,12},{5,13},{6,14},{7,15},{8,0},{9,1},... | collective-permute-start | bytes 196616 | tf_op jit(solution)/shard_map/ppermute | solution.py:193
  41.1 0.0 collective-permute-done.17
  41.1 1.6 %collective-permute-start.18 = (bf16[1024,256]{1,0:T(8,128)(2,1)S(1)}, bf16[1024,256]{1,0:T(8,128)(2,1)S(1)}, u32[]{:S(2)}, u32[]{:S(2)}) collective-permute-start(bf16[1024,256]{1,0:T(8,128)(2,1)S(1)} %pad_maximum_fusion.refs_2_), channel_id=1, source_target_pairs={{0,4},{1,5},{2,6},{3,7},{4,0},{5,1},{6,2},{7,3},{8,12},{9,13},{10,... | collective-permute-start | bytes 1572872 | tf_op jit(solution)/shard_map/ppermute | solution.py:193
  42.7 0.5 collective-permute-done.11
  43.2 2.2 %collective-permute-done.10 = bf16[64,512]{1,0:T(8,128)(2,1)S(1)} collective-permute-done((bf16[64,512]{1,0:T(8,128)(2,1)S(1)}, bf16[64,512]{1,0:T(8,128)(2,1)S(1)}, u32[]{:S(2)}, u32[]{:S(2)}) %collective-permute-start.10) | collective-permute-done | bytes 65568 | tf_op jit(solution)/shard_map/ppermute | solution.py:193
  45.5 0.0 collective-permute-done.8
  45.5 1.4 %collective-permute-start.14 = (bf16[64,512]{1,0:T(8,128)(2,1)S(1)}, bf16[64,512]{1,0:T(8,128)(2,1)S(1)}, u32[]{:S(2)}, u32[]{:S(2)}) collective-permute-start(bf16[64,512]{1,0:T(8,128)(2,1)S(1)} %add_convert_fusion), channel_id=1, source_target_pairs={{0,10},{1,11},{2,8},{3,9},{4,14},{5,15},{6,12},{7,13},{8,2},{9,3},... | collective-permute-start | bytes 196616 | tf_op jit(solution)/shard_map/ppermute | solution.py:193
  46.9 1.4 %collective-permute-start.13 = (bf16[64,512]{1,0:T(8,128)(2,1)S(1)}, bf16[64,512]{1,0:T(8,128)(2,1)S(1)}, u32[]{:S(2)}, u32[]{:S(2)}) collective-permute-start(bf16[64,512]{1,0:T(8,128)(2,1)S(1)} %add_convert_fusion), channel_id=1, source_target_pairs={{0,8},{1,9},{2,10},{3,11},{4,12},{5,13},{6,14},{7,15},{8,0},{9,1},... | collective-permute-start | bytes 196616 | tf_op jit(solution)/shard_map/ppermute | solution.py:193
  48.3 0.8 %collective-permute-start.12 = (bf16[64,512]{1,0:T(8,128)(2,1)S(1)}, bf16[64,512]{1,0:T(8,128)(2,1)S(1)}, u32[]{:S(2)}, u32[]{:S(2)}) collective-permute-start(bf16[64,512]{1,0:T(8,128)(2,1)S(1)} %add_convert_fusion), channel_id=1, source_target_pairs={{0,2},{1,3},{2,0},{3,1},{4,6},{5,7},{6,4},{7,5},{8,10},{9,11},{10,... | collective-permute-start | bytes 196616 | tf_op jit(solution)/shard_map/ppermute | solution.py:193
  49.1 2.0 %collective-permute-done.14 = bf16[64,512]{1,0:T(8,128)(2,1)S(1)} collective-permute-done((bf16[64,512]{1,0:T(8,128)(2,1)S(1)}, bf16[64,512]{1,0:T(8,128)(2,1)S(1)}, u32[]{:S(2)}, u32[]{:S(2)}) %collective-permute-start.14) | collective-permute-done | bytes 65568 | tf_op jit(solution)/shard_map/ppermute | solution.py:193
  51.1 0.3 collective-permute-done.13
  51.4 1.1 %collective-permute-done.12 = bf16[64,512]{1,0:T(8,128)(2,1)S(1)} collective-permute-done((bf16[64,512]{1,0:T(8,128)(2,1)S(1)}, bf16[64,512]{1,0:T(8,128)(2,1)S(1)}, u32[]{:S(2)}, u32[]{:S(2)}) %collective-permute-start.12) | collective-permute-done | bytes 65568 | tf_op jit(solution)/shard_map/ppermute | solution.py:193
  52.6 0.1 collective-permute-start.15
  52.6 1.5 %collective-permute-done.15.refs_1_ = bf16[256,512]{1,0:T(8,128)(2,1)S(1)} collective-permute-done((bf16[256,512]{1,0:T(8,128)(2,1)S(1)}, bf16[256,512]{1,0:T(8,128)(2,1)S(1)}, u32[]{:S(2)}, u32[]{:S(2)}) %collective-permute-start.15) | collective-permute-done | bytes 262176 | tf_op jit(solution)/shard_map/ppermute | solution.py:193
  54.2 0.0 collective-permute-done.18.refs_3_
  54.2 0.4 shard_map.61
  54.6 1.5 %collective-permute-start.19 = (bf16[64,512]{1,0:T(8,128)(2,1)S(1)}, bf16[64,512]{1,0:T(8,128)(2,1)S(1)}, u32[]{:S(2)}, u32[]{:S(2)}) collective-permute-start(bf16[64,512]{1,0:T(8,128)(2,1)S(1)} %get-tuple-element.22), channel_id=1, source_target_pairs={{0,2},{1,3},{2,0},{3,1},{4,6},{5,7},{6,4},{7,5},{8,10},{9,11},{10,... | collective-permute-start | bytes 196616 | tf_op jit(solution)/shard_map/ppermute | solution.py:193
  56.1 0.4 collective-permute-start.20
  56.5 1.7 %collective-permute-start.21 = (bf16[64,512]{1,0:T(8,128)(2,1)S(1)}, bf16[64,512]{1,0:T(8,128)(2,1)S(1)}, u32[]{:S(2)}, u32[]{:S(2)}) collective-permute-start(bf16[64,512]{1,0:T(8,128)(2,1)S(1)} %get-tuple-element.24), channel_id=1, source_target_pairs={{0,10},{1,11},{2,8},{3,9},{4,14},{5,15},{6,12},{7,13},{8,2},{9,3},... | collective-permute-start | bytes 196616 | tf_op jit(solution)/shard_map/ppermute | solution.py:193
  58.2 0.8 %collective-permute-done.19.refs_1_ = bf16[64,512]{1,0:T(8,128)(2,1)S(1)} collective-permute-done((bf16[64,512]{1,0:T(8,128)(2,1)S(1)}, bf16[64,512]{1,0:T(8,128)(2,1)S(1)}, u32[]{:S(2)}, u32[]{:S(2)}) %collective-permute-start.19) | collective-permute-done | bytes 65568 | tf_op jit(solution)/shard_map/ppermute | solution.py:193
  58.9 1.4 %collective-permute-done.20.refs_2_ = bf16[64,512]{1,0:T(8,128)(2,1)S(1)} collective-permute-done((bf16[64,512]{1,0:T(8,128)(2,1)S(1)}, bf16[64,512]{1,0:T(8,128)(2,1)S(1)}, u32[]{:S(2)}, u32[]{:S(2)}) %collective-permute-start.20) | collective-permute-done | bytes 65568 | tf_op jit(solution)/shard_map/ppermute | solution.py:193
  60.4 1.3 %collective-permute-done.21.refs_3_ = bf16[64,512]{1,0:T(8,128)(2,1)S(1)} collective-permute-done((bf16[64,512]{1,0:T(8,128)(2,1)S(1)}, bf16[64,512]{1,0:T(8,128)(2,1)S(1)}, u32[]{:S(2)}, u32[]{:S(2)}) %collective-permute-start.21) | collective-permute-done | bytes 65568 | tf_op jit(solution)/shard_map/ppermute | solution.py:193
  61.7 0.7 %shard_map.62 = bf16[64,2048]{1,0:T(8,128)(2,1)} custom-call(bf16[64,512]{1,0:T(8,128)(2,1)S(1)} %get-tuple-element.21.refs_0_, bf16[64,512]{1,0:T(8,128)(2,1)S(1)} %collective-permute-done.19.refs_1_, bf16[64,512]{1,0:T(8,128)(2,1)S(1)} %collective-permute-done.20.refs_2_, bf16[64,512]{1,0:T(8,128)(2,1)S(1)} %collective-permute-done.21.refs_3_), custom_call_target="tpu_custom_call" | custom-call | bytes 1048576 | tf_op jit(solution)/shard_map/pallas_call | solution.py:99
  (8 shorter events, 0.2 us)
Async XLA Ops:
  0.0 15.8 %copy-start = (bf16[1,2048,128]{2,1,0:T(8,128)(2,1)S(1)}, bf16[1,2048,128]{2,1,0:T(8,128)(2,1)}, u32[]{:S(2)}) copy-start(bf16[1,2048,128]{2,1,0:T(8,128)(2,1)} %param.6) | copy-start | bytes 1572868
  0.0 8.5 %collective-permute-start = (bf16[64,512]{1,0:T(8,128)(2,1)}, bf16[64,512]{1,0:T(8,128)(2,1)S(1)}, u32[]{:S(2)}, u32[]{:S(2)}) collective-permute-start(bf16[64,512]{1,0:T(8,128)(2,1)} %param.5), channel_id=1, source_target_pairs={{0,8},{1,9},{2,10},{3,11},{4,12},{5,13},{6,14},{7,15},{8,0},{9,1},... | collective-permute-start | bytes 196616 | tf_op jit(solution)/shard_map/ppermute | solution.py:193
  3.1 7.5 %collective-permute-start.1 = (bf16[64,512]{1,0:T(8,128)(2,1)}, bf16[64,512]{1,0:T(8,128)(2,1)S(1)}, u32[]{:S(2)}, u32[]{:S(2)}) collective-permute-start(bf16[64,512]{1,0:T(8,128)(2,1)} %param.5), channel_id=1, source_target_pairs={{0,16},{1,17},{2,18},{3,19},{4,20},{5,21},{6,22},{7,23},{8,24},{9,... | collective-permute-start | bytes 196616 | tf_op jit(solution)/shard_map/ppermute | solution.py:193
  5.6 6.5 %collective-permute-start.2 = (bf16[64,512]{1,0:T(8,128)(2,1)}, bf16[64,512]{1,0:T(8,128)(2,1)S(1)}, u32[]{:S(2)}, u32[]{:S(2)}) collective-permute-start(bf16[64,512]{1,0:T(8,128)(2,1)} %param.5), channel_id=1, source_target_pairs={{0,24},{1,25},{2,26},{3,27},{4,28},{5,29},{6,30},{7,31},{8,16},{9,... | collective-permute-start | bytes 196616 | tf_op jit(solution)/shard_map/ppermute | solution.py:193
  5.6 18.7 %collective-permute-start.4 = (bf16[2048,128]{1,0:T(8,128)(2,1)}, bf16[2048,128]{1,0:T(8,128)(2,1)S(1)}, u32[]{:S(2)}, u32[]{:S(2)}) collective-permute-start(bf16[2048,128]{1,0:T(8,128)(2,1)} %bitcast.2), channel_id=1, source_target_pairs={{0,2},{1,5},{2,0},{3,7},{4,6},{5,1},{6,4},{7,3},{8,10},{9,13},{10,... | collective-permute-start | bytes 1572872 | tf_op jit(solution)/shard_map/ppermute | solution.py:193
  7.4 17.0 %collective-permute-start.5 = (bf16[2048,128]{1,0:T(8,128)(2,1)}, bf16[2048,128]{1,0:T(8,128)(2,1)S(1)}, u32[]{:S(2)}, u32[]{:S(2)}) collective-permute-start(bf16[2048,128]{1,0:T(8,128)(2,1)} %bitcast.4), channel_id=1, source_target_pairs={{0,2},{1,5},{2,0},{3,7},{4,6},{5,1},{6,4},{7,3},{8,10},{9,13},{10,... | collective-permute-start | bytes 1572872 | tf_op jit(solution)/shard_map/ppermute | solution.py:193
  8.5 14.8 %collective-permute-start.16 = (bf16[512,256]{1,0:T(8,128)(2,1)}, bf16[512,256]{1,0:T(8,128)(2,1)}, u32[]{:S(2)}, u32[]{:S(2)}) collective-permute-start(bf16[512,256]{1,0:T(8,128)(2,1)} %param.9), channel_id=1, source_target_pairs={{0,16},{1,17},{2,18},{3,19},{4,20},{5,21},{6,22},{7,23},{8,24},{9,... | collective-permute-start | bytes 786440 | tf_op jit(solution)/shard_map/ppermute | solution.py:193
  12.1 12.3 %collective-permute-start.6 = (bf16[256,512]{1,0:T(8,128)(2,1)S(1)}, bf16[256,512]{1,0:T(8,128)(2,1)S(1)}, u32[]{:S(2)}, u32[]{:S(2)}) collective-permute-start(bf16[256,512]{1,0:T(8,128)(2,1)S(1)} %constant_dynamic-update-slice_fusion.q_ref), channel_id=1, source_target_pairs={{0,4},{1,3},{2,6},{3,1},{4,0},{5,7},{6,2},{7,5},{8,12},{9,11},{10,... | collective-permute-start | bytes 786440 | tf_op jit(solution)/shard_map/ppermute | solution.py:193
  14.3 10.1 %collective-permute-start.3 = (f32[8,16]{1,0:T(8,128)S(1)}, f32[8,16]{1,0:T(8,128)S(1)}, u32[]{:S(2)}, u32[]{:S(2)}) collective-permute-start(f32[8,16]{1,0:T(8,128)S(1)} %compare_select_fusion.refs_0_), channel_id=1, source_target_pairs={{0,2},{1,5},{2,0},{3,7},{4,6},{5,1},{6,4},{7,3},{8,10},{9,13},{10,... | collective-permute-start | bytes 1544 | tf_op jit(solution)/shard_map/ppermute | solution.py:193
  15.8 1.0 %copy-start.1 = (bf16[1,2048,128]{2,1,0:T(8,128)(2,1)S(1)}, bf16[1,2048,128]{2,1,0:T(8,128)(2,1)}, u32[]{:S(2)}) copy-start(bf16[1,2048,128]{2,1,0:T(8,128)(2,1)} %param.7) | copy-start | bytes 1572868
  16.8 6.4 %copy-start.2 = (bf16[512,256]{1,0:T(8,128)(2,1)S(1)}, bf16[512,256]{1,0:T(8,128)(2,1)}, u32[]{:S(2)}) copy-start(bf16[512,256]{1,0:T(8,128)(2,1)} %param.9) | copy-start | bytes 786436
  24.3 16.8 %collective-permute-start.17 = (bf16[512,256]{1,0:T(8,128)(2,1)S(1)}, bf16[512,256]{1,0:T(8,128)(2,1)S(1)}, u32[]{:S(2)}, u32[]{:S(2)}) collective-permute-start(bf16[512,256]{1,0:T(8,128)(2,1)S(1)} %get-tuple-element.26), channel_id=1, source_target_pairs={{0,1},{1,0},{2,3},{3,2},{4,5},{5,4},{6,7},{7,6},{8,9},{9,8},{10,11... | collective-permute-start | bytes 786440 | tf_op jit(solution)/shard_map/ppermute | solution.py:193
  26.9 9.6 %collective-permute-start.9 = (bf16[128,512]{1,0:T(8,128)(2,1)S(1)}, bf16[128,512]{1,0:T(8,128)(2,1)S(1)}, u32[]{:S(2)}, u32[]{:S(2)}) collective-permute-start(bf16[128,512]{1,0:T(8,128)(2,1)S(1)} %shard_map.59), channel_id=1, source_target_pairs={{0,4},{1,3},{2,6},{3,1},{4,0},{5,7},{6,2},{7,5},{8,12},{9,11},{10,... | collective-permute-start | bytes 393224 | tf_op jit(solution)/shard_map/ppermute | solution.py:193
  31.0 8.6 %collective-permute-start.7 = (bf16[128,512]{1,0:T(8,128)(2,1)S(1)}, bf16[128,512]{1,0:T(8,128)(2,1)S(1)}, u32[]{:S(2)}, u32[]{:S(2)}) collective-permute-start(bf16[128,512]{1,0:T(8,128)(2,1)S(1)} %shard_map.57), channel_id=1, source_target_pairs={{0,4},{1,3},{2,6},{3,1},{4,0},{5,7},{6,2},{7,5},{8,12},{9,11},{10,... | collective-permute-start | bytes 393224 | tf_op jit(solution)/shard_map/ppermute | solution.py:193
  36.5 6.7 %collective-permute-start.11 = (bf16[64,512]{1,0:T(8,128)(2,1)S(1)}, bf16[64,512]{1,0:T(8,128)(2,1)S(1)}, u32[]{:S(2)}, u32[]{:S(2)}) collective-permute-start(bf16[64,512]{1,0:T(8,128)(2,1)S(1)} %get-tuple-element.20), channel_id=1, source_target_pairs={{0,24},{1,25},{2,26},{3,27},{4,28},{5,29},{6,30},{7,31},{8,16},{9,... | collective-permute-start | bytes 196616 | tf_op jit(solution)/shard_map/ppermute | solution.py:193
  39.5 5.9 %collective-permute-start.10 = (bf16[64,512]{1,0:T(8,128)(2,1)S(1)}, bf16[64,512]{1,0:T(8,128)(2,1)S(1)}, u32[]{:S(2)}, u32[]{:S(2)}) collective-permute-start(bf16[64,512]{1,0:T(8,128)(2,1)S(1)} %get-tuple-element.19), channel_id=1, source_target_pairs={{0,16},{1,17},{2,18},{3,19},{4,20},{5,21},{6,22},{7,23},{8,24},{9,... | collective-permute-start | bytes 196616 | tf_op jit(solution)/shard_map/ppermute | solution.py:193
  39.6 5.9 %collective-permute-start.8 = (bf16[64,512]{1,0:T(8,128)(2,1)S(1)}, bf16[64,512]{1,0:T(8,128)(2,1)S(1)}, u32[]{:S(2)}, u32[]{:S(2)}) collective-permute-start(bf16[64,512]{1,0:T(8,128)(2,1)S(1)} %get-tuple-element.18), channel_id=1, source_target_pairs={{0,8},{1,9},{2,10},{3,11},{4,12},{5,13},{6,14},{7,15},{8,0},{9,1},... | collective-permute-start | bytes 196616 | tf_op jit(solution)/shard_map/ppermute | solution.py:193
  41.1 13.0 %collective-permute-start.18 = (bf16[1024,256]{1,0:T(8,128)(2,1)S(1)}, bf16[1024,256]{1,0:T(8,128)(2,1)S(1)}, u32[]{:S(2)}, u32[]{:S(2)}) collective-permute-start(bf16[1024,256]{1,0:T(8,128)(2,1)S(1)} %pad_maximum_fusion.refs_2_), channel_id=1, source_target_pairs={{0,4},{1,5},{2,6},{3,7},{4,0},{5,1},{6,2},{7,3},{8,12},{9,13},{10,... | collective-permute-start | bytes 1572872 | tf_op jit(solution)/shard_map/ppermute | solution.py:193
  45.5 5.5 %collective-permute-start.14 = (bf16[64,512]{1,0:T(8,128)(2,1)S(1)}, bf16[64,512]{1,0:T(8,128)(2,1)S(1)}, u32[]{:S(2)}, u32[]{:S(2)}) collective-permute-start(bf16[64,512]{1,0:T(8,128)(2,1)S(1)} %add_convert_fusion), channel_id=1, source_target_pairs={{0,10},{1,11},{2,8},{3,9},{4,14},{5,15},{6,12},{7,13},{8,2},{9,3},... | collective-permute-start | bytes 196616 | tf_op jit(solution)/shard_map/ppermute | solution.py:193
  46.9 4.5 %collective-permute-start.13 = (bf16[64,512]{1,0:T(8,128)(2,1)S(1)}, bf16[64,512]{1,0:T(8,128)(2,1)S(1)}, u32[]{:S(2)}, u32[]{:S(2)}) collective-permute-start(bf16[64,512]{1,0:T(8,128)(2,1)S(1)} %add_convert_fusion), channel_id=1, source_target_pairs={{0,8},{1,9},{2,10},{3,11},{4,12},{5,13},{6,14},{7,15},{8,0},{9,1},... | collective-permute-start | bytes 196616 | tf_op jit(solution)/shard_map/ppermute | solution.py:193
  48.3 4.3 %collective-permute-start.12 = (bf16[64,512]{1,0:T(8,128)(2,1)S(1)}, bf16[64,512]{1,0:T(8,128)(2,1)S(1)}, u32[]{:S(2)}, u32[]{:S(2)}) collective-permute-start(bf16[64,512]{1,0:T(8,128)(2,1)S(1)} %add_convert_fusion), channel_id=1, source_target_pairs={{0,2},{1,3},{2,0},{3,1},{4,6},{5,7},{6,4},{7,5},{8,10},{9,11},{10,... | collective-permute-start | bytes 196616 | tf_op jit(solution)/shard_map/ppermute | solution.py:193
  52.6 1.6 %collective-permute-start.15 = (bf16[256,512]{1,0:T(8,128)(2,1)S(1)}, bf16[256,512]{1,0:T(8,128)(2,1)S(1)}, u32[]{:S(2)}, u32[]{:S(2)}) collective-permute-start(bf16[256,512]{1,0:T(8,128)(2,1)S(1)} %pad_maximum_fusion.1.refs_0_), channel_id=1, source_target_pairs={{0,1},{1,0},{2,3},{3,2},{4,5},{5,4},{6,7},{7,6},{8,9},{9,8},{10,11... | collective-permute-start | bytes 786440 | tf_op jit(solution)/shard_map/ppermute | solution.py:193
  54.6 4.3 %collective-permute-start.19 = (bf16[64,512]{1,0:T(8,128)(2,1)S(1)}, bf16[64,512]{1,0:T(8,128)(2,1)S(1)}, u32[]{:S(2)}, u32[]{:S(2)}) collective-permute-start(bf16[64,512]{1,0:T(8,128)(2,1)S(1)} %get-tuple-element.22), channel_id=1, source_target_pairs={{0,2},{1,3},{2,0},{3,1},{4,6},{5,7},{6,4},{7,5},{8,10},{9,11},{10,... | collective-permute-start | bytes 196616 | tf_op jit(solution)/shard_map/ppermute | solution.py:193
  56.1 4.3 %collective-permute-start.20 = (bf16[64,512]{1,0:T(8,128)(2,1)S(1)}, bf16[64,512]{1,0:T(8,128)(2,1)S(1)}, u32[]{:S(2)}, u32[]{:S(2)}) collective-permute-start(bf16[64,512]{1,0:T(8,128)(2,1)S(1)} %get-tuple-element.23), channel_id=1, source_target_pairs={{0,8},{1,9},{2,10},{3,11},{4,12},{5,13},{6,14},{7,15},{8,0},{9,1},... | collective-permute-start | bytes 196616 | tf_op jit(solution)/shard_map/ppermute | solution.py:193
  56.5 5.2 %collective-permute-start.21 = (bf16[64,512]{1,0:T(8,128)(2,1)S(1)}, bf16[64,512]{1,0:T(8,128)(2,1)S(1)}, u32[]{:S(2)}, u32[]{:S(2)}) collective-permute-start(bf16[64,512]{1,0:T(8,128)(2,1)S(1)} %get-tuple-element.24), channel_id=1, source_target_pairs={{0,10},{1,11},{2,8},{3,9},{4,14},{5,15},{6,12},{7,13},{8,2},{9,3},... | collective-permute-start | bytes 196616 | tf_op jit(solution)/shard_map/ppermute | solution.py:193

commit v3 on v2

--- a/solution.py
+++ b/solution.py
@@ -16,7 +16,7 @@
 BOTH = ("seq", "head")
 
 
-def attend_kernel(own_rows, flip, members, sources, has_acc, q_ref, *refs):
+def attend_kernel(offset, own_rows, flip, members, sources, has_acc, q_ref, *refs):
     given, refs = refs[: 3 * sources], refs[3 * sources :]
     if has_acc:
         acc_in, refs = refs[0], refs[1:]
@@ -38,11 +38,12 @@
                 member * own_rows : (member + 1) * own_rows, i * head_size : (i + 1) * head_size
             ]
     for n in range(sources):
-        bias_ref, k_ref, v_ref = given[3 * n : 3 * n + 3]
+        mask_ref, k_ref, v_ref = given[3 * n : 3 * n + 3]
         biases = []
         for member in members:
             mask_row = ((line ^ member) * 4 + plane) * own_rows // BLK
-            biases.append(bias_ref[pl.ds(mask_row, 1), :])
+            live = mask_ref[pl.ds(mask_row, 1), :] > 0
+            biases.append(jnp.where(live, offset, 1e30).astype(jnp.float32))
         for t in range(cached // tile):
             score = lax.dot_general(
                 stacked[...],
@@ -69,11 +70,11 @@
             here = (slice(j * own_rows, (j + 1) * own_rows), slice(i * head_size, (i + 1) * head_size))
             value = total[j * part + i * own_rows : j * part + (i + 1) * own_rows, :]
             if has_acc:
-                value = value + acc_in[here]
+                value = value + acc_in[members[j] * own_rows : (members[j] + 1) * own_rows, here[1]]
             out_ref[here] = value.astype(out_ref.dtype)
 
 
-def attend(q, sources, own_rows, flip, members, acc, dtype):
+def attend(q, sources, offset, own_rows, flip, members, acc, dtype):
     width = q.shape[1]
     cached, head_size = sources[0][1].shape
     rows = len(members) * own_rows
@@ -82,7 +83,7 @@
     vmem = pl.BlockSpec(memory_space=pltpu.VMEM)
     args = [q] + [x for source in sources for x in source] + ([] if acc is None else [acc])
     return pl.pallas_call(
-        functools.partial(attend_kernel, own_rows, flip, members, len(sources), acc is not None),
+        functools.partial(attend_kernel, offset, own_rows, flip, members, len(sources), acc is not None),
         out_shape=jax.ShapeDtypeStruct((rows, width), dtype),
         in_specs=[vmem] * len(args),
         out_specs=vmem,
@@ -106,41 +107,15 @@
     )(*args)
 
 
-def stage_kernel(key_far, value_far, key_here, value_here, sems):
-    copies = [
-        pltpu.make_async_copy(far, here, sems.at[i])
-        for i, (far, here) in enumerate(((key_far, key_here), (value_far, value_here)))
-    ]
-    for copy in copies:
-        copy.start()
-    for copy in copies:
-        copy.wait()
-
-
-def stage(keys, values):
-    vmem = pl.BlockSpec(memory_space=pltpu.VMEM)
-    return pl.pallas_call(
-        stage_kernel,
-        name="stage",
-        out_shape=[jax.ShapeDtypeStruct(x.shape, x.dtype) for x in (keys, values)],
-        in_specs=[pl.BlockSpec(memory_space=pl.ANY)] * 2,
-        out_specs=[vmem] * 2,
-        scratch_shapes=[pltpu.SemaphoreType.DMA((2,))],
-        compiler_params=pltpu.CompilerParams(vmem_limit_bytes=VMEM_LIMIT),
-        cost_estimate=pl.CostEstimate(flops=0, transcendentals=0, bytes_accessed=4 * keys.size),
-    )(keys, values)
-
-
-def merge_kernel(members, part_ref, share_ref, *out_refs):
+def merge_kernel(part_ref, share_ref, *out_refs):
     own_rows = out_refs[0].shape[0]
-    for j, member in enumerate(members):
-        value = part_ref[member * own_rows : (member + 1) * own_rows, :]
-        value = value + share_ref[j * own_rows : (j + 1) * own_rows, :].astype(jnp.float32)
-        out_refs[j][...] = value.astype(out_refs[j].dtype)
+    for j, out_ref in enumerate(out_refs):
+        rows = slice(j * own_rows, (j + 1) * own_rows)
+        out_ref[...] = (part_ref[rows, :] + share_ref[rows, :].astype(jnp.float32)).astype(out_ref.dtype)
 
 
 def project_kernel(heads, *refs):
-    inputs, refs = refs[:heads], refs[heads:]
+    inputs, refs = refs[: 2 * heads], refs[2 * heads :]
     blocks, outs = refs[:-4], refs[-4:]
     own_rows = outs[0].shape[0]
     width = inputs[0].shape[1]
@@ -148,13 +123,12 @@
     for m, block in enumerate(blocks):
         value = None
         for k in range(heads):
-            term = jnp.dot(
-                inputs[k][...], block[k * width : (k + 1) * width, :], preferred_element_type=jnp.float32
-            )
+            rows = jnp.concatenate([inputs[2 * k][...], inputs[2 * k + 1][...]], axis=0)
+            term = jnp.dot(rows, block[k * width : (k + 1) * width, :], preferred_element_type=jnp.float32)
             value = term if value is None else value + term
         value = value.astype(jnp.bfloat16)
-        for k in range(4):
-            outs[k][:, m * columns : (m + 1) * columns] = value[k * own_rows : (k + 1) * own_rows]
+        for i, k in enumerate((0, 2, 3, 1)):
+            outs[k][:, m * columns : (m + 1) * columns] = value[i * own_rows : (i + 1) * own_rows]
 
 
 def place_kernel(*refs):
@@ -209,8 +183,8 @@
 
     key_own, value_own = keys[0], values[0]
     lined = [queries] + [along(queries, k) for k in range(1, lines)]
-    bias = jnp.where(mask > 0, jnp.float32(math.log(total_keys) * LOG2E), jnp.float32(1e30))
-    bias_pair, key_pair, value_pair = pair(bias), pair(key_own), pair(value_own)
+    offset = math.log(total_keys) * LOG2E
+    mask_pair, key_pair, value_pair = pair(mask), pair(key_own), pair(value_own)
     q_own = jnp.concatenate(lined, axis=0)
     q_other = other(q_own)
 
@@ -226,38 +200,45 @@
     rows_all = jnp.concatenate([held[0]] + [across(held[k], k) for k in range(1, heads)], axis=0)
     proj = [rows_all, move(rows_all, lambda z, p, h: (z, p ^ 2, h))]
 
-    near, far = (bias, *stage(key_own, value_own)), (bias_pair, key_pair, value_pair)
+    near, far = (mask, key_own, value_own), (mask_pair, key_pair, value_pair)
 
     def attention(q, sources, flip, members, acc=None, dtype=jnp.float32):
-        return attend(q, sources, own_rows, flip, members, acc, dtype)
-
-    every, upper, lower = range(lines), range(lines // 2, lines), range(lines // 2)
+        return attend(q, sources, offset, own_rows, flip, members, acc, dtype)
+
+    every, upper, lower = range(lines), range(2, lines), range(2)
     part = attention(q_own, [near], (0, 0), every)
     share_upper = attention(q_other, [near, far], (2, 1), upper, dtype=jnp.bfloat16)
     share_upper = other(share_upper)
+    part_upper = attention(q_own, [far], (0, 0), upper, part)
     share_lower = attention(q_other, [near, far], (2, 1), lower, dtype=jnp.bfloat16)
     share_lower = other(share_lower)
-    part = attention(q_own, [far], (0, 0), every, part)
+    part_lower = attention(q_own, [far], (0, 0), lower, part)
     width = part.shape[1]
 
-    def merge(share, members):
-        shapes = [jax.ShapeDtypeStruct((own_rows, width), jnp.bfloat16 if m else jnp.float32) for m in members]
-        return small_call(functools.partial(merge_kernel, members), shapes, [part, share])
-
-    merged = merge(share_upper, upper)
-    merged = merge(share_lower, lower) + merged
-    sums = merged[0]
-    for k in range(1, lines):
-        sums = sums + along(merged[k], k).astype(jnp.float32)
+    def merge(own, share, members):
+        shapes = [jax.ShapeDtypeStruct((own_rows, width), jnp.bfloat16 if m % 2 else jnp.float32) for m in members]
+        return small_call(merge_kernel, shapes, [own, share])
+
+    merged = merge(part_upper, share_upper, upper)
+    passed = along(jnp.concatenate(merged[1::2], axis=0), 1)
+    sends = [
+        (block + passed[i * own_rows : (i + 1) * own_rows].astype(jnp.float32)).astype(jnp.bfloat16)
+        for i, block in enumerate(merged[::2])
+    ]
+    sums, near_block = merge(part_lower, share_lower, lower)
+    for i, block in enumerate(sends):
+        sums = sums + along(block, 2 * i + 2).astype(jnp.float32)
+    sums = sums + along(near_block, 1).astype(jnp.float32)
     attended = sums.astype(jnp.bfloat16)
 
-    quad = jnp.concatenate([attended] + [inside(attended, k) for k in range(1, 4)], axis=0)
-    full = [quad] + [across(quad, k) for k in range(1, heads)]
+    gathered = [inside(attended, k) for k in range(1, 4)]
+    groups = [jnp.concatenate([attended, gathered[1], gathered[2]], axis=0), gathered[0]]
+    full = [groups] + [[across(g, k) for g in groups] for k in range(1, heads)]
     piece = jax.ShapeDtypeStruct((own_rows, per_head * columns), jnp.bfloat16)
     result = small_call(
         functools.partial(project_kernel, heads),
         [piece] * 4,
-        full + proj,
+        [g for groups in full for g in groups] + proj,
         flops=8 * own_rows * heads * width * per_head * columns,
     )
     got = [result[0]] + [inside(result[k], k) for k in range(1, 4)]

time: 62.7 us -> 63.4 us (1.011)
  waiting for transfers between devices: 19.2 us -> 21.3 us
  other arithmetic: 1.76 us -> 0.13 us
  local copies, waits for them, and re-layouts: 1.91 us -> 2.59 us
    ppermute x22 -> x23, waiting for transfers between devices: 19.2 us -> 21.3 us  [move(): return lax.ppermute(x, BOTH, pairs)]
    select_n x1, other arithmetic: 0.99 us -> 0.04 us  [on_device(): held = [jnp.where(here, held[i ^ bit], held[i]) for i in range(heads)]]
    select_n x1 -> x0, other arithmetic: 0.69 us -> none  [on_device(): jnp.where(mask > 0, jnp.float32(math.log(total_keys) * LOG2E), jnp.float3...]
    unnamed x9 -> x11, local copies, waits for them, and re-layouts: 1.9 us -> 2.59 us
    ppermute x22 -> x23, starting transfers between devices: 28.1 us -> 27.6 us  [move(): return lax.ppermute(x, BOTH, pairs)]
  transfers between devices with their start and end apart: 22 -> 23, of which waited for: 12 -> 13; matrix products, arithmetic and copies ran while one was open for 4% -> 2% of each run, Pallas kernels for 16% -> 16%
where the time goes in v3:
time: 63.4 us; the launch traced here: 63.2 us
  starting transfers between devices  27.6 us (44%)
  waiting for transfers between devices  21.3 us (34%)
  Pallas kernels  11.4 us (18%)
  local copies, waits for them, and re-layouts  2.59 us (4%)
    ppermute x23, starting transfers between devices, move(): return lax.ppermute(x, BOTH, pairs)  27.6 us
    ppermute x23, waiting for transfers between devices, move(): return lax.ppermute(x, BOTH, pairs)  21.3 us
    pallas_call x5, Pallas kernels, attend(): pl.pallas_call(functools.partial(attend_kernel, offset, own_rows, flip, m...  10.2 us
    unnamed x11, local copies, waits for them, and re-layouts  2.59 us
  transfers between devices with their start and end apart: 23, of which 13 were waited for; matrix products, arithmetic and copies ran while one was open for 2% of the time, Pallas kernels for 16%

profile of v3, /device:TPU:0, one launch (start us, length us, event | category | flops | bytes accessed | tf_op | source)
XLA Modules:
  0.0 63.2 jit_solution(9490533517547516593)
XLA Ops:
  0.0 0.0 copy-start
  0.0 3.1 %collective-permute-start = (bf16[64,512]{1,0:T(8,128)(2,1)}, bf16[64,512]{1,0:T(8,128)(2,1)S(1)}, u32[]{:S(2)}, u32[]{:S(2)}) collective-permute-start(bf16[64,512]{1,0:T(8,128)(2,1)} %param.5), channel_id=1, source_target_pairs={{0,8},{1,9},{2,10},{3,11},{4,12},{5,13},{6,14},{7,15},{8,0},{9,1},... | collective-permute-start | bytes 196616 | tf_op jit(solution)/shard_map/ppermute | solution.py:167
  3.1 2.6 %collective-permute-start.1 = (bf16[64,512]{1,0:T(8,128)(2,1)}, bf16[64,512]{1,0:T(8,128)(2,1)S(1)}, u32[]{:S(2)}, u32[]{:S(2)}) collective-permute-start(bf16[64,512]{1,0:T(8,128)(2,1)} %param.5), channel_id=1, source_target_pairs={{0,16},{1,17},{2,18},{3,19},{4,20},{5,21},{6,22},{7,23},{8,24},{9,... | collective-permute-start | bytes 196616 | tf_op jit(solution)/shard_map/ppermute | solution.py:167
  5.6 0.0 collective-permute-start.2
  5.6 1.7 %collective-permute-start.4 = (bf16[2048,128]{1,0:T(8,128)(2,1)}, bf16[2048,128]{1,0:T(8,128)(2,1)S(1)}, u32[]{:S(2)}, u32[]{:S(2)}) collective-permute-start(bf16[2048,128]{1,0:T(8,128)(2,1)} %bitcast.2), channel_id=1, source_target_pairs={{0,2},{1,5},{2,0},{3,7},{4,6},{5,1},{6,4},{7,3},{8,10},{9,13},{10,... | collective-permute-start | bytes 1572872 | tf_op jit(solution)/shard_map/ppermute | solution.py:167
  7.4 0.3 collective-permute-start.5
  7.7 0.8 %constant_dynamic-update-slice_fusion.3 = bf16[256,512]{1,0:T(8,128)(2,1)S(1)} fusion(bf16[64,512]{1,0:T(8,128)(2,1)} %param.5), kind=kLoop, calls=%fused_computation.9 | loop fusion | bytes 131072
  8.5 0.0 collective-permute-done
  8.5 2.0 %collective-permute-done.1 = bf16[64,512]{1,0:T(8,128)(2,1)S(1)} collective-permute-done((bf16[64,512]{1,0:T(8,128)(2,1)}, bf16[64,512]{1,0:T(8,128)(2,1)S(1)}, u32[]{:S(2)}, u32[]{:S(2)}) %collective-permute-start.1) | collective-permute-done | bytes 65568 | tf_op jit(solution)/shard_map/ppermute | solution.py:167
  10.6 1.4 %collective-permute-done.2 = bf16[64,512]{1,0:T(8,128)(2,1)S(1)} collective-permute-done((bf16[64,512]{1,0:T(8,128)(2,1)}, bf16[64,512]{1,0:T(8,128)(2,1)S(1)}, u32[]{:S(2)}, u32[]{:S(2)}) %collective-permute-start.2) | collective-permute-done | bytes 65568 | tf_op jit(solution)/shard_map/ppermute | solution.py:167
  12.0 1.5 %collective-permute-start.6 = (bf16[256,512]{1,0:T(8,128)(2,1)S(1)}, bf16[256,512]{1,0:T(8,128)(2,1)S(1)}, u32[]{:S(2)}, u32[]{:S(2)}) collective-permute-start(bf16[256,512]{1,0:T(8,128)(2,1)S(1)} %constant_dynamic-update-slice_fusion.q_ref), channel_id=1, source_target_pairs={{0,4},{1,3},{2,6},{3,1},{4,0},{5,7},{6,2},{7,5},{8,12},{9,11},{10,... | collective-permute-start | bytes 786440 | tf_op jit(solution)/shard_map/ppermute | solution.py:167
  13.5 1.5 %collective-permute-start.3 = (s32[8,16]{1,0:T(8,128)}, s32[8,16]{1,0:T(8,128)S(1)}, u32[]{:S(2)}, u32[]{:S(2)}) collective-permute-start(s32[8,16]{1,0:T(8,128)} %refs_0_.5), channel_id=1, source_target_pairs={{0,2},{1,5},{2,0},{3,7},{4,6},{5,1},{6,4},{7,3},{8,10},{9,13},{10,... | collective-permute-start | bytes 1544 | tf_op jit(solution)/shard_map/ppermute | solution.py:167
  15.0 1.6 %collective-permute-start.17 = (bf16[512,256]{1,0:T(8,128)(2,1)}, bf16[512,256]{1,0:T(8,128)(2,1)S(1)}, u32[]{:S(2)}, u32[]{:S(2)}) collective-permute-start(bf16[512,256]{1,0:T(8,128)(2,1)} %param.9), channel_id=1, source_target_pairs={{0,16},{1,17},{2,18},{3,19},{4,20},{5,21},{6,22},{7,23},{8,24},{9,... | collective-permute-start | bytes 786440 | tf_op jit(solution)/shard_map/ppermute | solution.py:167
  16.5 0.0 copy-start.2
  16.5 0.0 copy-done
  16.5 0.7 %copy-done.2 = s32[8,16]{1,0:T(8,128)S(1)} copy-done((s32[8,16]{1,0:T(8,128)S(1)}, s32[8,16]{1,0:T(8,128)}, u32[]{:S(2)}) %copy-start.2) | copy-done | bytes 536
  17.2 0.0 copy-start.1
  17.2 1.0 %copy-done.1 = bf16[1,2048,128]{2,1,0:T(8,128)(2,1)S(1)} copy-done((bf16[1,2048,128]{2,1,0:T(8,128)(2,1)S(1)}, bf16[1,2048,128]{2,1,0:T(8,128)(2,1)}, u32[]{:S(2)}) %copy-start.1) | copy-done | bytes 524312
  18.3 2.5 %shard_map.55.refs_3_ = f32[256,512]{1,0:T(8,128)S(1)} custom-call(bf16[256,512]{1,0:T(8,128)(2,1)S(1)} %constant_dynamic-update-slice_fusion.q_ref, s32[8,16]{1,0:T(8,128)S(1)} %copy-done.2, bf16[2048,128]{1,0:T(8,128)(2,1)S(1)} %bitcast.3, bf16[2048,128]{1,0:T(8,128)(2,1)S(1)} %bitcast.7), custom_call_target="tpu_custom_call" | custom-call | flops 1073741824 | bytes 1048576 | tf_op jit(solution)/shard_map/pallas_call | solution.py:85
  20.7 2.8 %collective-permute-done.3.refs_0_.refs_3_ = s32[8,16]{1,0:T(8,128)S(1)} collective-permute-done((s32[8,16]{1,0:T(8,128)}, s32[8,16]{1,0:T(8,128)S(1)}, u32[]{:S(2)}, u32[]{:S(2)}) %collective-permute-start.3) | collective-permute-done | bytes 544 | tf_op jit(solution)/shard_map/ppermute | solution.py:167
  23.5 0.0 collective-permute-done.6.q_ref
  23.5 0.0 collective-permute-done.4.refs_1_.refs_4_
  23.5 0.0 collective-permute-done.5.refs_2_.refs_5_
  23.5 2.5 %shard_map.60 = bf16[128,512]{1,0:T(8,128)(2,1)S(1)} custom-call(bf16[256,512]{1,0:T(8,128)(2,1)S(1)} %collective-permute-done.6.q_ref, s32[8,16]{1,0:T(8,128)S(1)} %copy-done.2, bf16[2048,128]{1,0:T(8,128)(2,1)S(1)} %bitcast.4, bf16[2048,128]{1,0:T(8,128)(2,1)S(1)} %bitcast.8, s32[8,16]{1,0:T(8,128)S(1)} %collective-permute-done.3.refs_0_.refs_3_, ...), custom_call_target="tpu_custom_call" | custom-call | flops 1073741824 | bytes 1048576 | tf_op jit(solution)/shard_map/pallas_call | solution.py:85
  26.0 1.8 %collective-permute-start.8 = (bf16[128,512]{1,0:T(8,128)(2,1)S(1)}, bf16[128,512]{1,0:T(8,128)(2,1)S(1)}, u32[]{:S(2)}, u32[]{:S(2)}) collective-permute-start(bf16[128,512]{1,0:T(8,128)(2,1)S(1)} %shard_map.60), channel_id=1, source_target_pairs={{0,4},{1,3},{2,6},{3,1},{4,0},{5,7},{6,2},{7,5},{8,12},{9,11},{10,... | collective-permute-start | bytes 393224 | tf_op jit(solution)/shard_map/ppermute | solution.py:167
  27.8 2.5 %shard_map.57 = bf16[128,512]{1,0:T(8,128)(2,1)S(1)} custom-call(bf16[256,512]{1,0:T(8,128)(2,1)S(1)} %collective-permute-done.6.q_ref, s32[8,16]{1,0:T(8,128)S(1)} %copy-done.2, bf16[2048,128]{1,0:T(8,128)(2,1)S(1)} %bitcast.5, bf16[2048,128]{1,0:T(8,128)(2,1)S(1)} %bitcast.9, s32[8,16]{1,0:T(8,128)S(1)} %collective-permute-done.3.refs_0_.refs_3_, ...), custom_call_target="tpu_custom_call" | custom-call | flops 1073741824 | bytes 1048576 | tf_op jit(solution)/shard_map/pallas_call | solution.py:85
  30.3 0.4 collective-permute-start.7
  30.6 1.4 %shard_map.59.part_ref = f32[128,512]{1,0:T(8,128)S(1)} custom-call(bf16[256,512]{1,0:T(8,128)(2,1)S(1)} %constant_dynamic-update-slice_fusion.q_ref, s32[8,16]{1,0:T(8,128)S(1)} %collective-permute-done.3.refs_0_.refs_3_, bf16[2048,128]{1,0:T(8,128)(2,1)S(1)} %collective-permute-done.4.refs_1_.refs_4_, ...), custom_call_target="tpu_custom_call" | custom-call | flops 536870912 | bytes 1048576 | tf_op jit(solution)/shard_map/pallas_call | solution.py:85
  32.0 0.0 copy-start.3
  32.0 0.0 collective-permute-done.8.share_ref
  32.1 1.0 %collective-permute-start.9 = (bf16[64,512]{1,0:T(8,128)(2,1)S(1)}, bf16[64,512]{1,0:T(8,128)(2,1)S(1)}, u32[]{:S(2)}, u32[]{:S(2)}) collective-permute-start(bf16[64,512]{1,0:T(8,128)(2,1)S(1)} %get-tuple-element.15), channel_id=1, source_target_pairs={{0,8},{1,9},{2,10},{3,11},{4,12},{5,13},{6,14},{7,15},{8,0},{9,1},... | collective-permute-start | bytes 196616 | tf_op jit(solution)/shard_map/ppermute | solution.py:167
  33.0 0.0 collective-permute-done.17
  33.0 0.0 copy-done.3
  33.1 0.1 collective-permute-start.18
  33.2 1.4 %shard_map.56.part_ref = f32[128,512]{1,0:T(8,128)S(1)} custom-call(bf16[256,512]{1,0:T(8,128)(2,1)S(1)} %constant_dynamic-update-slice_fusion.q_ref, s32[8,16]{1,0:T(8,128)S(1)} %collective-permute-done.3.refs_0_.refs_3_, bf16[2048,128]{1,0:T(8,128)(2,1)S(1)} %collective-permute-done.4.refs_1_.refs_4_, ...), custom_call_target="tpu_custom_call" | custom-call | flops 536870912 | bytes 1048576 | tf_op jit(solution)/shard_map/pallas_call | solution.py:85
  34.6 0.8 %collective-permute-done.7.share_ref = bf16[128,512]{1,0:T(8,128)(2,1)S(1)} collective-permute-done((bf16[128,512]{1,0:T(8,128)(2,1)S(1)}, bf16[128,512]{1,0:T(8,128)(2,1)S(1)}, u32[]{:S(2)}, u32[]{:S(2)}) %collective-permute-start.7) | collective-permute-done | bytes 131104 | tf_op jit(solution)/shard_map/ppermute | solution.py:167
  35.3 0.7 %collective-permute-start.11 = (bf16[64,512]{1,0:T(8,128)(2,1)S(1)}, bf16[64,512]{1,0:T(8,128)(2,1)S(1)}, u32[]{:S(2)}, u32[]{:S(2)}) collective-permute-start(bf16[64,512]{1,0:T(8,128)(2,1)S(1)} %get-tuple-element.16), channel_id=1, source_target_pairs={{0,8},{1,9},{2,10},{3,11},{4,12},{5,13},{6,14},{7,15},{8,0},{9,1},... | collective-permute-start | bytes 196616 | tf_op jit(solution)/shard_map/ppermute | solution.py:167
  36.1 0.3 collective-permute-done.9
  36.4 3.2 %collective-permute-start.10 = (bf16[64,512]{1,0:T(8,128)(2,1)S(1)}, bf16[64,512]{1,0:T(8,128)(2,1)S(1)}, u32[]{:S(2)}, u32[]{:S(2)}) collective-permute-start(bf16[64,512]{1,0:T(8,128)(2,1)S(1)} %add_convert_fusion.1), channel_id=1, source_target_pairs={{0,16},{1,17},{2,18},{3,19},{4,20},{5,21},{6,22},{7,23},{8,24},{9,... | collective-permute-start | bytes 196616 | tf_op jit(solution)/shard_map/ppermute | solution.py:167
  39.7 0.0 collective-permute-done.18
  39.7 1.0 %collective-permute-start.19 = (bf16[1024,256]{1,0:T(8,128)(2,1)S(1)}, bf16[1024,256]{1,0:T(8,128)(2,1)S(1)}, u32[]{:S(2)}, u32[]{:S(2)}) collective-permute-start(bf16[1024,256]{1,0:T(8,128)(2,1)S(1)} %pad_maximum_fusion.refs_4_), channel_id=1, source_target_pairs={{0,4},{1,5},{2,6},{3,7},{4,0},{5,1},{6,2},{7,3},{8,12},{9,13},{10,... | collective-permute-start | bytes 1572872 | tf_op jit(solution)/shard_map/ppermute | solution.py:167
  40.7 0.0 collective-permute-done.11
  40.7 1.5 %collective-permute-done.10 = bf16[64,512]{1,0:T(8,128)(2,1)S(1)} collective-permute-done((bf16[64,512]{1,0:T(8,128)(2,1)S(1)}, bf16[64,512]{1,0:T(8,128)(2,1)S(1)}, u32[]{:S(2)}, u32[]{:S(2)}) %collective-permute-start.10) | collective-permute-done | bytes 65568 | tf_op jit(solution)/shard_map/ppermute | solution.py:167
  42.2 2.8 %collective-permute-start.13 = (bf16[64,512]{1,0:T(8,128)(2,1)S(1)}, bf16[64,512]{1,0:T(8,128)(2,1)S(1)}, u32[]{:S(2)}, u32[]{:S(2)}) collective-permute-start(bf16[64,512]{1,0:T(8,128)(2,1)S(1)} %add_convert_fusion), channel_id=1, source_target_pairs={{0,10},{1,11},{2,8},{3,9},{4,14},{5,15},{6,12},{7,13},{8,2},{9,3},... | collective-permute-start | bytes 196616 | tf_op jit(solution)/shard_map/ppermute | solution.py:167
  45.1 0.2 collective-permute-start.12
  45.2 2.7 %collective-permute-done.13 = bf16[64,512]{1,0:T(8,128)(2,1)S(1)} collective-permute-done((bf16[64,512]{1,0:T(8,128)(2,1)S(1)}, bf16[64,512]{1,0:T(8,128)(2,1)S(1)}, u32[]{:S(2)}, u32[]{:S(2)}) %collective-permute-start.13) | collective-permute-done | bytes 65568 | tf_op jit(solution)/shard_map/ppermute | solution.py:167
  47.9 1.4 %collective-permute-done.12 = bf16[64,512]{1,0:T(8,128)(2,1)S(1)} collective-permute-done((bf16[64,512]{1,0:T(8,128)(2,1)S(1)}, bf16[64,512]{1,0:T(8,128)(2,1)S(1)}, u32[]{:S(2)}, u32[]{:S(2)}) %collective-permute-start.12) | collective-permute-done | bytes 65568 | tf_op jit(solution)/shard_map/ppermute | solution.py:167
  49.4 0.1 collective-permute-start.15
  49.4 0.6 collective-permute-start.14
  50.0 3.9 %collective-permute-done.14.refs_1_ = bf16[64,512]{1,0:T(8,128)(2,1)S(1)} collective-permute-done((bf16[64,512]{1,0:T(8,128)(2,1)S(1)}, bf16[64,512]{1,0:T(8,128)(2,1)S(1)}, u32[]{:S(2)}, u32[]{:S(2)}) %collective-permute-start.14) | collective-permute-done | bytes 65568 | tf_op jit(solution)/shard_map/ppermute | solution.py:167
  53.9 0.0 collective-permute-start.16
  53.9 1.3 %collective-permute-done.16.refs_3_ = bf16[64,512]{1,0:T(8,128)(2,1)S(1)} collective-permute-done((bf16[64,512]{1,0:T(8,128)(2,1)S(1)}, bf16[64,512]{1,0:T(8,128)(2,1)S(1)}, u32[]{:S(2)}, u32[]{:S(2)}) %collective-permute-start.16) | collective-permute-done | bytes 65568 | tf_op jit(solution)/shard_map/ppermute | solution.py:167
  55.2 0.0 collective-permute-done.15.refs_2_
  55.2 0.0 collective-permute-done.19.refs_5_
  55.2 0.4 shard_map.62
  55.6 0.6 collective-permute-start.20
  56.2 1.0 %collective-permute-start.21 = (bf16[64,512]{1,0:T(8,128)(2,1)S(1)}, bf16[64,512]{1,0:T(8,128)(2,1)S(1)}, u32[]{:S(2)}, u32[]{:S(2)}) collective-permute-start(bf16[64,512]{1,0:T(8,128)(2,1)S(1)} %get-tuple-element.19), channel_id=1, source_target_pairs={{0,8},{1,9},{2,10},{3,11},{4,12},{5,13},{6,14},{7,15},{8,0},{9,1},... | collective-permute-start | bytes 196616 | tf_op jit(solution)/shard_map/ppermute | solution.py:167
  57.2 1.9 %collective-permute-start.22 = (bf16[64,512]{1,0:T(8,128)(2,1)S(1)}, bf16[64,512]{1,0:T(8,128)(2,1)S(1)}, u32[]{:S(2)}, u32[]{:S(2)}) collective-permute-start(bf16[64,512]{1,0:T(8,128)(2,1)S(1)} %get-tuple-element.20), channel_id=1, source_target_pairs={{0,10},{1,11},{2,8},{3,9},{4,14},{5,15},{6,12},{7,13},{8,2},{9,3},... | collective-permute-start | bytes 196616 | tf_op jit(solution)/shard_map/ppermute | solution.py:167
  59.2 0.8 %collective-permute-done.20.refs_1_ = bf16[64,512]{1,0:T(8,128)(2,1)S(1)} collective-permute-done((bf16[64,512]{1,0:T(8,128)(2,1)S(1)}, bf16[64,512]{1,0:T(8,128)(2,1)S(1)}, u32[]{:S(2)}, u32[]{:S(2)}) %collective-permute-start.20) | collective-permute-done | bytes 65568 | tf_op jit(solution)/shard_map/ppermute | solution.py:167
  60.0 0.9 %collective-permute-done.21.refs_2_ = bf16[64,512]{1,0:T(8,128)(2,1)S(1)} collective-permute-done((bf16[64,512]{1,0:T(8,128)(2,1)S(1)}, bf16[64,512]{1,0:T(8,128)(2,1)S(1)}, u32[]{:S(2)}, u32[]{:S(2)}) %collective-permute-start.21) | collective-permute-done | bytes 65568 | tf_op jit(solution)/shard_map/ppermute | solution.py:167
  60.9 1.6 %collective-permute-done.22.refs_3_ = bf16[64,512]{1,0:T(8,128)(2,1)S(1)} collective-permute-done((bf16[64,512]{1,0:T(8,128)(2,1)S(1)}, bf16[64,512]{1,0:T(8,128)(2,1)S(1)}, u32[]{:S(2)}, u32[]{:S(2)}) %collective-permute-start.22) | collective-permute-done | bytes 65568 | tf_op jit(solution)/shard_map/ppermute | solution.py:167
  62.4 0.7 %shard_map.63 = bf16[64,2048]{1,0:T(8,128)(2,1)} custom-call(bf16[64,512]{1,0:T(8,128)(2,1)S(1)} %get-tuple-element.17.refs_0_, bf16[64,512]{1,0:T(8,128)(2,1)S(1)} %collective-permute-done.20.refs_1_, bf16[64,512]{1,0:T(8,128)(2,1)S(1)} %collective-permute-done.21.refs_2_, bf16[64,512]{1,0:T(8,128)(2,1)S(1)} %collective-permute-done.22.refs_3_), custom_call_target="tpu_custom_call" | custom-call | bytes 1048576 | tf_op jit(solution)/shard_map/pallas_call | solution.py:100
  (10 shorter events, 0.2 us)
Async XLA Ops:
  0.0 16.5 %copy-start = (bf16[1,2048,128]{2,1,0:T(8,128)(2,1)S(1)}, bf16[1,2048,128]{2,1,0:T(8,128)(2,1)}, u32[]{:S(2)}) copy-start(bf16[1,2048,128]{2,1,0:T(8,128)(2,1)} %param.6) | copy-start | bytes 1572868
  0.0 8.5 %collective-permute-start = (bf16[64,512]{1,0:T(8,128)(2,1)}, bf16[64,512]{1,0:T(8,128)(2,1)S(1)}, u32[]{:S(2)}, u32[]{:S(2)}) collective-permute-start(bf16[64,512]{1,0:T(8,128)(2,1)} %param.5), channel_id=1, source_target_pairs={{0,8},{1,9},{2,10},{3,11},{4,12},{5,13},{6,14},{7,15},{8,0},{9,1},... | collective-permute-start | bytes 196616 | tf_op jit(solution)/shard_map/ppermute | solution.py:167
  3.1 7.5 %collective-permute-start.1 = (bf16[64,512]{1,0:T(8,128)(2,1)}, bf16[64,512]{1,0:T(8,128)(2,1)S(1)}, u32[]{:S(2)}, u32[]{:S(2)}) collective-permute-start(bf16[64,512]{1,0:T(8,128)(2,1)} %param.5), channel_id=1, source_target_pairs={{0,16},{1,17},{2,18},{3,19},{4,20},{5,21},{6,22},{7,23},{8,24},{9,... | collective-permute-start | bytes 196616 | tf_op jit(solution)/shard_map/ppermute | solution.py:167
  5.6 6.3 %collective-permute-start.2 = (bf16[64,512]{1,0:T(8,128)(2,1)}, bf16[64,512]{1,0:T(8,128)(2,1)S(1)}, u32[]{:S(2)}, u32[]{:S(2)}) collective-permute-start(bf16[64,512]{1,0:T(8,128)(2,1)} %param.5), channel_id=1, source_target_pairs={{0,24},{1,25},{2,26},{3,27},{4,28},{5,29},{6,30},{7,31},{8,16},{9,... | collective-permute-start | bytes 196616 | tf_op jit(solution)/shard_map/ppermute | solution.py:167
  5.6 17.9 %collective-permute-start.4 = (bf16[2048,128]{1,0:T(8,128)(2,1)}, bf16[2048,128]{1,0:T(8,128)(2,1)S(1)}, u32[]{:S(2)}, u32[]{:S(2)}) collective-permute-start(bf16[2048,128]{1,0:T(8,128)(2,1)} %bitcast.2), channel_id=1, source_target_pairs={{0,2},{1,5},{2,0},{3,7},{4,6},{5,1},{6,4},{7,3},{8,10},{9,13},{10,... | collective-permute-start | bytes 1572872 | tf_op jit(solution)/shard_map/ppermute | solution.py:167
  7.4 16.2 %collective-permute-start.5 = (bf16[2048,128]{1,0:T(8,128)(2,1)}, bf16[2048,128]{1,0:T(8,128)(2,1)S(1)}, u32[]{:S(2)}, u32[]{:S(2)}) collective-permute-start(bf16[2048,128]{1,0:T(8,128)(2,1)} %bitcast.6), channel_id=1, source_target_pairs={{0,2},{1,5},{2,0},{3,7},{4,6},{5,1},{6,4},{7,3},{8,10},{9,13},{10,... | collective-permute-start | bytes 1572872 | tf_op jit(solution)/shard_map/ppermute | solution.py:167
  12.0 11.6 %collective-permute-start.6 = (bf16[256,512]{1,0:T(8,128)(2,1)S(1)}, bf16[256,512]{1,0:T(8,128)(2,1)S(1)}, u32[]{:S(2)}, u32[]{:S(2)}) collective-permute-start(bf16[256,512]{1,0:T(8,128)(2,1)S(1)} %constant_dynamic-update-slice_fusion.q_ref), channel_id=1, source_target_pairs={{0,4},{1,3},{2,6},{3,1},{4,0},{5,7},{6,2},{7,5},{8,12},{9,11},{10,... | collective-permute-start | bytes 786440 | tf_op jit(solution)/shard_map/ppermute | solution.py:167
  13.5 10.0 %collective-permute-start.3 = (s32[8,16]{1,0:T(8,128)}, s32[8,16]{1,0:T(8,128)S(1)}, u32[]{:S(2)}, u32[]{:S(2)}) collective-permute-start(s32[8,16]{1,0:T(8,128)} %refs_0_.5), channel_id=1, source_target_pairs={{0,2},{1,5},{2,0},{3,7},{4,6},{5,1},{6,4},{7,3},{8,10},{9,13},{10,... | collective-permute-start | bytes 1544 | tf_op jit(solution)/shard_map/ppermute | solution.py:167
  15.0 18.1 %collective-permute-start.17 = (bf16[512,256]{1,0:T(8,128)(2,1)}, bf16[512,256]{1,0:T(8,128)(2,1)S(1)}, u32[]{:S(2)}, u32[]{:S(2)}) collective-permute-start(bf16[512,256]{1,0:T(8,128)(2,1)} %param.9), channel_id=1, source_target_pairs={{0,16},{1,17},{2,18},{3,19},{4,20},{5,21},{6,22},{7,23},{8,24},{9,... | collective-permute-start | bytes 786440 | tf_op jit(solution)/shard_map/ppermute | solution.py:167
  16.5 0.7 %copy-start.2 = (s32[8,16]{1,0:T(8,128)S(1)}, s32[8,16]{1,0:T(8,128)}, u32[]{:S(2)}) copy-start(s32[8,16]{1,0:T(8,128)} %refs_0_.5) | copy-start | bytes 1540
  17.2 1.0 %copy-start.1 = (bf16[1,2048,128]{2,1,0:T(8,128)(2,1)S(1)}, bf16[1,2048,128]{2,1,0:T(8,128)(2,1)}, u32[]{:S(2)}) copy-start(bf16[1,2048,128]{2,1,0:T(8,128)(2,1)} %param.7) | copy-start | bytes 1572868
  26.0 6.0 %collective-permute-start.8 = (bf16[128,512]{1,0:T(8,128)(2,1)S(1)}, bf16[128,512]{1,0:T(8,128)(2,1)S(1)}, u32[]{:S(2)}, u32[]{:S(2)}) collective-permute-start(bf16[128,512]{1,0:T(8,128)(2,1)S(1)} %shard_map.60), channel_id=1, source_target_pairs={{0,4},{1,3},{2,6},{3,1},{4,0},{5,7},{6,2},{7,5},{8,12},{9,11},{10,... | collective-permute-start | bytes 393224 | tf_op jit(solution)/shard_map/ppermute | solution.py:167
  30.3 5.0 %collective-permute-start.7 = (bf16[128,512]{1,0:T(8,128)(2,1)S(1)}, bf16[128,512]{1,0:T(8,128)(2,1)S(1)}, u32[]{:S(2)}, u32[]{:S(2)}) collective-permute-start(bf16[128,512]{1,0:T(8,128)(2,1)S(1)} %shard_map.57), channel_id=1, source_target_pairs={{0,4},{1,3},{2,6},{3,1},{4,0},{5,7},{6,2},{7,5},{8,12},{9,11},{10,... | collective-permute-start | bytes 393224 | tf_op jit(solution)/shard_map/ppermute | solution.py:167
  32.0 1.0 %copy-start.3 = (bf16[512,256]{1,0:T(8,128)(2,1)S(1)}, bf16[512,256]{1,0:T(8,128)(2,1)}, u32[]{:S(2)}) copy-start(bf16[512,256]{1,0:T(8,128)(2,1)} %param.9) | copy-start | bytes 786436
  32.1 4.3 %collective-permute-start.9 = (bf16[64,512]{1,0:T(8,128)(2,1)S(1)}, bf16[64,512]{1,0:T(8,128)(2,1)S(1)}, u32[]{:S(2)}, u32[]{:S(2)}) collective-permute-start(bf16[64,512]{1,0:T(8,128)(2,1)S(1)} %get-tuple-element.15), channel_id=1, source_target_pairs={{0,8},{1,9},{2,10},{3,11},{4,12},{5,13},{6,14},{7,15},{8,0},{9,1},... | collective-permute-start | bytes 196616 | tf_op jit(solution)/shard_map/ppermute | solution.py:167
  33.1 6.6 %collective-permute-start.18 = (bf16[512,256]{1,0:T(8,128)(2,1)S(1)}, bf16[512,256]{1,0:T(8,128)(2,1)S(1)}, u32[]{:S(2)}, u32[]{:S(2)}) collective-permute-start(bf16[512,256]{1,0:T(8,128)(2,1)S(1)} %get-tuple-element.22), channel_id=1, source_target_pairs={{0,1},{1,0},{2,3},{3,2},{4,5},{5,4},{6,7},{7,6},{8,9},{9,8},{10,11... | collective-permute-start | bytes 786440 | tf_op jit(solution)/shard_map/ppermute | solution.py:167
  35.3 5.4 %collective-permute-start.11 = (bf16[64,512]{1,0:T(8,128)(2,1)S(1)}, bf16[64,512]{1,0:T(8,128)(2,1)S(1)}, u32[]{:S(2)}, u32[]{:S(2)}) collective-permute-start(bf16[64,512]{1,0:T(8,128)(2,1)S(1)} %get-tuple-element.16), channel_id=1, source_target_pairs={{0,8},{1,9},{2,10},{3,11},{4,12},{5,13},{6,14},{7,15},{8,0},{9,1},... | collective-permute-start | bytes 196616 | tf_op jit(solution)/shard_map/ppermute | solution.py:167
  36.4 5.8 %collective-permute-start.10 = (bf16[64,512]{1,0:T(8,128)(2,1)S(1)}, bf16[64,512]{1,0:T(8,128)(2,1)S(1)}, u32[]{:S(2)}, u32[]{:S(2)}) collective-permute-start(bf16[64,512]{1,0:T(8,128)(2,1)S(1)} %add_convert_fusion.1), channel_id=1, source_target_pairs={{0,16},{1,17},{2,18},{3,19},{4,20},{5,21},{6,22},{7,23},{8,24},{9,... | collective-permute-start | bytes 196616 | tf_op jit(solution)/shard_map/ppermute | solution.py:167
  39.7 15.5 %collective-permute-start.19 = (bf16[1024,256]{1,0:T(8,128)(2,1)S(1)}, bf16[1024,256]{1,0:T(8,128)(2,1)S(1)}, u32[]{:S(2)}, u32[]{:S(2)}) collective-permute-start(bf16[1024,256]{1,0:T(8,128)(2,1)S(1)} %pad_maximum_fusion.refs_4_), channel_id=1, source_target_pairs={{0,4},{1,5},{2,6},{3,7},{4,0},{5,1},{6,2},{7,3},{8,12},{9,13},{10,... | collective-permute-start | bytes 1572872 | tf_op jit(solution)/shard_map/ppermute | solution.py:167
  42.2 5.7 %collective-permute-start.13 = (bf16[64,512]{1,0:T(8,128)(2,1)S(1)}, bf16[64,512]{1,0:T(8,128)(2,1)S(1)}, u32[]{:S(2)}, u32[]{:S(2)}) collective-permute-start(bf16[64,512]{1,0:T(8,128)(2,1)S(1)} %add_convert_fusion), channel_id=1, source_target_pairs={{0,10},{1,11},{2,8},{3,9},{4,14},{5,15},{6,12},{7,13},{8,2},{9,3},... | collective-permute-start | bytes 196616 | tf_op jit(solution)/shard_map/ppermute | solution.py:167
  45.1 4.3 %collective-permute-start.12 = (bf16[64,512]{1,0:T(8,128)(2,1)S(1)}, bf16[64,512]{1,0:T(8,128)(2,1)S(1)}, u32[]{:S(2)}, u32[]{:S(2)}) collective-permute-start(bf16[64,512]{1,0:T(8,128)(2,1)S(1)} %add_convert_fusion), channel_id=1, source_target_pairs={{0,8},{1,9},{2,10},{3,11},{4,12},{5,13},{6,14},{7,15},{8,0},{9,1},... | collective-permute-start | bytes 196616 | tf_op jit(solution)/shard_map/ppermute | solution.py:167
  49.4 5.8 %collective-permute-start.15 = (bf16[192,512]{1,0:T(8,128)(2,1)S(1)}, bf16[192,512]{1,0:T(8,128)(2,1)S(1)}, u32[]{:S(2)}, u32[]{:S(2)}) collective-permute-start(bf16[192,512]{1,0:T(8,128)(2,1)S(1)} %pad_maximum_fusion.1.refs_0_), channel_id=1, source_target_pairs={{0,1},{1,0},{2,3},{3,2},{4,5},{5,4},{6,7},{7,6},{8,9},{9,8},{10,11... | collective-permute-start | bytes 589832 | tf_op jit(solution)/shard_map/ppermute | solution.py:167
  49.4 4.5 %collective-permute-start.14 = (bf16[64,512]{1,0:T(8,128)(2,1)S(1)}, bf16[64,512]{1,0:T(8,128)(2,1)S(1)}, u32[]{:S(2)}, u32[]{:S(2)}) collective-permute-start(bf16[64,512]{1,0:T(8,128)(2,1)S(1)} %add_convert_fusion), channel_id=1, source_target_pairs={{0,2},{1,3},{2,0},{3,1},{4,6},{5,7},{6,4},{7,5},{8,10},{9,11},{10,... | collective-permute-start | bytes 196616 | tf_op jit(solution)/shard_map/ppermute | solution.py:167
  53.9 1.3 %collective-permute-start.16 = (bf16[64,512]{1,0:T(8,128)(2,1)S(1)}, bf16[64,512]{1,0:T(8,128)(2,1)S(1)}, u32[]{:S(2)}, u32[]{:S(2)}) collective-permute-start(bf16[64,512]{1,0:T(8,128)(2,1)S(1)} %collective-permute-done.14.refs_1_), channel_id=1, source_target_pairs={{0,1},{1,0},{2,3},{3,2},{4,5},{5,4},{6,7},{7,6},{8,9},{9,8},{10,11... | collective-permute-start | bytes 196616 | tf_op jit(solution)/shard_map/ppermute | solution.py:167
  55.6 4.3 %collective-permute-start.20 = (bf16[64,512]{1,0:T(8,128)(2,1)S(1)}, bf16[64,512]{1,0:T(8,128)(2,1)S(1)}, u32[]{:S(2)}, u32[]{:S(2)}) collective-permute-start(bf16[64,512]{1,0:T(8,128)(2,1)S(1)} %get-tuple-element.18), channel_id=1, source_target_pairs={{0,2},{1,3},{2,0},{3,1},{4,6},{5,7},{6,4},{7,5},{8,10},{9,11},{10,... | collective-permute-start | bytes 196616 | tf_op jit(solution)/shard_map/ppermute | solution.py:167
  56.2 4.6 %collective-permute-start.21 = (bf16[64,512]{1,0:T(8,128)(2,1)S(1)}, bf16[64,512]{1,0:T(8,128)(2,1)S(1)}, u32[]{:S(2)}, u32[]{:S(2)}) collective-permute-start(bf16[64,512]{1,0:T(8,128)(2,1)S(1)} %get-tuple-element.19), channel_id=1, source_target_pairs={{0,8},{1,9},{2,10},{3,11},{4,12},{5,13},{6,14},{7,15},{8,0},{9,1},... | collective-permute-start | bytes 196616 | tf_op jit(solution)/shard_map/ppermute | solution.py:167
  57.2 5.2 %collective-permute-start.22 = (bf16[64,512]{1,0:T(8,128)(2,1)S(1)}, bf16[64,512]{1,0:T(8,128)(2,1)S(1)}, u32[]{:S(2)}, u32[]{:S(2)}) collective-permute-start(bf16[64,512]{1,0:T(8,128)(2,1)S(1)} %get-tuple-element.20), channel_id=1, source_target_pairs={{0,10},{1,11},{2,8},{3,9},{4,14},{5,15},{6,12},{7,13},{8,2},{9,3},... | collective-permute-start | bytes 196616 | tf_op jit(solution)/shard_map/ppermute | solution.py:167

commit v4 on v3

--- a/solution.py
+++ b/solution.py
@@ -70,7 +70,7 @@
             here = (slice(j * own_rows, (j + 1) * own_rows), slice(i * head_size, (i + 1) * head_size))
             value = total[j * part + i * own_rows : j * part + (i + 1) * own_rows, :]
             if has_acc:
-                value = value + acc_in[members[j] * own_rows : (members[j] + 1) * own_rows, here[1]]
+                value = value + acc_in[here]
             out_ref[here] = value.astype(out_ref.dtype)
 
 
@@ -107,11 +107,12 @@
     )(*args)
 
 
-def merge_kernel(part_ref, share_ref, *out_refs):
+def merge_kernel(members, part_ref, share_ref, *out_refs):
     own_rows = out_refs[0].shape[0]
-    for j, out_ref in enumerate(out_refs):
-        rows = slice(j * own_rows, (j + 1) * own_rows)
-        out_ref[...] = (part_ref[rows, :] + share_ref[rows, :].astype(jnp.float32)).astype(out_ref.dtype)
+    for j, member in enumerate(members):
+        value = part_ref[member * own_rows : (member + 1) * own_rows, :]
+        value = value + share_ref[j * own_rows : (j + 1) * own_rows, :].astype(jnp.float32)
+        out_refs[j][...] = value.astype(out_refs[j].dtype)
 
 
 def project_kernel(heads, *refs):
@@ -205,30 +206,24 @@
     def attention(q, sources, flip, members, acc=None, dtype=jnp.float32):
         return attend(q, sources, offset, own_rows, flip, members, acc, dtype)
 
-    every, upper, lower = range(lines), range(2, lines), range(2)
+    every, upper, lower = range(lines), range(lines // 2, lines), range(lines // 2)
     part = attention(q_own, [near], (0, 0), every)
     share_upper = attention(q_other, [near, far], (2, 1), upper, dtype=jnp.bfloat16)
     share_upper = other(share_upper)
-    part_upper = attention(q_own, [far], (0, 0), upper, part)
     share_lower = attention(q_other, [near, far], (2, 1), lower, dtype=jnp.bfloat16)
     share_lower = other(share_lower)
-    part_lower = attention(q_own, [far], (0, 0), lower, part)
+    part = attention(q_own, [far], (0, 0), every, part)
     width = part.shape[1]
 
-    def merge(own, share, members):
-        shapes = [jax.ShapeDtypeStruct((own_rows, width), jnp.bfloat16 if m % 2 else jnp.float32) for m in members]
-        return small_call(merge_kernel, shapes, [own, share])
-
-    merged = merge(part_upper, share_upper, upper)
-    passed = along(jnp.concatenate(merged[1::2], axis=0), 1)
-    sends = [
-        (block + passed[i * own_rows : (i + 1) * own_rows].astype(jnp.float32)).astype(jnp.bfloat16)
-        for i, block in enumerate(merged[::2])
-    ]
-    sums, near_block = merge(part_lower, share_lower, lower)
-    for i, block in enumerate(sends):
-        sums = sums + along(block, 2 * i + 2).astype(jnp.float32)
-    sums = sums + along(near_block, 1).astype(jnp.float32)
+    def merge(share, members):
+        shapes = [jax.ShapeDtypeStruct((own_rows, width), jnp.bfloat16 if m else jnp.float32) for m in members]
+        return small_call(functools.partial(merge_kernel, members), shapes, [part, share])
+
+    merged = merge(share_upper, upper)
+    merged = merge(share_lower, lower) + merged
+    sums = merged[0]
+    for k in range(1, lines):
+        sums = sums + along(merged[k], k).astype(jnp.float32)
     attended = sums.astype(jnp.bfloat16)
 
     gathered = [inside(attended, k) for k in range(1, 4)]

time: 63.4 us -> 65.1 us (1.027)
  waiting for transfers between devices: 21.3 us -> 24 us
  local copies, waits for them, and re-layouts: 2.59 us -> 0.87 us
  starting transfers between devices: 27.6 us -> 28.7 us
    ppermute x23, waiting for transfers between devices: 21.3 us -> 24 us  [move(): return lax.ppermute(x, BOTH, pairs)]
    unnamed x11, local copies, waits for them, and re-layouts: 2.59 us -> 0.87 us
    ppermute x23, starting transfers between devices: 27.6 us -> 28.7 us  [move(): return lax.ppermute(x, BOTH, pairs)]
    pallas_call x5 -> x4, Pallas kernels: 10.2 us -> 9.9 us  [attend(): pl.pallas_call(functools.partial(attend_kernel, offset, own_rows, flip, m...]
  transfers between devices with their start and end apart: 23 -> 23, of which waited for: 13 -> 11; matrix products, arithmetic and copies ran while one was open for 2% -> 2% of each run, Pallas kernels for 16% -> 15%
where the time goes in v4:
time: 65.1 us; the launch traced here: 65 us
  starting transfers between devices  28.7 us (44%)
  waiting for transfers between devices  24 us (37%)
  Pallas kernels  11.1 us (17%)
  local copies, waits for them, and re-layouts  0.87 us (1%)
    ppermute x23, starting transfers between devices, move(): return lax.ppermute(x, BOTH, pairs)  28.7 us
    ppermute x23, waiting for transfers between devices, move(): return lax.ppermute(x, BOTH, pairs)  24 us
    pallas_call x4, Pallas kernels, attend(): pl.pallas_call(functools.partial(attend_kernel, offset, own_rows, flip, m...  9.9 us
  transfers between devices with their start and end apart: 23, of which 11 were waited for; matrix products, arithmetic and copies ran while one was open for 2% of the time, Pallas kernels for 15%

profile of v4, /device:TPU:0, one launch (start us, length us, event | category | flops | bytes accessed | tf_op | source)
XLA Modules:
  0.0 65.0 jit_solution(776015067103095228)
XLA Ops:
  0.0 3.1 %collective-permute-start = (bf16[64,512]{1,0:T(8,128)(2,1)}, bf16[64,512]{1,0:T(8,128)(2,1)S(1)}, u32[]{:S(2)}, u32[]{:S(2)}) collective-permute-start(bf16[64,512]{1,0:T(8,128)(2,1)} %param.5), channel_id=1, source_target_pairs={{0,8},{1,9},{2,10},{3,11},{4,12},{5,13},{6,14},{7,15},{8,0},{9,1},... | collective-permute-start | bytes 196616 | tf_op jit(solution)/shard_map/ppermute | solution.py:168
  3.1 2.6 %collective-permute-start.1 = (bf16[64,512]{1,0:T(8,128)(2,1)}, bf16[64,512]{1,0:T(8,128)(2,1)S(1)}, u32[]{:S(2)}, u32[]{:S(2)}) collective-permute-start(bf16[64,512]{1,0:T(8,128)(2,1)} %param.5), channel_id=1, source_target_pairs={{0,16},{1,17},{2,18},{3,19},{4,20},{5,21},{6,22},{7,23},{8,24},{9,... | collective-permute-start | bytes 196616 | tf_op jit(solution)/shard_map/ppermute | solution.py:168
  5.6 0.0 collective-permute-start.2
  5.6 1.7 %collective-permute-start.4 = (bf16[2048,128]{1,0:T(8,128)(2,1)}, bf16[2048,128]{1,0:T(8,128)(2,1)S(1)}, u32[]{:S(2)}, u32[]{:S(2)}) collective-permute-start(bf16[2048,128]{1,0:T(8,128)(2,1)} %bitcast.2), channel_id=1, source_target_pairs={{0,2},{1,5},{2,0},{3,7},{4,6},{5,1},{6,4},{7,3},{8,10},{9,13},{10,... | collective-permute-start | bytes 1572872 | tf_op jit(solution)/shard_map/ppermute | solution.py:168
  7.4 0.3 collective-permute-start.5
  7.7 0.8 %constant_dynamic-update-slice_fusion.3 = bf16[256,512]{1,0:T(8,128)(2,1)S(1)} fusion(bf16[64,512]{1,0:T(8,128)(2,1)} %param.5), kind=kLoop, calls=%fused_computation.8 | loop fusion | bytes 131072
  8.5 0.0 copy-start.3
  8.5 0.0 collective-permute-done
  8.5 2.0 %collective-permute-start.17 = (bf16[512,256]{1,0:T(8,128)(2,1)}, bf16[512,256]{1,0:T(8,128)(2,1)S(1)}, u32[]{:S(2)}, u32[]{:S(2)}) collective-permute-start(bf16[512,256]{1,0:T(8,128)(2,1)} %param.9), channel_id=1, source_target_pairs={{0,16},{1,17},{2,18},{3,19},{4,20},{5,21},{6,22},{7,23},{8,24},{9,... | collective-permute-start | bytes 786440 | tf_op jit(solution)/shard_map/ppermute | solution.py:168
  10.5 0.0 collective-permute-done.1
  10.5 0.0 copy-start.2
  10.6 1.5 %collective-permute-done.2 = bf16[64,512]{1,0:T(8,128)(2,1)S(1)} collective-permute-done((bf16[64,512]{1,0:T(8,128)(2,1)}, bf16[64,512]{1,0:T(8,128)(2,1)S(1)}, u32[]{:S(2)}, u32[]{:S(2)}) %collective-permute-start.2) | collective-permute-done | bytes 65568 | tf_op jit(solution)/shard_map/ppermute | solution.py:168
  12.0 1.5 %collective-permute-start.6 = (bf16[256,512]{1,0:T(8,128)(2,1)S(1)}, bf16[256,512]{1,0:T(8,128)(2,1)S(1)}, u32[]{:S(2)}, u32[]{:S(2)}) collective-permute-start(bf16[256,512]{1,0:T(8,128)(2,1)S(1)} %constant_dynamic-update-slice_fusion.q_ref), channel_id=1, source_target_pairs={{0,4},{1,3},{2,6},{3,1},{4,0},{5,7},{6,2},{7,5},{8,12},{9,11},{10,... | collective-permute-start | bytes 786440 | tf_op jit(solution)/shard_map/ppermute | solution.py:168
  13.5 0.0 copy-done.2
  13.6 1.5 %collective-permute-start.3 = (s32[8,16]{1,0:T(8,128)S(1)}, s32[8,16]{1,0:T(8,128)S(1)}, u32[]{:S(2)}, u32[]{:S(2)}) collective-permute-start(s32[8,16]{1,0:T(8,128)S(1)} %copy-done.2), channel_id=1, source_target_pairs={{0,2},{1,5},{2,0},{3,7},{4,6},{5,1},{6,4},{7,3},{8,10},{9,13},{10,... | collective-permute-start | bytes 1544 | tf_op jit(solution)/shard_map/ppermute | solution.py:168
  15.0 0.0 copy-start
  15.0 0.0 copy-start.1
  15.0 8.1 %collective-permute-done.17 = bf16[512,256]{1,0:T(8,128)(2,1)S(1)} collective-permute-done((bf16[512,256]{1,0:T(8,128)(2,1)}, bf16[512,256]{1,0:T(8,128)(2,1)S(1)}, u32[]{:S(2)}, u32[]{:S(2)}) %collective-permute-start.17) | collective-permute-done | bytes 262176 | tf_op jit(solution)/shard_map/ppermute | solution.py:168
  23.2 0.0 copy-done.3
  23.2 0.1 collective-permute-start.18
  23.3 0.2 collective-permute-done.3.refs_0_.refs_3_
  23.5 0.0 collective-permute-done.6.q_ref
  23.5 0.0 collective-permute-done.4.refs_1_.refs_4_
  23.5 0.0 collective-permute-done.5.refs_2_.refs_5_
  23.5 0.0 copy-done
  23.5 0.0 copy-done.1
  23.5 2.5 %shard_map.59 = bf16[128,512]{1,0:T(8,128)(2,1)S(1)} custom-call(bf16[256,512]{1,0:T(8,128)(2,1)S(1)} %collective-permute-done.6.q_ref, s32[8,16]{1,0:T(8,128)S(1)} %copy-done.2, bf16[2048,128]{1,0:T(8,128)(2,1)S(1)} %bitcast.3, bf16[2048,128]{1,0:T(8,128)(2,1)S(1)} %bitcast.7, s32[8,16]{1,0:T(8,128)S(1)} %collective-permute-done.3.refs_0_.refs_3_, ...), custom_call_target="tpu_custom_call" | custom-call | flops 1073741824 | bytes 1048576 | tf_op jit(solution)/shard_map/pallas_call | solution.py:85
  26.0 1.8 %collective-permute-start.9 = (bf16[128,512]{1,0:T(8,128)(2,1)S(1)}, bf16[128,512]{1,0:T(8,128)(2,1)S(1)}, u32[]{:S(2)}, u32[]{:S(2)}) collective-permute-start(bf16[128,512]{1,0:T(8,128)(2,1)S(1)} %shard_map.59), channel_id=1, source_target_pairs={{0,4},{1,3},{2,6},{3,1},{4,0},{5,7},{6,2},{7,5},{8,12},{9,11},{10,... | collective-permute-start | bytes 393224 | tf_op jit(solution)/shard_map/ppermute | solution.py:168
  27.8 2.5 %shard_map.57 = bf16[128,512]{1,0:T(8,128)(2,1)S(1)} custom-call(bf16[256,512]{1,0:T(8,128)(2,1)S(1)} %collective-permute-done.6.q_ref, s32[8,16]{1,0:T(8,128)S(1)} %copy-done.2, bf16[2048,128]{1,0:T(8,128)(2,1)S(1)} %bitcast.4, bf16[2048,128]{1,0:T(8,128)(2,1)S(1)} %bitcast.8, s32[8,16]{1,0:T(8,128)S(1)} %collective-permute-done.3.refs_0_.refs_3_, ...), custom_call_target="tpu_custom_call" | custom-call | flops 1073741824 | bytes 1048576 | tf_op jit(solution)/shard_map/pallas_call | solution.py:85
  30.3 0.4 collective-permute-start.7
  30.7 2.5 %shard_map.55.refs_3_ = f32[256,512]{1,0:T(8,128)S(1)} custom-call(bf16[256,512]{1,0:T(8,128)(2,1)S(1)} %constant_dynamic-update-slice_fusion.q_ref, s32[8,16]{1,0:T(8,128)S(1)} %copy-done.2, bf16[2048,128]{1,0:T(8,128)(2,1)S(1)} %bitcast.5, bf16[2048,128]{1,0:T(8,128)(2,1)S(1)} %bitcast.9), custom_call_target="tpu_custom_call" | custom-call | flops 1073741824 | bytes 1048576 | tf_op jit(solution)/shard_map/pallas_call | solution.py:85
  33.1 2.5 %shard_map.56.part_ref = f32[256,512]{1,0:T(8,128)S(1)} custom-call(bf16[256,512]{1,0:T(8,128)(2,1)S(1)} %constant_dynamic-update-slice_fusion.q_ref, s32[8,16]{1,0:T(8,128)S(1)} %collective-permute-done.3.refs_0_.refs_3_, bf16[2048,128]{1,0:T(8,128)(2,1)S(1)} %collective-permute-done.4.refs_1_.refs_4_, ...), custom_call_target="tpu_custom_call" | custom-call | flops 1073741824 | bytes 1048576 | tf_op jit(solution)/shard_map/pallas_call | solution.py:85
  35.6 0.0 collective-permute-done.9.share_ref
  35.7 3.9 %collective-permute-start.11 = (bf16[64,512]{1,0:T(8,128)(2,1)S(1)}, bf16[64,512]{1,0:T(8,128)(2,1)S(1)}, u32[]{:S(2)}, u32[]{:S(2)}) collective-permute-start(bf16[64,512]{1,0:T(8,128)(2,1)S(1)} %get-tuple-element.16), channel_id=1, source_target_pairs={{0,24},{1,25},{2,26},{3,27},{4,28},{5,29},{6,30},{7,31},{8,16},{9,... | collective-permute-start | bytes 196616 | tf_op jit(solution)/shard_map/ppermute | solution.py:168
  39.5 0.0 collective-permute-start.10
  39.6 0.0 collective-permute-done.7.share_ref
  39.6 0.7 %collective-permute-start.8 = (bf16[64,512]{1,0:T(8,128)(2,1)S(1)}, bf16[64,512]{1,0:T(8,128)(2,1)S(1)}, u32[]{:S(2)}, u32[]{:S(2)}) collective-permute-start(bf16[64,512]{1,0:T(8,128)(2,1)S(1)} %get-tuple-element.14), channel_id=1, source_target_pairs={{0,8},{1,9},{2,10},{3,11},{4,12},{5,13},{6,14},{7,15},{8,0},{9,1},... | collective-permute-start | bytes 196616 | tf_op jit(solution)/shard_map/ppermute | solution.py:168
  40.3 0.0 collective-permute-done.18
  40.3 1.7 %collective-permute-start.19 = (bf16[1024,256]{1,0:T(8,128)(2,1)S(1)}, bf16[1024,256]{1,0:T(8,128)(2,1)S(1)}, u32[]{:S(2)}, u32[]{:S(2)}) collective-permute-start(bf16[1024,256]{1,0:T(8,128)(2,1)S(1)} %pad_maximum_fusion.refs_4_), channel_id=1, source_target_pairs={{0,4},{1,5},{2,6},{3,7},{4,0},{5,1},{6,2},{7,3},{8,12},{9,13},{10,... | collective-permute-start | bytes 1572872 | tf_op jit(solution)/shard_map/ppermute | solution.py:168
  42.1 0.0 collective-permute-done.11
  42.1 2.7 %collective-permute-done.10 = bf16[64,512]{1,0:T(8,128)(2,1)S(1)} collective-permute-done((bf16[64,512]{1,0:T(8,128)(2,1)S(1)}, bf16[64,512]{1,0:T(8,128)(2,1)S(1)}, u32[]{:S(2)}, u32[]{:S(2)}) %collective-permute-start.10) | collective-permute-done | bytes 65568 | tf_op jit(solution)/shard_map/ppermute | solution.py:168
  44.8 0.0 collective-permute-done.8
  44.9 1.4 %collective-permute-start.13 = (bf16[64,512]{1,0:T(8,128)(2,1)S(1)}, bf16[64,512]{1,0:T(8,128)(2,1)S(1)}, u32[]{:S(2)}, u32[]{:S(2)}) collective-permute-start(bf16[64,512]{1,0:T(8,128)(2,1)S(1)} %add_convert_fusion), channel_id=1, source_target_pairs={{0,10},{1,11},{2,8},{3,9},{4,14},{5,15},{6,12},{7,13},{8,2},{9,3},... | collective-permute-start | bytes 196616 | tf_op jit(solution)/shard_map/ppermute | solution.py:168
  46.3 1.6 %collective-permute-start.12 = (bf16[64,512]{1,0:T(8,128)(2,1)S(1)}, bf16[64,512]{1,0:T(8,128)(2,1)S(1)}, u32[]{:S(2)}, u32[]{:S(2)}) collective-permute-start(bf16[64,512]{1,0:T(8,128)(2,1)S(1)} %add_convert_fusion), channel_id=1, source_target_pairs={{0,8},{1,9},{2,10},{3,11},{4,12},{5,13},{6,14},{7,15},{8,0},{9,1},... | collective-permute-start | bytes 196616 | tf_op jit(solution)/shard_map/ppermute | solution.py:168
  47.9 2.2 %collective-permute-done.13 = bf16[64,512]{1,0:T(8,128)(2,1)S(1)} collective-permute-done((bf16[64,512]{1,0:T(8,128)(2,1)S(1)}, bf16[64,512]{1,0:T(8,128)(2,1)S(1)}, u32[]{:S(2)}, u32[]{:S(2)}) %collective-permute-start.13) | collective-permute-done | bytes 65568 | tf_op jit(solution)/shard_map/ppermute | solution.py:168
  50.1 0.7 %collective-permute-done.12 = bf16[64,512]{1,0:T(8,128)(2,1)S(1)} collective-permute-done((bf16[64,512]{1,0:T(8,128)(2,1)S(1)}, bf16[64,512]{1,0:T(8,128)(2,1)S(1)}, u32[]{:S(2)}, u32[]{:S(2)}) %collective-permute-start.12) | collective-permute-done | bytes 65568 | tf_op jit(solution)/shard_map/ppermute | solution.py:168
  50.8 0.1 collective-permute-start.15
  50.9 0.8 %collective-permute-start.14 = (bf16[64,512]{1,0:T(8,128)(2,1)S(1)}, bf16[64,512]{1,0:T(8,128)(2,1)S(1)}, u32[]{:S(2)}, u32[]{:S(2)}) collective-permute-start(bf16[64,512]{1,0:T(8,128)(2,1)S(1)} %add_convert_fusion), channel_id=1, source_target_pairs={{0,2},{1,3},{2,0},{3,1},{4,6},{5,7},{6,4},{7,5},{8,10},{9,11},{10,... | collective-permute-start | bytes 196616 | tf_op jit(solution)/shard_map/ppermute | solution.py:168
  51.7 3.7 %collective-permute-done.14.refs_1_ = bf16[64,512]{1,0:T(8,128)(2,1)S(1)} collective-permute-done((bf16[64,512]{1,0:T(8,128)(2,1)S(1)}, bf16[64,512]{1,0:T(8,128)(2,1)S(1)}, u32[]{:S(2)}, u32[]{:S(2)}) %collective-permute-start.14) | collective-permute-done | bytes 65568 | tf_op jit(solution)/shard_map/ppermute | solution.py:168
  55.4 0.0 collective-permute-start.16
  55.4 1.3 %collective-permute-done.16.refs_3_ = bf16[64,512]{1,0:T(8,128)(2,1)S(1)} collective-permute-done((bf16[64,512]{1,0:T(8,128)(2,1)S(1)}, bf16[64,512]{1,0:T(8,128)(2,1)S(1)}, u32[]{:S(2)}, u32[]{:S(2)}) %collective-permute-start.16) | collective-permute-done | bytes 65568 | tf_op jit(solution)/shard_map/ppermute | solution.py:168
  56.7 0.0 collective-permute-done.15.refs_2_
  56.7 0.0 collective-permute-done.19.refs_5_
  56.7 0.4 shard_map.61
  57.1 0.8 %collective-permute-start.20 = (bf16[64,512]{1,0:T(8,128)(2,1)S(1)}, bf16[64,512]{1,0:T(8,128)(2,1)S(1)}, u32[]{:S(2)}, u32[]{:S(2)}) collective-permute-start(bf16[64,512]{1,0:T(8,128)(2,1)S(1)} %get-tuple-element.18), channel_id=1, source_target_pairs={{0,2},{1,3},{2,0},{3,1},{4,6},{5,7},{6,4},{7,5},{8,10},{9,11},{10,... | collective-permute-start | bytes 196616 | tf_op jit(solution)/shard_map/ppermute | solution.py:168
  57.9 1.1 %collective-permute-start.21 = (bf16[64,512]{1,0:T(8,128)(2,1)S(1)}, bf16[64,512]{1,0:T(8,128)(2,1)S(1)}, u32[]{:S(2)}, u32[]{:S(2)}) collective-permute-start(bf16[64,512]{1,0:T(8,128)(2,1)S(1)} %get-tuple-element.19), channel_id=1, source_target_pairs={{0,8},{1,9},{2,10},{3,11},{4,12},{5,13},{6,14},{7,15},{8,0},{9,1},... | collective-permute-start | bytes 196616 | tf_op jit(solution)/shard_map/ppermute | solution.py:168
  59.0 1.6 %collective-permute-start.22 = (bf16[64,512]{1,0:T(8,128)(2,1)S(1)}, bf16[64,512]{1,0:T(8,128)(2,1)S(1)}, u32[]{:S(2)}, u32[]{:S(2)}) collective-permute-start(bf16[64,512]{1,0:T(8,128)(2,1)S(1)} %get-tuple-element.20), channel_id=1, source_target_pairs={{0,10},{1,11},{2,8},{3,9},{4,14},{5,15},{6,12},{7,13},{8,2},{9,3},... | collective-permute-start | bytes 196616 | tf_op jit(solution)/shard_map/ppermute | solution.py:168
  60.7 0.8 %collective-permute-done.20.refs_1_ = bf16[64,512]{1,0:T(8,128)(2,1)S(1)} collective-permute-done((bf16[64,512]{1,0:T(8,128)(2,1)S(1)}, bf16[64,512]{1,0:T(8,128)(2,1)S(1)}, u32[]{:S(2)}, u32[]{:S(2)}) %collective-permute-start.20) | collective-permute-done | bytes 65568 | tf_op jit(solution)/shard_map/ppermute | solution.py:168
  61.5 0.8 %collective-permute-done.21.refs_2_ = bf16[64,512]{1,0:T(8,128)(2,1)S(1)} collective-permute-done((bf16[64,512]{1,0:T(8,128)(2,1)S(1)}, bf16[64,512]{1,0:T(8,128)(2,1)S(1)}, u32[]{:S(2)}, u32[]{:S(2)}) %collective-permute-start.21) | collective-permute-done | bytes 65568 | tf_op jit(solution)/shard_map/ppermute | solution.py:168
  62.3 2.0 %collective-permute-done.22.refs_3_ = bf16[64,512]{1,0:T(8,128)(2,1)S(1)} collective-permute-done((bf16[64,512]{1,0:T(8,128)(2,1)S(1)}, bf16[64,512]{1,0:T(8,128)(2,1)S(1)}, u32[]{:S(2)}, u32[]{:S(2)}) %collective-permute-start.22) | collective-permute-done | bytes 65568 | tf_op jit(solution)/shard_map/ppermute | solution.py:168
  64.2 0.7 %shard_map.62 = bf16[64,2048]{1,0:T(8,128)(2,1)} custom-call(bf16[64,512]{1,0:T(8,128)(2,1)S(1)} %get-tuple-element.17.refs_0_, bf16[64,512]{1,0:T(8,128)(2,1)S(1)} %collective-permute-done.20.refs_1_, bf16[64,512]{1,0:T(8,128)(2,1)S(1)} %collective-permute-done.21.refs_2_, bf16[64,512]{1,0:T(8,128)(2,1)S(1)} %collective-permute-done.22.refs_3_), custom_call_target="tpu_custom_call" | custom-call | bytes 1048576 | tf_op jit(solution)/shard_map/pallas_call | solution.py:100
  (9 shorter events, 0.2 us)
Async XLA Ops:
  0.0 8.5 %collective-permute-start = (bf16[64,512]{1,0:T(8,128)(2,1)}, bf16[64,512]{1,0:T(8,128)(2,1)S(1)}, u32[]{:S(2)}, u32[]{:S(2)}) collective-permute-start(bf16[64,512]{1,0:T(8,128)(2,1)} %param.5), channel_id=1, source_target_pairs={{0,8},{1,9},{2,10},{3,11},{4,12},{5,13},{6,14},{7,15},{8,0},{9,1},... | collective-permute-start | bytes 196616 | tf_op jit(solution)/shard_map/ppermute | solution.py:168
  3.1 7.5 %collective-permute-start.1 = (bf16[64,512]{1,0:T(8,128)(2,1)}, bf16[64,512]{1,0:T(8,128)(2,1)S(1)}, u32[]{:S(2)}, u32[]{:S(2)}) collective-permute-start(bf16[64,512]{1,0:T(8,128)(2,1)} %param.5), channel_id=1, source_target_pairs={{0,16},{1,17},{2,18},{3,19},{4,20},{5,21},{6,22},{7,23},{8,24},{9,... | collective-permute-start | bytes 196616 | tf_op jit(solution)/shard_map/ppermute | solution.py:168
  5.6 6.4 %collective-permute-start.2 = (bf16[64,512]{1,0:T(8,128)(2,1)}, bf16[64,512]{1,0:T(8,128)(2,1)S(1)}, u32[]{:S(2)}, u32[]{:S(2)}) collective-permute-start(bf16[64,512]{1,0:T(8,128)(2,1)} %param.5), channel_id=1, source_target_pairs={{0,24},{1,25},{2,26},{3,27},{4,28},{5,29},{6,30},{7,31},{8,16},{9,... | collective-permute-start | bytes 196616 | tf_op jit(solution)/shard_map/ppermute | solution.py:168
  5.6 17.9 %collective-permute-start.4 = (bf16[2048,128]{1,0:T(8,128)(2,1)}, bf16[2048,128]{1,0:T(8,128)(2,1)S(1)}, u32[]{:S(2)}, u32[]{:S(2)}) collective-permute-start(bf16[2048,128]{1,0:T(8,128)(2,1)} %bitcast.2), channel_id=1, source_target_pairs={{0,2},{1,5},{2,0},{3,7},{4,6},{5,1},{6,4},{7,3},{8,10},{9,13},{10,... | collective-permute-start | bytes 1572872 | tf_op jit(solution)/shard_map/ppermute | solution.py:168
  7.4 16.2 %collective-permute-start.5 = (bf16[2048,128]{1,0:T(8,128)(2,1)}, bf16[2048,128]{1,0:T(8,128)(2,1)S(1)}, u32[]{:S(2)}, u32[]{:S(2)}) collective-permute-start(bf16[2048,128]{1,0:T(8,128)(2,1)} %bitcast.6), channel_id=1, source_target_pairs={{0,2},{1,5},{2,0},{3,7},{4,6},{5,1},{6,4},{7,3},{8,10},{9,13},{10,... | collective-permute-start | bytes 1572872 | tf_op jit(solution)/shard_map/ppermute | solution.py:168
  8.5 14.7 %copy-start.3 = (bf16[512,256]{1,0:T(8,128)(2,1)S(1)}, bf16[512,256]{1,0:T(8,128)(2,1)}, u32[]{:S(2)}) copy-start(bf16[512,256]{1,0:T(8,128)(2,1)} %param.9) | copy-start | bytes 786436
  8.5 14.7 %collective-permute-start.17 = (bf16[512,256]{1,0:T(8,128)(2,1)}, bf16[512,256]{1,0:T(8,128)(2,1)S(1)}, u32[]{:S(2)}, u32[]{:S(2)}) collective-permute-start(bf16[512,256]{1,0:T(8,128)(2,1)} %param.9), channel_id=1, source_target_pairs={{0,16},{1,17},{2,18},{3,19},{4,20},{5,21},{6,22},{7,23},{8,24},{9,... | collective-permute-start | bytes 786440 | tf_op jit(solution)/shard_map/ppermute | solution.py:168
  10.5 3.0 %copy-start.2 = (s32[8,16]{1,0:T(8,128)S(1)}, s32[8,16]{1,0:T(8,128)}, u32[]{:S(2)}) copy-start(s32[8,16]{1,0:T(8,128)} %refs_0_.5) | copy-start | bytes 1540
  12.0 11.5 %collective-permute-start.6 = (bf16[256,512]{1,0:T(8,128)(2,1)S(1)}, bf16[256,512]{1,0:T(8,128)(2,1)S(1)}, u32[]{:S(2)}, u32[]{:S(2)}) collective-permute-start(bf16[256,512]{1,0:T(8,128)(2,1)S(1)} %constant_dynamic-update-slice_fusion.q_ref), channel_id=1, source_target_pairs={{0,4},{1,3},{2,6},{3,1},{4,0},{5,7},{6,2},{7,5},{8,12},{9,11},{10,... | collective-permute-start | bytes 786440 | tf_op jit(solution)/shard_map/ppermute | solution.py:168
  13.6 10.0 %collective-permute-start.3 = (s32[8,16]{1,0:T(8,128)S(1)}, s32[8,16]{1,0:T(8,128)S(1)}, u32[]{:S(2)}, u32[]{:S(2)}) collective-permute-start(s32[8,16]{1,0:T(8,128)S(1)} %copy-done.2), channel_id=1, source_target_pairs={{0,2},{1,5},{2,0},{3,7},{4,6},{5,1},{6,4},{7,3},{8,10},{9,13},{10,... | collective-permute-start | bytes 1544 | tf_op jit(solution)/shard_map/ppermute | solution.py:168
  15.0 8.5 %copy-start = (bf16[1,2048,128]{2,1,0:T(8,128)(2,1)S(1)}, bf16[1,2048,128]{2,1,0:T(8,128)(2,1)}, u32[]{:S(2)}) copy-start(bf16[1,2048,128]{2,1,0:T(8,128)(2,1)} %param.6) | copy-start | bytes 1572868
  15.0 8.5 %copy-start.1 = (bf16[1,2048,128]{2,1,0:T(8,128)(2,1)S(1)}, bf16[1,2048,128]{2,1,0:T(8,128)(2,1)}, u32[]{:S(2)}) copy-start(bf16[1,2048,128]{2,1,0:T(8,128)(2,1)} %param.7) | copy-start | bytes 1572868
  23.2 17.1 %collective-permute-start.18 = (bf16[512,256]{1,0:T(8,128)(2,1)S(1)}, bf16[512,256]{1,0:T(8,128)(2,1)S(1)}, u32[]{:S(2)}, u32[]{:S(2)}) collective-permute-start(bf16[512,256]{1,0:T(8,128)(2,1)S(1)} %get-tuple-element.22), channel_id=1, source_target_pairs={{0,1},{1,0},{2,3},{3,2},{4,5},{5,4},{6,7},{7,6},{8,9},{9,8},{10,11... | collective-permute-start | bytes 786440 | tf_op jit(solution)/shard_map/ppermute | solution.py:168
  26.0 9.6 %collective-permute-start.9 = (bf16[128,512]{1,0:T(8,128)(2,1)S(1)}, bf16[128,512]{1,0:T(8,128)(2,1)S(1)}, u32[]{:S(2)}, u32[]{:S(2)}) collective-permute-start(bf16[128,512]{1,0:T(8,128)(2,1)S(1)} %shard_map.59), channel_id=1, source_target_pairs={{0,4},{1,3},{2,6},{3,1},{4,0},{5,7},{6,2},{7,5},{8,12},{9,11},{10,... | collective-permute-start | bytes 393224 | tf_op jit(solution)/shard_map/ppermute | solution.py:168
  30.3 9.3 %collective-permute-start.7 = (bf16[128,512]{1,0:T(8,128)(2,1)S(1)}, bf16[128,512]{1,0:T(8,128)(2,1)S(1)}, u32[]{:S(2)}, u32[]{:S(2)}) collective-permute-start(bf16[128,512]{1,0:T(8,128)(2,1)S(1)} %shard_map.57), channel_id=1, source_target_pairs={{0,4},{1,3},{2,6},{3,1},{4,0},{5,7},{6,2},{7,5},{8,12},{9,11},{10,... | collective-permute-start | bytes 393224 | tf_op jit(solution)/shard_map/ppermute | solution.py:168
  35.7 6.4 %collective-permute-start.11 = (bf16[64,512]{1,0:T(8,128)(2,1)S(1)}, bf16[64,512]{1,0:T(8,128)(2,1)S(1)}, u32[]{:S(2)}, u32[]{:S(2)}) collective-permute-start(bf16[64,512]{1,0:T(8,128)(2,1)S(1)} %get-tuple-element.16), channel_id=1, source_target_pairs={{0,24},{1,25},{2,26},{3,27},{4,28},{5,29},{6,30},{7,31},{8,16},{9,... | collective-permute-start | bytes 196616 | tf_op jit(solution)/shard_map/ppermute | solution.py:168
  39.5 5.3 %collective-permute-start.10 = (bf16[64,512]{1,0:T(8,128)(2,1)S(1)}, bf16[64,512]{1,0:T(8,128)(2,1)S(1)}, u32[]{:S(2)}, u32[]{:S(2)}) collective-permute-start(bf16[64,512]{1,0:T(8,128)(2,1)S(1)} %get-tuple-element.15), channel_id=1, source_target_pairs={{0,16},{1,17},{2,18},{3,19},{4,20},{5,21},{6,22},{7,23},{8,24},{9,... | collective-permute-start | bytes 196616 | tf_op jit(solution)/shard_map/ppermute | solution.py:168
  39.6 5.2 %collective-permute-start.8 = (bf16[64,512]{1,0:T(8,128)(2,1)S(1)}, bf16[64,512]{1,0:T(8,128)(2,1)S(1)}, u32[]{:S(2)}, u32[]{:S(2)}) collective-permute-start(bf16[64,512]{1,0:T(8,128)(2,1)S(1)} %get-tuple-element.14), channel_id=1, source_target_pairs={{0,8},{1,9},{2,10},{3,11},{4,12},{5,13},{6,14},{7,15},{8,0},{9,1},... | collective-permute-start | bytes 196616 | tf_op jit(solution)/shard_map/ppermute | solution.py:168
  40.3 16.3 %collective-permute-start.19 = (bf16[1024,256]{1,0:T(8,128)(2,1)S(1)}, bf16[1024,256]{1,0:T(8,128)(2,1)S(1)}, u32[]{:S(2)}, u32[]{:S(2)}) collective-permute-start(bf16[1024,256]{1,0:T(8,128)(2,1)S(1)} %pad_maximum_fusion.refs_4_), channel_id=1, source_target_pairs={{0,4},{1,5},{2,6},{3,7},{4,0},{5,1},{6,2},{7,3},{8,12},{9,13},{10,... | collective-permute-start | bytes 1572872 | tf_op jit(solution)/shard_map/ppermute | solution.py:168
  44.9 5.2 %collective-permute-start.13 = (bf16[64,512]{1,0:T(8,128)(2,1)S(1)}, bf16[64,512]{1,0:T(8,128)(2,1)S(1)}, u32[]{:S(2)}, u32[]{:S(2)}) collective-permute-start(bf16[64,512]{1,0:T(8,128)(2,1)S(1)} %add_convert_fusion), channel_id=1, source_target_pairs={{0,10},{1,11},{2,8},{3,9},{4,14},{5,15},{6,12},{7,13},{8,2},{9,3},... | collective-permute-start | bytes 196616 | tf_op jit(solution)/shard_map/ppermute | solution.py:168
  46.3 4.5 %collective-permute-start.12 = (bf16[64,512]{1,0:T(8,128)(2,1)S(1)}, bf16[64,512]{1,0:T(8,128)(2,1)S(1)}, u32[]{:S(2)}, u32[]{:S(2)}) collective-permute-start(bf16[64,512]{1,0:T(8,128)(2,1)S(1)} %add_convert_fusion), channel_id=1, source_target_pairs={{0,8},{1,9},{2,10},{3,11},{4,12},{5,13},{6,14},{7,15},{8,0},{9,1},... | collective-permute-start | bytes 196616 | tf_op jit(solution)/shard_map/ppermute | solution.py:168
  50.8 5.8 %collective-permute-start.15 = (bf16[192,512]{1,0:T(8,128)(2,1)S(1)}, bf16[192,512]{1,0:T(8,128)(2,1)S(1)}, u32[]{:S(2)}, u32[]{:S(2)}) collective-permute-start(bf16[192,512]{1,0:T(8,128)(2,1)S(1)} %pad_maximum_fusion.1.refs_0_), channel_id=1, source_target_pairs={{0,1},{1,0},{2,3},{3,2},{4,5},{5,4},{6,7},{7,6},{8,9},{9,8},{10,11... | collective-permute-start | bytes 589832 | tf_op jit(solution)/shard_map/ppermute | solution.py:168
  50.9 4.5 %collective-permute-start.14 = (bf16[64,512]{1,0:T(8,128)(2,1)S(1)}, bf16[64,512]{1,0:T(8,128)(2,1)S(1)}, u32[]{:S(2)}, u32[]{:S(2)}) collective-permute-start(bf16[64,512]{1,0:T(8,128)(2,1)S(1)} %add_convert_fusion), channel_id=1, source_target_pairs={{0,2},{1,3},{2,0},{3,1},{4,6},{5,7},{6,4},{7,5},{8,10},{9,11},{10,... | collective-permute-start | bytes 196616 | tf_op jit(solution)/shard_map/ppermute | solution.py:168
  55.4 1.3 %collective-permute-start.16 = (bf16[64,512]{1,0:T(8,128)(2,1)S(1)}, bf16[64,512]{1,0:T(8,128)(2,1)S(1)}, u32[]{:S(2)}, u32[]{:S(2)}) collective-permute-start(bf16[64,512]{1,0:T(8,128)(2,1)S(1)} %collective-permute-done.14.refs_1_), channel_id=1, source_target_pairs={{0,1},{1,0},{2,3},{3,2},{4,5},{5,4},{6,7},{7,6},{8,9},{9,8},{10,11... | collective-permute-start | bytes 196616 | tf_op jit(solution)/shard_map/ppermute | solution.py:168
  57.1 4.3 %collective-permute-start.20 = (bf16[64,512]{1,0:T(8,128)(2,1)S(1)}, bf16[64,512]{1,0:T(8,128)(2,1)S(1)}, u32[]{:S(2)}, u32[]{:S(2)}) collective-permute-start(bf16[64,512]{1,0:T(8,128)(2,1)S(1)} %get-tuple-element.18), channel_id=1, source_target_pairs={{0,2},{1,3},{2,0},{3,1},{4,6},{5,7},{6,4},{7,5},{8,10},{9,11},{10,... | collective-permute-start | bytes 196616 | tf_op jit(solution)/shard_map/ppermute | solution.py:168
  57.9 4.3 %collective-permute-start.21 = (bf16[64,512]{1,0:T(8,128)(2,1)S(1)}, bf16[64,512]{1,0:T(8,128)(2,1)S(1)}, u32[]{:S(2)}, u32[]{:S(2)}) collective-permute-start(bf16[64,512]{1,0:T(8,128)(2,1)S(1)} %get-tuple-element.19), channel_id=1, source_target_pairs={{0,8},{1,9},{2,10},{3,11},{4,12},{5,13},{6,14},{7,15},{8,0},{9,1},... | collective-permute-start | bytes 196616 | tf_op jit(solution)/shard_map/ppermute | solution.py:168
  59.0 5.2 %collective-permute-start.22 = (bf16[64,512]{1,0:T(8,128)(2,1)S(1)}, bf16[64,512]{1,0:T(8,128)(2,1)S(1)}, u32[]{:S(2)}, u32[]{:S(2)}) collective-permute-start(bf16[64,512]{1,0:T(8,128)(2,1)S(1)} %get-tuple-element.20), channel_id=1, source_target_pairs={{0,10},{1,11},{2,8},{3,9},{4,14},{5,15},{6,12},{7,13},{8,2},{9,3},... | collective-permute-start | bytes 196616 | tf_op jit(solution)/shard_map/ppermute | solution.py:168
